TPU v7x, 256 devices: a whole 4x4x8 slice. The times are simulated.
256 devices in a mesh: gx: 8 (over y, core), gy: 32 (over z, x).
Axes of the slice: x: 4, y: 4, z: 8, core: 2. Of those that a mesh axis runs over, the one named last changes fastest.
Arguments:
- field: float32 [32, 2048, 2048], P(None, 'gy', 'gx'), may hold values from -6 to 6
- row_scale: float32 [2048], replicated, may hold values from 0.5 to 2
- col_scale: float32 [2048], P('gx'), may hold values from 0.5 to 2
- row_rate: float32 [2048], replicated, may hold values from 0.2 to 1
- col_shift: float32 [2048], P('gx'), may hold values from -1 to 1
- col_mix: float32 [2048], P('gx'), may hold values from -1 to 1
Outputs:
- latent: float32 [2, 32, 2048, 2048], P(None, 'gy', None, 'gx')
- loglik: float32 [], replicated
All inputs are finite; a program needn't handle non-finite values.
Results may differ from a plain program's by a relative error of at most 0.000075.
Values sent between devices are 32-bit elements; how exact they have to be, the bound alone decides.
A program may use at most 128 MiB of HBM per device.

v0:
```python
import functools
import math

import jax
import jax.numpy as jnp
from jax import lax
from jax.experimental import pallas as pl
from jax.experimental.pallas import tpu as pltpu
from jax.sharding import PartitionSpec as P

precision_top = lax.Precision.HIGHEST


def reverse_bits(value, count):
    result = value * 0
    for place in range(count):
        result = result + (value >> place & 1) * (1 << count - 1 - place)
    return result


def root_table(row_index, freqs, length):
    phase = row_index[:, None] * freqs[None, :] % length
    angle = phase.astype(jnp.float32) * (-2.0 * math.pi / length)
    return (jnp.cos(angle), jnp.sin(angle))


def complex_einsum(form, real_part, imag_part, cos_part, sin_part):
    first = jnp.einsum(form, real_part, cos_part, precision=precision_top)
    second = jnp.einsum(form, real_part, sin_part, precision=precision_top)
    first = first - jnp.einsum(form, imag_part, sin_part, precision=precision_top)
    second = second + jnp.einsum(form, imag_part, cos_part, precision=precision_top)
    return (first, second)


def x_stage(rows, devices):
    count, length = rows.shape
    width = length // devices
    levels = devices.bit_length() - 1
    shaped = rows.reshape(count, devices, width)
    group = jnp.arange(devices, dtype=jnp.int32)
    residue = reverse_bits(group, levels)
    cos_8, sin_8 = root_table(group, residue, devices)
    part_real = jnp.einsum("ygn,gd->dyn", shaped, cos_8, precision=precision_top)
    part_imag = jnp.einsum("ygn,gd->dyn", shaped, sin_8, precision=precision_top)
    local_index = jnp.arange(width, dtype=jnp.int32)
    twist_cos, twist_sin = root_table(residue, local_index, length)
    twist_cos = twist_cos[:, None, :]
    twist_sin = twist_sin[:, None, :]
    turned_real = part_real * twist_cos - part_imag * twist_sin
    turned_imag = part_real * twist_sin + part_imag * twist_cos
    cos_w, sin_w = root_table(local_index, local_index, width)
    return complex_einsum("dyn,nk->dyk", turned_real, turned_imag, cos_w, sin_w)


def y_transform(real_part, imag_part):
    planes, length, width = real_part.shape
    outer = 1 << (length.bit_length() - 1) // 2
    inner = length // outer
    outer_index = jnp.arange(outer, dtype=jnp.int32)
    inner_index = jnp.arange(inner, dtype=jnp.int32)
    cos_one, sin_one = root_table(outer_index, outer_index, outer)
    cos_two, sin_two = root_table(inner_index, inner_index, inner)
    cos_mid, sin_mid = root_table(outer_index, inner_index, length)
    shaped_real = real_part.reshape(planes, outer, inner, width)
    shaped_imag = imag_part.reshape(planes, outer, inner, width)
    step_real, step_imag = complex_einsum(
        "zabc,ak->zkbc", shaped_real, shaped_imag, cos_one, sin_one
    )
    twist_cos = cos_mid[None, :, :, None]
    twist_sin = sin_mid[None, :, :, None]
    turned_real = step_real * twist_cos - step_imag * twist_sin
    turned_imag = step_real * twist_sin + step_imag * twist_cos
    final_real, final_imag = complex_einsum(
        "zkbc,bj->zjkc", turned_real, turned_imag, cos_two, sin_two
    )
    return (final_real.reshape(planes, length, width), final_imag.reshape(planes, length, width))


def y_kernel(norm_factor, cos_a_ref, sin_a_ref, twist_cos_ref, twist_sin_ref,
             cos_b_ref, sin_b_ref, row_scale_ref, row_rate_ref, col_scale_ref, col_shift_ref,
             col_mix_ref, real_hbm, imag_hbm, out_hbm, sum_ref,
             held, step_real, step_imag, staged, in_sems, out_sems):
    size_a, size_b, width = real_hbm.shape
    half = width // 2
    loads = []
    for part, source in enumerate((real_hbm, imag_hbm)):
        for index in range(size_b):
            copy = pltpu.make_async_copy(
                source.at[:, index, :], held.at[part, index], in_sems.at[part, index]
            )
            copy.start()
            loads.append(copy)

    def dot(left, right):
        return jnp.dot(left, right, precision=precision_top, preferred_element_type=jnp.float32)

    cos_a = cos_a_ref[...]
    sin_a = sin_a_ref[...]
    for index in range(size_b):
        loads[index].wait()
        loads[size_b + index].wait()
        part_real = held[0, index]
        part_imag = held[1, index]
        out_real = dot(cos_a, part_real) - dot(sin_a, part_imag)
        out_imag = dot(cos_a, part_imag) + dot(sin_a, part_real)
        rows = pl.ds(index * size_a, size_a)
        twist_cos = twist_cos_ref[rows, :]
        twist_sin = twist_sin_ref[rows, :]
        turned_real = out_real * twist_cos - out_imag * twist_sin
        turned_imag = out_real * twist_sin + out_imag * twist_cos
        for side in range(2):
            lanes = slice(side * half, (side + 1) * half)
            step_real[side, rows, :] = turned_real[:, lanes]
            step_imag[side, rows, :] = turned_imag[:, lanes]

    col_scale = col_scale_ref[...]
    col_shift = col_shift_ref[...]
    col_mix = col_mix_ref[...]
    cos_b = cos_b_ref[...]
    sin_b = sin_b_ref[...]

    def second(index, total):
        picked = pl.ds(index, size_b, stride=size_a)
        part_real = jnp.concatenate([step_real[0, picked, :], step_real[1, picked, :]], axis=1)
        part_imag = jnp.concatenate([step_imag[0, picked, :], step_imag[1, picked, :]], axis=1)
        spec_real = dot(cos_b, part_real) - dot(sin_b, part_imag)
        spec_imag = dot(cos_b, part_imag) + dot(sin_b, part_real)
        rows = pl.ds(pl.multiple_of(index * size_b, size_b), size_b)
        scale = row_scale_ref[rows, :] * col_scale
        latent_u = spec_real * norm_factor * scale
        latent_v = spec_imag * norm_factor * scale
        log_scale = row_rate_ref[rows, :] * jnp.tanh(latent_u + col_shift)
        latent_w = latent_v * jnp.exp(log_scale) + col_mix * latent_u
        terms = (
            -0.5 * (latent_u * latent_u + latent_w * latent_w)
            - math.log(2.0 * math.pi)
            + log_scale
            + 2.0 * jnp.log(scale)
        )
        staged[0, index] = latent_u
        staged[1, index] = latent_w
        for part in range(2):
            pltpu.make_async_copy(
                staged.at[part, index], out_hbm.at[part, :, index, :], out_sems.at[part, index]
            ).start()
        return total + terms

    total = lax.fori_loop(0, size_a, second, jnp.zeros((size_b, width), jnp.float32))
    sum_ref[...] = jnp.broadcast_to(jnp.sum(total), sum_ref.shape)

    def finish(index, carry):
        for part in range(2):
            pltpu.make_async_copy(
                staged.at[part, index], out_hbm.at[part, :, index, :], out_sems.at[part, index]
            ).wait()
        return carry

    lax.fori_loop(0, size_a, finish, 0)


def y_stage(real_part, imag_part, row_scale, col_scale, row_rate, col_shift, col_mix, norm_factor):
    length, width = real_part.shape
    size_b = 1 << (length.bit_length() - 1) // 2
    size_a = length // size_b
    index_a = jnp.arange(size_a, dtype=jnp.int32)
    index_b = jnp.arange(size_b, dtype=jnp.int32)
    cos_a, sin_a = root_table(index_a, index_a, size_a)
    cos_b, sin_b = root_table(index_b, index_b, size_b)
    twist_cos, twist_sin = root_table(index_b, index_a, length)
    twist_cos = twist_cos.reshape(length, 1)
    twist_sin = twist_sin.reshape(length, 1)
    row_scale_t = row_scale.reshape(size_b, size_a).T.reshape(length, 1)
    row_rate_t = row_rate.reshape(size_b, size_a).T.reshape(length, 1)
    vmem = pl.BlockSpec(memory_space=pltpu.VMEM)
    anywhere = pl.BlockSpec(memory_space=pl.ANY)
    latent, sums = pl.pallas_call(
        functools.partial(y_kernel, norm_factor),
        out_shape=(
            jax.ShapeDtypeStruct((2, size_b, size_a, width), jnp.float32),
            jax.ShapeDtypeStruct((8, 128), jnp.float32),
        ),
        in_specs=[vmem] * 11 + [anywhere] * 2,
        out_specs=(anywhere, vmem),
        scratch_shapes=[
            pltpu.VMEM((2, size_b, size_a, width), jnp.float32),
            pltpu.VMEM((2, length, width // 2), jnp.float32),
            pltpu.VMEM((2, length, width // 2), jnp.float32),
            pltpu.VMEM((2, size_a, size_b, width), jnp.float32),
            pltpu.SemaphoreType.DMA((2, size_b)),
            pltpu.SemaphoreType.DMA((2, size_a)),
        ],
        compiler_params=pltpu.CompilerParams(vmem_limit_bytes=60 * 1024 * 1024),
    )(
        cos_a, sin_a, twist_cos, twist_sin, cos_b, sin_b,
        row_scale_t, row_rate_t, col_scale.reshape(1, width), col_shift.reshape(1, width),
        col_mix.reshape(1, width),
        real_part.reshape(size_a, size_b, width), imag_part.reshape(size_a, size_b, width),
    )
    return latent.reshape(2, length, width), sums[0, 0]

MESH_IDS = pl.DeviceIdType.MESH


def total_kernel(value_ref, out_ref, slots_a, slots_b, send_a, recv_a, send_b, recv_b):
    count_x = lax.axis_size("gx")
    count_y = lax.axis_size("gy")
    me_x = lax.axis_index("gx")
    me_y = lax.axis_index("gy")
    barrier = pltpu.get_barrier_semaphore()
    for step in range(1, count_x):
        pl.semaphore_signal(
            barrier, inc=1, device_id=((me_x + step) % count_x, me_y), device_id_type=MESH_IDS
        )
    for step in range(1, count_y):
        pl.semaphore_signal(
            barrier, inc=1, device_id=(me_x, (me_y + step) % count_y), device_id_type=MESH_IDS
        )
    slots_a[0] = value_ref[...]
    pl.semaphore_wait(barrier, count_x - 1 + count_y - 1)
    sends = []
    for step in range(1, count_x):
        copy = pltpu.make_async_remote_copy(
            src_ref=value_ref,
            dst_ref=slots_a.at[step],
            send_sem=send_a.at[step],
            recv_sem=recv_a.at[step],
            device_id=((me_x + step) % count_x, me_y),
            device_id_type=MESH_IDS,
        )
        copy.start()
        sends.append(copy)
    for copy in sends:
        copy.wait_recv()
    group_sum = slots_a[(me_x - 0) % count_x]
    for source in range(1, count_x):
        group_sum = group_sum + slots_a[(me_x - source + count_x) % count_x]
    slots_b[0] = group_sum
    later = []
    for step in range(1, count_y):
        copy = pltpu.make_async_remote_copy(
            src_ref=slots_b.at[0],
            dst_ref=slots_b.at[step],
            send_sem=send_b.at[step],
            recv_sem=recv_b.at[step],
            device_id=(me_x, (me_y + step) % count_y),
            device_id_type=MESH_IDS,
        )
        copy.start()
        later.append(copy)
    for copy in later:
        copy.wait_recv()
    grand = slots_b[(me_y - 0) % count_y]
    for source in range(1, count_y):
        grand = grand + slots_b[(me_y - source + count_y) % count_y]
    out_ref[...] = grand
    for copy in sends:
        copy.wait_send()
    for copy in later:
        copy.wait_send()


def total_everywhere(value):
    count_x = lax.axis_size("gx")
    count_y = lax.axis_size("gy")
    tile = jnp.broadcast_to(value, (8, 128)).astype(jnp.float32)
    result = pl.pallas_call(
        total_kernel,
        out_shape=jax.ShapeDtypeStruct((8, 128), jnp.float32),
        in_specs=[pl.BlockSpec(memory_space=pltpu.VMEM)],
        out_specs=pl.BlockSpec(memory_space=pltpu.VMEM),
        scratch_shapes=[
            pltpu.VMEM((count_x, 8, 128), jnp.float32),
            pltpu.VMEM((count_y, 8, 128), jnp.float32),
            pltpu.SemaphoreType.DMA((count_x,)),
            pltpu.SemaphoreType.DMA((count_x,)),
            pltpu.SemaphoreType.DMA((count_y,)),
            pltpu.SemaphoreType.DMA((count_y,)),
        ],
        compiler_params=pltpu.CompilerParams(collective_id=0, has_side_effects=True),
    )(tile)
    return result[0, 0]


def per_device(field, row_scale, col_scale, row_rate, col_shift, col_mix):
    devices = lax.axis_size("gx")
    plane = lax.all_to_all(field, "gy", split_axis=0, concat_axis=1, tiled=True)
    plane = plane[0]
    rows = lax.all_to_all(plane, "gx", split_axis=0, concat_axis=1, tiled=True)
    spec_real, spec_imag = x_stage(rows, devices)
    both = jnp.stack([spec_real, spec_imag])
    both = lax.all_to_all(both, "gx", split_axis=1, concat_axis=2, tiled=True)
    length = both.shape[2]
    total_cols = both.shape[3] * devices
    norm_factor = 1.0 / math.sqrt(length * total_cols)
    latent, part_sum = y_stage(
        both[0, 0], both[1, 0], row_scale, col_scale, row_rate, col_shift, col_mix, norm_factor
    )
    total_sum = total_everywhere(part_sum)
    mode_count = length * total_cols * lax.axis_size("gy")
    loglik = total_sum / mode_count
    return (latent[:, None], loglik)


def solution(mesh):
    return jax.shard_map(
        per_device,
        mesh=mesh,
        in_specs=(P(None, "gy", "gx"), P(), P("gx"), P(), P("gx"), P("gx")),
        out_specs=(P(None, "gy", None, "gx"), P()),
        check_vma=False,
    )
```

profile of v0, /device:TPU:1, one launch (start us, length us, event | category | flops | bytes accessed | tf_op | source)
XLA Modules:
  0.0 236.9 jit_solution(9913416022962938514)
XLA Ops:
  0.6 60.7 %all_to_all.34 = f32[32,64,256]{2,1,0:T(8,128)} all-to-all(f32[32,64,256]{2,1,0:T(8,128)} %param.6), channel_id=1, replica_groups=mesh['gx'=8,'gy'=32] {'gy'}, dimensions={0} | all-to-all | bytes 4194304 | tf_op jit(solution)/shard_map/all_to_all | solution.py:286
  61.3 7.3 %all-to-all-start.1 = ((f32[8,256,256]{2,1,0:T(8,128)}), f32[8,256,256]{2,1,0:T(8,128)S(1)}, u32[]{:S(2)}, u32[]{:S(2)}) async-start(f32[8,256,256]{2,1,0:T(8,128)} %bitcast.44), calls=%async_computation.1 | async-start | bytes 4194304 | tf_op jit(solution)/shard_map/all_to_all | solution.py:288
  68.7 26.2 %all-to-all-done.1 = f32[8,256,256]{2,1,0:T(8,128)S(1)} async-done(((f32[8,256,256]{2,1,0:T(8,128)}), f32[8,256,256]{2,1,0:T(8,128)S(1)}, u32[]{:S(2)}, u32[]{:S(2)}) %all-to-all-start.1) | async-done | bytes 2097184 | tf_op jit(solution)/shard_map/all_to_all | solution.py:288
  94.9 2.9 %fusion.2 = f32[8,256,256]{2,0,1:T(8,128)S(1)} fusion(f32[8,256,256]{2,1,0:T(8,128)S(1)} %all-to-all-done.1, s32[8]{0:T(128)S(1)} %fusion.75), kind=kOutput, calls=%fused_computation.3 | convolution fusion | flops 50332544 | bytes 4194336 | tf_op jit(solution)/shard_map/ygn,gd->dyn/dot_general | solution.py:43
  97.8 3.4 %multiply_subtract_fusion = (f32[8,256,256]{2,0,1:T(8,128)S(1)}, f32[8,256,256]{2,0,1:T(8,128)S(1)}) fusion(f32[8,256,256]{2,0,1:T(8,128)S(1)} %fusion.2, f32[8,256]{1,0:T(8,128)S(1)} %get-tuple-element.21, f32[8,256]{1,0:T(8,128)S(1)} %get-tuple-element.20, f32[8,256,256]{2,1,0:T(8,128)S(1)} %all-to-all-done.1, s32[8]{0:T(128)S(1)} %fusion.75), kind=kOutput, calls=%fused_computation.8 | convolution fusion | flops 53478272 | bytes 8405024 | tf_op jit(solution)/shard_map/ygn,gd->dyn/dot_general | solution.py:44
  101.2 3.2 %fusion.6 = f32[8,256,256]{2,1,0:T(8,128)S(1)} fusion(f32[8,256,256]{2,0,1:T(8,128)S(1)} %get-tuple-element.15), kind=kOutput, calls=%fused_computation.11 | convolution fusion | flops 1611530240 | bytes 4194304 | tf_op jit(solution)/shard_map/dyn,nk->dyk/dot_general | solution.py:30
  104.4 3.4 %fusion.4 = f32[8,256,256]{2,1,0:T(8,128)S(1)} fusion(f32[8,256,256]{2,0,1:T(8,128)S(1)} %get-tuple-element.15), kind=kOutput, calls=%fused_computation.9 | convolution fusion | flops 1611530240 | bytes 4194304 | tf_op jit(solution)/shard_map/dyn,nk->dyk/dot_general | solution.py:31
  107.8 3.2 %subtract_bitcast_fusion = f32[1,8,256,256]{3,2,1,0:T(8,128)S(1)} fusion(f32[8,256,256]{2,1,0:T(8,128)S(1)} %fusion.6, f32[8,256,256]{2,0,1:T(8,128)S(1)} %get-tuple-element.14), kind=kOutput, calls=%fused_computation.6 | convolution fusion | flops 1612054528 | bytes 6291456 | tf_op jit(solution)/shard_map/dyn,nk->dyk/dot_general | solution.py:28
  111.1 3.2 %add_bitcast_fusion = f32[1,8,256,256]{3,2,1,0:T(8,128)S(1)} fusion(f32[8,256,256]{2,1,0:T(8,128)S(1)} %fusion.4, f32[8,256,256]{2,0,1:T(8,128)S(1)} %get-tuple-element.14), kind=kOutput, calls=%fused_computation.5 | convolution fusion | flops 1612054528 | bytes 6291456 | tf_op jit(solution)/shard_map/dyn,nk->dyk/dot_general | solution.py:29
  114.3 0.4 pad_maximum_fusion
  114.7 2.4 %copy.48 = f32[2,8,256,256]{3,2,0,1:T(8,128)} copy(f32[2,8,256,256]{3,2,1,0:T(8,128)S(1)} %pad_maximum_fusion) | data formatting | bytes 8388608 | tf_op jit(solution)/shard_map/stack | solution.py:290
  117.1 5.4 %all-to-all-start.2 = ((f32[2,8,256,256]{3,2,0,1:T(8,128)}), f32[2,8,256,256]{3,2,0,1:T(8,128)}, u32[]{:S(2)}, u32[]{:S(2)}) async-start(f32[2,8,256,256]{3,2,0,1:T(8,128)} %copy.48), calls=%async_computation.2 | async-start | bytes 8388608 | tf_op jit(solution)/shard_map/all_to_all | solution.py:291
  123.2 2.1 reshape.215.row_scale_ref
  125.5 2.1 reshape.216.row_rate_ref
  127.6 0.7 fusion.55
  128.3 0.8 fusion.45
  129.1 4.5 %multiply_sine_fusion = (f32[2048,1]{1,0:T(8,128)}, f32[2048,1]{1,0:T(8,128)}) fusion(f32[2048,1]{1,0:T(8,128)S(1)} %copy.40), kind=kLoop, calls=%fused_computation.19 | loop fusion | flops 2048 | bytes 24576 | tf_op jit(solution)/shard_map/sin | solution.py:24
  133.6 37.9 %all-to-all-done.2 = f32[2,8,256,256]{3,2,0,1:T(8,128)} async-done(((f32[2,8,256,256]{3,2,0,1:T(8,128)}), f32[2,8,256,256]{3,2,0,1:T(8,128)}, u32[]{:S(2)}, u32[]{:S(2)}) %all-to-all-start.2) | async-done | bytes 4194336 | tf_op jit(solution)/shard_map/all_to_all | solution.py:291
  171.5 4.6 %fusion.103 = (f32[1,8,256,256]{3,2,0,1:T(8,128)}, f32[1,8,256,256]{3,2,0,1:T(8,128)}) fusion(f32[2,8,256,256]{3,2,0,1:T(8,128)} %all-to-all-done.2), kind=kLoop, calls=%fused_computation.122 | loop fusion | bytes 8388608 | tf_op jit(solution)/shard_map/slice | solution.py:296
  176.1 38.5 %shard_map.77 = (f32[2,32,64,256]{3,2,1,0:T(8,128)}, f32[8,128]{1,0:T(8,128)}) custom-call(f32[64,64]{1,0:T(8,128)} %get-tuple-element.23.cos_a_ref, f32[64,64]{1,0:T(8,128)} %get-tuple-element.22.sin_a_ref, f32[2048,1]{1,0:T(8,128)} %get-tuple-element.19.twist_cos_ref, f32[2048,1]{1,0:T(8,128)} %get-tuple-element.18.twist_sin_ref, ...), custom_call_target="tpu_custom_call" | custom-call | tf_op jit(solution)/shard_map/pallas_call | solution.py:176
  214.6 1.2 slice.17
  215.8 1.2 broadcast_in_dim.2.value_ref
  217.1 16.9 %shard_map.78 = f32[8,128]{1,0:T(8,128)} custom-call(f32[8,128]{1,0:T(8,128)} %broadcast_in_dim.2.value_ref), custom_call_target="tpu_custom_call" | custom-call | tf_op jit(solution)/shard_map/pallas_call | solution.py:266
  233.9 1.2 slice.18
  (14 shorter events, 0.9 us)
Async XLA Ops:
  61.3 33.6 %all-to-all-start.1 = ((f32[8,256,256]{2,1,0:T(8,128)}), f32[8,256,256]{2,1,0:T(8,128)S(1)}, u32[]{:S(2)}, u32[]{:S(2)}) async-start(f32[8,256,256]{2,1,0:T(8,128)} %bitcast.44), calls=%async_computation.1 | async-start | bytes 4194304 | tf_op jit(solution)/shard_map/all_to_all | solution.py:288
  117.1 5.9 %copy-start = (f32[2048]{0:T(1024)S(1)}, f32[2048]{0:T(1024)}, u32[]{:S(2)}) copy-start(f32[2048]{0:T(1024)} %param.7) | copy-start | bytes 24580
  117.1 54.4 %all-to-all-start.2 = ((f32[2,8,256,256]{3,2,0,1:T(8,128)}), f32[2,8,256,256]{3,2,0,1:T(8,128)}, u32[]{:S(2)}, u32[]{:S(2)}) async-start(f32[2,8,256,256]{3,2,0,1:T(8,128)} %copy.48), calls=%async_computation.2 | async-start | bytes 8388608 | tf_op jit(solution)/shard_map/all_to_all | solution.py:291
  122.6 2.7 %copy-start.1 = (f32[2048]{0:T(1024)S(1)}, f32[2048]{0:T(1024)}, u32[]{:S(2)}) copy-start(f32[2048]{0:T(1024)} %param.9) | copy-start | bytes 24580
where the time goes:
time: 237 us
  waiting for transfers between devices  64.1 us (27%)
  blocking collectives  60.7 us (26%)
  Pallas kernels  55.4 us (23%)
  matrix products  19.3 us (8%)
  local copies, waits for them, and re-layouts  15.6 us (7%)
  starting transfers between devices  12.7 us (5%)
  other arithmetic  6.56 us (3%)
  between operations  2.51 us (1%)
    all_to_all x1, blocking collectives, per_device(): plane = lax.all_to_all(field, 'gy', split_axis=0, concat_axis=1, tiled=True)  60.7 us
    pallas_call x1, Pallas kernels, y_stage(): pl.pallas_call(functools.partial(y_kernel, norm_factor), out_shape=(jax.S...  38.5 us
    all_to_all x1, waiting for transfers between devices, per_device(): both = lax.all_to_all(both, 'gx', split_axis=1, concat_axis=2, tiled=True)  37.9 us
    all_to_all x1, waiting for transfers between devices, per_device(): rows = lax.all_to_all(plane, 'gx', split_axis=0, concat_axis=1, tiled=True)  26.2 us
    pallas_call x1, Pallas kernels, total_everywhere(): pl.pallas_call(total_kernel, out_shape=jax.ShapeDtypeStruct((8, 128), jnp...  16.9 us
    all_to_all x1, starting transfers between devices, per_device(): rows = lax.all_to_all(plane, 'gx', split_axis=0, concat_axis=1, tiled=True)  7.3 us
    sin x3, other arithmetic, root_table(): return (jnp.cos(angle), jnp.sin(angle))  6 us
    all_to_all x1, starting transfers between devices, per_device(): both = lax.all_to_all(both, 'gx', split_axis=1, concat_axis=2, tiled=True)  5.44 us
  transfers between devices with their start and end apart: 2, of which 2 were waited for; matrix products, arithmetic and copies ran while one was open for 5% of the time, Pallas kernels for 0%

commit v1 on v0

--- a/solution.py
+++ b/solution.py
@@ -80,13 +80,17 @@
              cos_b_ref, sin_b_ref, row_scale_ref, row_rate_ref, col_scale_ref, col_shift_ref,
              col_mix_ref, real_hbm, imag_hbm, out_hbm, sum_ref,
              held, step_real, step_imag, staged, in_sems, out_sems):
-    size_a, size_b, width = real_hbm.shape
+    high, low, blocks, rows, width = real_hbm.shape
+    size_b = low * rows
+    size_a = high * blocks
     half = width // 2
     loads = []
     for part, source in enumerate((real_hbm, imag_hbm)):
         for index in range(size_b):
             copy = pltpu.make_async_copy(
-                source.at[:, index, :], held.at[part, index], in_sems.at[part, index]
+                source.at[:, index // rows, :, index % rows, :],
+                held.at[part, index],
+                in_sems.at[part, index],
             )
             copy.start()
             loads.append(copy)
@@ -99,8 +103,8 @@
     for index in range(size_b):
         loads[index].wait()
         loads[size_b + index].wait()
-        part_real = held[0, index]
-        part_imag = held[1, index]
+        part_real = held[0, index].reshape(size_a, width)
+        part_imag = held[1, index].reshape(size_a, width)
         out_real = dot(cos_a, part_real) - dot(sin_a, part_imag)
         out_imag = dot(cos_a, part_imag) + dot(sin_a, part_real)
         rows = pl.ds(index * size_a, size_a)
@@ -158,13 +162,18 @@
     lax.fori_loop(0, size_a, finish, 0)
 
 
-def y_stage(real_part, imag_part, row_scale, col_scale, row_rate, col_shift, col_mix, norm_factor):
-    length, width = real_part.shape
+def y_stage(spectrum, row_scale, col_scale, row_rate, col_shift, col_mix, norm_factor, devices, height):
+    _, length, width = spectrum.shape
     size_b = 1 << (length.bit_length() - 1) // 2
     size_a = length // size_b
+    blocks = length // height
+    rows = height // devices
+    low = size_b // rows
+    high = devices // low
     index_a = jnp.arange(size_a, dtype=jnp.int32)
     index_b = jnp.arange(size_b, dtype=jnp.int32)
-    cos_a, sin_a = root_table(index_a, index_a, size_a)
+    order_a = (index_a % blocks) * high + index_a // blocks
+    cos_a, sin_a = root_table(index_a, order_a, size_a)
     cos_b, sin_b = root_table(index_b, index_b, size_b)
     twist_cos, twist_sin = root_table(index_b, index_a, length)
     twist_cos = twist_cos.reshape(length, 1)
@@ -173,6 +182,7 @@
     row_rate_t = row_rate.reshape(size_b, size_a).T.reshape(length, 1)
     vmem = pl.BlockSpec(memory_space=pltpu.VMEM)
     anywhere = pl.BlockSpec(memory_space=pl.ANY)
+    shaped = spectrum.reshape(2, high, low, blocks, rows, width)
     latent, sums = pl.pallas_call(
         functools.partial(y_kernel, norm_factor),
         out_shape=(
@@ -182,7 +192,7 @@
         in_specs=[vmem] * 11 + [anywhere] * 2,
         out_specs=(anywhere, vmem),
         scratch_shapes=[
-            pltpu.VMEM((2, size_b, size_a, width), jnp.float32),
+            pltpu.VMEM((2, size_b, high, blocks, width), jnp.float32),
             pltpu.VMEM((2, length, width // 2), jnp.float32),
             pltpu.VMEM((2, length, width // 2), jnp.float32),
             pltpu.VMEM((2, size_a, size_b, width), jnp.float32),
@@ -193,8 +203,7 @@
     )(
         cos_a, sin_a, twist_cos, twist_sin, cos_b, sin_b,
         row_scale_t, row_rate_t, col_scale.reshape(1, width), col_shift.reshape(1, width),
-        col_mix.reshape(1, width),
-        real_part.reshape(size_a, size_b, width), imag_part.reshape(size_a, size_b, width),
+        col_mix.reshape(1, width), shaped[0], shaped[1],
     )
     return latent.reshape(2, length, width), sums[0, 0]
 
@@ -283,17 +292,21 @@
 
 def per_device(field, row_scale, col_scale, row_rate, col_shift, col_mix):
     devices = lax.axis_size("gx")
-    plane = lax.all_to_all(field, "gy", split_axis=0, concat_axis=1, tiled=True)
-    plane = plane[0]
-    rows = lax.all_to_all(plane, "gx", split_axis=0, concat_axis=1, tiled=True)
-    spec_real, spec_imag = x_stage(rows, devices)
+    planes, height, width = field.shape
+    rows = height // devices
+    outgoing = field.reshape(planes, devices, rows, width).transpose(1, 0, 2, 3)
+    outgoing = outgoing.reshape(devices * planes, rows, width)
+    incoming = lax.all_to_all(outgoing, ("gx", "gy"), split_axis=0, concat_axis=0, tiled=True)
+    incoming = incoming.reshape(devices, planes, rows, width).transpose(1, 2, 0, 3)
+    block = incoming.reshape(planes * rows, devices * width)
+    spec_real, spec_imag = x_stage(block, devices)
     both = jnp.stack([spec_real, spec_imag])
     both = lax.all_to_all(both, "gx", split_axis=1, concat_axis=2, tiled=True)
     length = both.shape[2]
     total_cols = both.shape[3] * devices
     norm_factor = 1.0 / math.sqrt(length * total_cols)
     latent, part_sum = y_stage(
-        both[0, 0], both[1, 0], row_scale, col_scale, row_rate, col_shift, col_mix, norm_factor
+        both[:, 0], row_scale, col_scale, row_rate, col_shift, col_mix, norm_factor, devices, height
     )
     total_sum = total_everywhere(part_sum)
     mode_count = length * total_cols * lax.axis_size("gy")

time: 237 us -> 212 us (0.89)
  blocking collectives: 60.7 us -> 0 us
  waiting for transfers between devices: 64.1 us -> 90.7 us
  starting transfers between devices: 12.7 us -> 20.5 us
  local copies, waits for them, and re-layouts: 15.6 us -> 19.9 us
    all_to_all x1 -> x0, blocking collectives: 60.7 us -> none  [per_device(): plane = lax.all_to_all(field, 'gy', split_axis=0, concat_axis=1, tiled=True)]
    all_to_all x1, waiting for transfers between devices: 26.2 us -> 53.5 us  [per_device(): lax.all_to_all(outgoing, ('gx', 'gy'), split_axis=0, concat_axis=0, tiled...]
    all_to_all x1, starting transfers between devices: 7.3 us -> 15.7 us  [per_device(): lax.all_to_all(outgoing, ('gx', 'gy'), split_axis=0, concat_axis=0, tiled...]
    transpose x0 -> x2, local copies, waits for them, and re-layouts: none -> 4.33 us  [the longest x1 3.11 us: per_device(): outgoing = field.reshape(planes, devices, rows, width).transpose(1, 0, 2, 3)]
where the time goes in v1:
time: 212 us
  waiting for transfers between devices  90.7 us (43%)
  Pallas kernels  53.9 us (25%)
  starting transfers between devices  20.5 us (10%)
  local copies, waits for them, and re-layouts  19.9 us (9%)
  matrix products  17.5 us (8%)
  other arithmetic  6.56 us (3%)
  between operations  2.55 us (1%)
    all_to_all x1, waiting for transfers between devices, per_device(): lax.all_to_all(outgoing, ('gx', 'gy'), split_axis=0, concat_axis=0, tiled...  53.5 us
    pallas_call x1, Pallas kernels, y_stage(): pl.pallas_call(functools.partial(y_kernel, norm_factor), out_shape=(jax.S...  38.5 us
    all_to_all x1, waiting for transfers between devices, per_device(): both = lax.all_to_all(both, 'gx', split_axis=1, concat_axis=2, tiled=True)  37.2 us
    all_to_all x1, starting transfers between devices, per_device(): lax.all_to_all(outgoing, ('gx', 'gy'), split_axis=0, concat_axis=0, tiled...  15.7 us
    pallas_call x1, Pallas kernels, total_everywhere(): pl.pallas_call(total_kernel, out_shape=jax.ShapeDtypeStruct((8, 128), jnp...  15.4 us
    sin x3, other arithmetic, root_table(): return (jnp.cos(angle), jnp.sin(angle))  6 us
    all_to_all x1, starting transfers between devices, per_device(): both = lax.all_to_all(both, 'gx', split_axis=1, concat_axis=2, tiled=True)  4.86 us
    slice x1, local copies, waits for them, and re-layouts, y_stage(): shaped[1]  4.58 us
  transfers between devices with their start and end apart: 2, of which 2 were waited for; matrix products, arithmetic and copies ran while one was open for 5% of the time, Pallas kernels for 0%

profile of v1, /device:TPU:1, one launch (start us, length us, event | category | flops | bytes accessed | tf_op | source)
XLA Modules:
  0.0 211.6 jit_solution(14421710154251404349)
XLA Ops:
  0.6 3.1 %copy.58 = f32[8,32,8,256]{3,2,1,0:T(8,128)} copy(f32[8,32,8,256]{3,2,0,1:T(8,128)} %bitcast.50) | data formatting | bytes 4194304 | tf_op jit(solution)/shard_map/transpose | solution.py:297
  3.7 15.7 %all-to-all-start = ((f32[256,8,256]{2,1,0:T(8,128)}), f32[256,8,256]{2,1,0:T(8,128)S(1)}, u32[]{:S(2)}, u32[]{:S(2)}) async-start(f32[256,8,256]{2,1,0:T(8,128)} %bitcast.49), calls=%async_computation | async-start | bytes 4194304 | tf_op jit(solution)/shard_map/all_to_all | solution.py:299
  19.5 53.5 %all-to-all-done = f32[256,8,256]{2,1,0:T(8,128)S(1)} async-done(((f32[256,8,256]{2,1,0:T(8,128)}), f32[256,8,256]{2,1,0:T(8,128)S(1)}, u32[]{:S(2)}, u32[]{:S(2)}) %all-to-all-start) | async-done | bytes 2097184 | tf_op jit(solution)/shard_map/all_to_all | solution.py:299
  73.1 1.2 copy.59
  74.3 2.0 fusion.57
  76.3 2.4 %multiply_subtract_fusion = (f32[8,256,256]{2,0,1:T(8,128)S(1)}, f32[8,256,256]{2,0,1:T(8,128)S(1)}) fusion(f32[8,256,256]{2,0,1:T(8,128)S(1)} %fusion.57, f32[8,256]{1,0:T(8,128)S(1)} %get-tuple-element.23, f32[8,256]{1,0:T(8,128)S(1)} %get-tuple-element.22, f32[256,8,256]{2,1,0:T(8,128)S(1)} %bitcast.45, s32[8]{0:T(128)S(1)} %fusion.73), kind=kOutput, calls=%fused_computation.4 | convolution fusion | flops 53478272 | bytes 8405024 | tf_op jit(solution)/shard_map/ygn,gd->dyn/dot_general | solution.py:44
  78.7 3.2 %fusion.2 = f32[8,256,256]{2,1,0:T(8,128)S(1)} fusion(f32[8,256,256]{2,0,1:T(8,128)S(1)} %get-tuple-element.17), kind=kOutput, calls=%fused_computation.7 | convolution fusion | flops 1611530240 | bytes 4194304 | tf_op jit(solution)/shard_map/dyn,nk->dyk/dot_general | solution.py:30
  81.9 3.4 %fusion = f32[8,256,256]{2,1,0:T(8,128)S(1)} fusion(f32[8,256,256]{2,0,1:T(8,128)S(1)} %get-tuple-element.17), kind=kOutput, calls=%fused_computation.5 | convolution fusion | flops 1611530240 | bytes 4194304 | tf_op jit(solution)/shard_map/dyn,nk->dyk/dot_general | solution.py:31
  85.3 3.2 %subtract_bitcast_fusion = f32[1,8,256,256]{3,2,1,0:T(8,128)S(1)} fusion(f32[8,256,256]{2,1,0:T(8,128)S(1)} %fusion.2, f32[8,256,256]{2,0,1:T(8,128)S(1)} %get-tuple-element.16), kind=kOutput, calls=%fused_computation.2 | convolution fusion | flops 1612054528 | bytes 6291456 | tf_op jit(solution)/shard_map/dyn,nk->dyk/dot_general | solution.py:28
  88.5 3.2 %add_bitcast_fusion = f32[1,8,256,256]{3,2,1,0:T(8,128)S(1)} fusion(f32[8,256,256]{2,1,0:T(8,128)S(1)} %fusion, f32[8,256,256]{2,0,1:T(8,128)S(1)} %get-tuple-element.16), kind=kOutput, calls=%fused_computation.1 | convolution fusion | flops 1612054528 | bytes 6291456 | tf_op jit(solution)/shard_map/dyn,nk->dyk/dot_general | solution.py:29
  92.2 2.4 %copy.64 = f32[2,8,256,256]{3,2,0,1:T(8,128)} copy(f32[2,8,256,256]{3,2,1,0:T(8,128)S(1)} %pad_maximum_fusion) | data formatting | bytes 8388608 | tf_op jit(solution)/shard_map/stack | solution.py:303
  94.6 4.9 %all-to-all-start.1 = ((f32[2,8,256,256]{3,2,0,1:T(8,128)}), f32[2,8,256,256]{3,2,0,1:T(8,128)}, u32[]{:S(2)}, u32[]{:S(2)}) async-start(f32[2,8,256,256]{3,2,0,1:T(8,128)} %copy.64), calls=%async_computation.1 | async-start | bytes 8388608 | tf_op jit(solution)/shard_map/all_to_all | solution.py:304
  100.2 2.1 reshape.240.row_scale_ref
  102.4 2.1 reshape.241.row_rate_ref
  104.5 0.7 fusion.49
  105.2 0.8 fusion.39
  106.0 4.5 %multiply_sine_fusion = (f32[2048,1]{1,0:T(8,128)}, f32[2048,1]{1,0:T(8,128)}) fusion(f32[2048,1]{1,0:T(8,128)S(1)} %copy.55), kind=kLoop, calls=%fused_computation.13 | loop fusion | flops 2048 | bytes 24576 | tf_op jit(solution)/shard_map/sin | solution.py:24
  110.5 37.2 %all-to-all-done.1 = f32[2,8,256,256]{3,2,0,1:T(8,128)} async-done(((f32[2,8,256,256]{3,2,0,1:T(8,128)}), f32[2,8,256,256]{3,2,0,1:T(8,128)}, u32[]{:S(2)}, u32[]{:S(2)}) %all-to-all-start.1) | async-done | bytes 4194336 | tf_op jit(solution)/shard_map/all_to_all | solution.py:304
  147.7 4.6 %fusion.101 = (f32[1,8,256,256]{3,2,0,1:T(8,128)}, f32[1,8,256,256]{3,2,0,1:T(8,128)}) fusion(f32[2,8,256,256]{3,2,0,1:T(8,128)} %all-to-all-done.1), kind=kLoop, calls=%fused_computation.125 | loop fusion | bytes 8388608 | tf_op jit(solution)/shard_map/slice | solution.py:206
  152.3 38.5 %shard_map.77 = (f32[2,32,64,256]{3,2,1,0:T(8,128)}, f32[8,128]{1,0:T(8,128)}) custom-call(f32[64,64]{1,0:T(8,128)} %get-tuple-element.25.cos_a_ref, f32[64,64]{1,0:T(8,128)} %get-tuple-element.24.sin_a_ref, f32[2048,1]{1,0:T(8,128)} %get-tuple-element.21.twist_cos_ref, f32[2048,1]{1,0:T(8,128)} %get-tuple-element.20.twist_sin_ref, ...), custom_call_target="tpu_custom_call" | custom-call | tf_op jit(solution)/shard_map/pallas_call | solution.py:186
  190.8 1.2 slice.17
  192.0 1.2 broadcast_in_dim.2.value_ref
  193.2 15.4 %shard_map.78 = f32[8,128]{1,0:T(8,128)} custom-call(f32[8,128]{1,0:T(8,128)} %broadcast_in_dim.2.value_ref), custom_call_target="tpu_custom_call" | custom-call | tf_op jit(solution)/shard_map/pallas_call | solution.py:275
  208.7 1.2 slice.18
  (16 shorter events, 1.3 us)
Async XLA Ops:
  3.7 69.3 %all-to-all-start = ((f32[256,8,256]{2,1,0:T(8,128)}), f32[256,8,256]{2,1,0:T(8,128)S(1)}, u32[]{:S(2)}, u32[]{:S(2)}) async-start(f32[256,8,256]{2,1,0:T(8,128)} %bitcast.49), calls=%async_computation | async-start | bytes 4194304 | tf_op jit(solution)/shard_map/all_to_all | solution.py:299
  94.6 5.4 %copy-start = (f32[2048]{0:T(1024)S(1)}, f32[2048]{0:T(1024)}, u32[]{:S(2)}) copy-start(f32[2048]{0:T(1024)} %param.7) | copy-start | bytes 24580
  94.6 53.1 %all-to-all-start.1 = ((f32[2,8,256,256]{3,2,0,1:T(8,128)}), f32[2,8,256,256]{3,2,0,1:T(8,128)}, u32[]{:S(2)}, u32[]{:S(2)}) async-start(f32[2,8,256,256]{3,2,0,1:T(8,128)} %copy.64), calls=%async_computation.1 | async-start | bytes 8388608 | tf_op jit(solution)/shard_map/all_to_all | solution.py:304
  99.5 2.8 %copy-start.1 = (f32[2048]{0:T(1024)S(1)}, f32[2048]{0:T(1024)}, u32[]{:S(2)}) copy-start(f32[2048]{0:T(1024)} %param.9) | copy-start | bytes 24580

commit v2 on v1

--- a/solution.py
+++ b/solution.py
@@ -78,17 +78,17 @@
 
 def y_kernel(norm_factor, cos_a_ref, sin_a_ref, twist_cos_ref, twist_sin_ref,
              cos_b_ref, sin_b_ref, row_scale_ref, row_rate_ref, col_scale_ref, col_shift_ref,
-             col_mix_ref, real_hbm, imag_hbm, out_hbm, sum_ref,
+             col_mix_ref, spectrum_hbm, out_hbm, sum_ref,
              held, step_real, step_imag, staged, in_sems, out_sems):
-    high, low, blocks, rows, width = real_hbm.shape
+    _, high, low, blocks, rows, width = spectrum_hbm.shape
     size_b = low * rows
     size_a = high * blocks
     half = width // 2
     loads = []
-    for part, source in enumerate((real_hbm, imag_hbm)):
+    for part in range(2):
         for index in range(size_b):
             copy = pltpu.make_async_copy(
-                source.at[:, index // rows, :, index % rows, :],
+                spectrum_hbm.at[part, :, index // rows, :, index % rows, :],
                 held.at[part, index],
                 in_sems.at[part, index],
             )
@@ -98,37 +98,47 @@
     def dot(left, right):
         return jnp.dot(left, right, precision=precision_top, preferred_element_type=jnp.float32)
 
-    cos_a = cos_a_ref[...]
-    sin_a = sin_a_ref[...]
-    for index in range(size_b):
-        loads[index].wait()
-        loads[size_b + index].wait()
+    both_a = jnp.concatenate([cos_a_ref[...], sin_a_ref[...]], axis=0)
+
+    def first(index, carry):
+        for part in range(2):
+            pltpu.make_async_copy(
+                spectrum_hbm.at[part, :, index // rows, :, index % rows, :],
+                held.at[part, index],
+                in_sems.at[part, index],
+            ).wait()
         part_real = held[0, index].reshape(size_a, width)
         part_imag = held[1, index].reshape(size_a, width)
-        out_real = dot(cos_a, part_real) - dot(sin_a, part_imag)
-        out_imag = dot(cos_a, part_imag) + dot(sin_a, part_real)
-        rows = pl.ds(index * size_a, size_a)
-        twist_cos = twist_cos_ref[rows, :]
-        twist_sin = twist_sin_ref[rows, :]
+        from_real = dot(both_a, part_real)
+        from_imag = dot(both_a, part_imag)
+        out_real = from_real[:size_a] - from_imag[size_a:]
+        out_imag = from_imag[:size_a] + from_real[size_a:]
+        rows_here = pl.ds(pl.multiple_of(index * size_a, size_a), size_a)
+        twist_cos = twist_cos_ref[rows_here, :]
+        twist_sin = twist_sin_ref[rows_here, :]
         turned_real = out_real * twist_cos - out_imag * twist_sin
         turned_imag = out_real * twist_sin + out_imag * twist_cos
         for side in range(2):
             lanes = slice(side * half, (side + 1) * half)
-            step_real[side, rows, :] = turned_real[:, lanes]
-            step_imag[side, rows, :] = turned_imag[:, lanes]
+            step_real[side, rows_here, :] = turned_real[:, lanes]
+            step_imag[side, rows_here, :] = turned_imag[:, lanes]
+        return carry
+
+    lax.fori_loop(0, size_b, first, 0)
 
     col_scale = col_scale_ref[...]
     col_shift = col_shift_ref[...]
     col_mix = col_mix_ref[...]
-    cos_b = cos_b_ref[...]
-    sin_b = sin_b_ref[...]
+    both_b = jnp.concatenate([cos_b_ref[...], sin_b_ref[...]], axis=0)
 
     def second(index, total):
         picked = pl.ds(index, size_b, stride=size_a)
         part_real = jnp.concatenate([step_real[0, picked, :], step_real[1, picked, :]], axis=1)
         part_imag = jnp.concatenate([step_imag[0, picked, :], step_imag[1, picked, :]], axis=1)
-        spec_real = dot(cos_b, part_real) - dot(sin_b, part_imag)
-        spec_imag = dot(cos_b, part_imag) + dot(sin_b, part_real)
+        from_real = dot(both_b, part_real)
+        from_imag = dot(both_b, part_imag)
+        spec_real = from_real[:size_b] - from_imag[size_b:]
+        spec_imag = from_imag[:size_b] + from_real[size_b:]
         rows = pl.ds(pl.multiple_of(index * size_b, size_b), size_b)
         scale = row_scale_ref[rows, :] * col_scale
         latent_u = spec_real * norm_factor * scale
@@ -189,7 +199,7 @@
             jax.ShapeDtypeStruct((2, size_b, size_a, width), jnp.float32),
             jax.ShapeDtypeStruct((8, 128), jnp.float32),
         ),
-        in_specs=[vmem] * 11 + [anywhere] * 2,
+        in_specs=[vmem] * 11 + [anywhere],
         out_specs=(anywhere, vmem),
         scratch_shapes=[
             pltpu.VMEM((2, size_b, high, blocks, width), jnp.float32),
@@ -203,7 +213,7 @@
     )(
         cos_a, sin_a, twist_cos, twist_sin, cos_b, sin_b,
         row_scale_t, row_rate_t, col_scale.reshape(1, width), col_shift.reshape(1, width),
-        col_mix.reshape(1, width), shaped[0], shaped[1],
+        col_mix.reshape(1, width), shaped,
     )
     return latent.reshape(2, length, width), sums[0, 0]
 

time: 212 us -> 214 us (level)
  Pallas kernels: 53.9 us -> 56.2 us
    slice x1 -> x0, local copies, waits for them, and re-layouts: 4.58 us -> none  [y_stage(): shaped[1]]
    all_to_all x0 -> x1, local copies, waits for them, and re-layouts: none -> 4.54 us  [per_device(): both = lax.all_to_all(both, 'gx', split_axis=1, concat_axis=2, tiled=True)]
    pallas_call x1, Pallas kernels: 38.5 us -> 40.8 us  [y_stage(): pl.pallas_call(functools.partial(y_kernel, norm_factor), out_shape=(jax.S...]
where the time goes in v2:
time: 214 us
  waiting for transfers between devices  90.8 us (42%)
  Pallas kernels  56.2 us (26%)
  starting transfers between devices  20.5 us (10%)
  local copies, waits for them, and re-layouts  19.8 us (9%)
  matrix products  17.5 us (8%)
  other arithmetic  6.53 us (3%)
  between operations  2.55 us (1%)
    all_to_all x1, waiting for transfers between devices, per_device(): lax.all_to_all(outgoing, ('gx', 'gy'), split_axis=0, concat_axis=0, tiled...  53.5 us
    pallas_call x1, Pallas kernels, y_stage(): pl.pallas_call(functools.partial(y_kernel, norm_factor), out_shape=(jax.S...  40.8 us
    all_to_all x1, waiting for transfers between devices, per_device(): both = lax.all_to_all(both, 'gx', split_axis=1, concat_axis=2, tiled=True)  37.3 us
    all_to_all x1, starting transfers between devices, per_device(): lax.all_to_all(outgoing, ('gx', 'gy'), split_axis=0, concat_axis=0, tiled...  15.7 us
    pallas_call x1, Pallas kernels, total_everywhere(): pl.pallas_call(total_kernel, out_shape=jax.ShapeDtypeStruct((8, 128), jnp...  15.4 us
    sin x3, other arithmetic, root_table(): return (jnp.cos(angle), jnp.sin(angle))  5.97 us
    all_to_all x1, starting transfers between devices, per_device(): both = lax.all_to_all(both, 'gx', split_axis=1, concat_axis=2, tiled=True)  4.86 us
    all_to_all x1, local copies, waits for them, and re-layouts, per_device(): both = lax.all_to_all(both, 'gx', split_axis=1, concat_axis=2, tiled=True)  4.54 us
  transfers between devices with their start and end apart: 2, of which 2 were waited for; matrix products, arithmetic and copies ran while one was open for 5% of the time, Pallas kernels for 0%

profile of v2, /device:TPU:1, one launch (start us, length us, event | category | flops | bytes accessed | tf_op | source)
XLA Modules:
  0.0 213.8 jit_solution(18034402160210248068)
XLA Ops:
  0.6 3.1 %copy.59 = f32[8,32,8,256]{3,2,1,0:T(8,128)} copy(f32[8,32,8,256]{3,2,0,1:T(8,128)} %bitcast.48) | data formatting | bytes 4194304 | tf_op jit(solution)/shard_map/transpose | solution.py:307
  3.7 15.7 %all-to-all-start = ((f32[256,8,256]{2,1,0:T(8,128)}), f32[256,8,256]{2,1,0:T(8,128)S(1)}, u32[]{:S(2)}, u32[]{:S(2)}) async-start(f32[256,8,256]{2,1,0:T(8,128)} %bitcast.47), calls=%async_computation | async-start | bytes 4194304 | tf_op jit(solution)/shard_map/all_to_all | solution.py:309
  19.5 53.5 %all-to-all-done = f32[256,8,256]{2,1,0:T(8,128)S(1)} async-done(((f32[256,8,256]{2,1,0:T(8,128)}), f32[256,8,256]{2,1,0:T(8,128)S(1)}, u32[]{:S(2)}, u32[]{:S(2)}) %all-to-all-start) | async-done | bytes 2097184 | tf_op jit(solution)/shard_map/all_to_all | solution.py:309
  73.1 1.2 copy.60
  74.3 2.0 fusion.57
  76.3 2.4 %multiply_subtract_fusion = (f32[8,256,256]{2,0,1:T(8,128)S(1)}, f32[8,256,256]{2,0,1:T(8,128)S(1)}) fusion(f32[8,256,256]{2,0,1:T(8,128)S(1)} %fusion.57, f32[8,256]{1,0:T(8,128)S(1)} %get-tuple-element.21, f32[8,256]{1,0:T(8,128)S(1)} %get-tuple-element.20, f32[256,8,256]{2,1,0:T(8,128)S(1)} %bitcast.44, s32[8]{0:T(128)S(1)} %fusion.73), kind=kOutput, calls=%fused_computation.4 | convolution fusion | flops 53478272 | bytes 8405024 | tf_op jit(solution)/shard_map/ygn,gd->dyn/dot_general | solution.py:44
  78.7 3.2 %fusion.2 = f32[8,256,256]{2,1,0:T(8,128)S(1)} fusion(f32[8,256,256]{2,0,1:T(8,128)S(1)} %get-tuple-element.17), kind=kOutput, calls=%fused_computation.7 | convolution fusion | flops 1611530240 | bytes 4194304 | tf_op jit(solution)/shard_map/dyn,nk->dyk/dot_general | solution.py:30
  81.9 3.4 %fusion = f32[8,256,256]{2,1,0:T(8,128)S(1)} fusion(f32[8,256,256]{2,0,1:T(8,128)S(1)} %get-tuple-element.17), kind=kOutput, calls=%fused_computation.5 | convolution fusion | flops 1611530240 | bytes 4194304 | tf_op jit(solution)/shard_map/dyn,nk->dyk/dot_general | solution.py:31
  85.3 3.2 %subtract_bitcast_fusion = f32[1,8,256,256]{3,2,1,0:T(8,128)S(1)} fusion(f32[8,256,256]{2,1,0:T(8,128)S(1)} %fusion.2, f32[8,256,256]{2,0,1:T(8,128)S(1)} %get-tuple-element.16), kind=kOutput, calls=%fused_computation.2 | convolution fusion | flops 1612054528 | bytes 6291456 | tf_op jit(solution)/shard_map/dyn,nk->dyk/dot_general | solution.py:28
  88.5 3.2 %add_bitcast_fusion = f32[1,8,256,256]{3,2,1,0:T(8,128)S(1)} fusion(f32[8,256,256]{2,1,0:T(8,128)S(1)} %fusion, f32[8,256,256]{2,0,1:T(8,128)S(1)} %get-tuple-element.16), kind=kOutput, calls=%fused_computation.1 | convolution fusion | flops 1612054528 | bytes 6291456 | tf_op jit(solution)/shard_map/dyn,nk->dyk/dot_general | solution.py:29
  92.2 2.4 %copy.65 = f32[2,8,256,256]{3,2,0,1:T(8,128)} copy(f32[2,8,256,256]{3,2,1,0:T(8,128)S(1)} %pad_maximum_fusion) | data formatting | bytes 8388608 | tf_op jit(solution)/shard_map/stack | solution.py:313
  94.6 4.9 %all-to-all-start.1 = ((f32[2,8,256,256]{3,2,0,1:T(8,128)}), f32[2,8,256,256]{3,2,0,1:T(8,128)}, u32[]{:S(2)}, u32[]{:S(2)}) async-start(f32[2,8,256,256]{3,2,0,1:T(8,128)} %copy.65), calls=%async_computation.1 | async-start | bytes 8388608 | tf_op jit(solution)/shard_map/all_to_all | solution.py:314
  100.2 2.1 reshape.234.row_scale_ref
  102.4 2.1 reshape.235.row_rate_ref
  104.5 0.7 fusion.49
  105.2 0.8 fusion.39
  105.9 4.5 %multiply_sine_fusion = (f32[2048,1]{1,0:T(8,128)}, f32[2048,1]{1,0:T(8,128)}) fusion(f32[2048,1]{1,0:T(8,128)S(1)} %copy.56), kind=kLoop, calls=%fused_computation.13 | loop fusion | flops 2048 | bytes 24576 | tf_op jit(solution)/shard_map/sin | solution.py:24
  110.4 37.3 %all-to-all-done.1 = f32[2,8,256,256]{3,2,0,1:T(8,128)} async-done(((f32[2,8,256,256]{3,2,0,1:T(8,128)}), f32[2,8,256,256]{3,2,0,1:T(8,128)}, u32[]{:S(2)}, u32[]{:S(2)}) %all-to-all-start.1) | async-done | bytes 4194336 | tf_op jit(solution)/shard_map/all_to_all | solution.py:314
  147.7 4.5 %copy.66 = f32[2,8,256,256]{3,2,1,0:T(8,128)} copy(f32[2,8,256,256]{3,2,0,1:T(8,128)} %all-to-all-done.1) | data formatting | bytes 8388608 | tf_op jit(solution)/shard_map/all_to_all | solution.py:314
  152.2 40.8 %shard_map.77 = (f32[2,32,64,256]{3,2,1,0:T(8,128)}, f32[8,128]{1,0:T(8,128)}) custom-call(f32[64,64]{1,0:T(8,128)} %get-tuple-element.23.cos_a_ref, f32[64,64]{1,0:T(8,128)} %get-tuple-element.22.sin_a_ref, f32[2048,1]{1,0:T(8,128)} %get-tuple-element.19.twist_cos_ref, f32[2048,1]{1,0:T(8,128)} %get-tuple-element.18.twist_sin_ref, ...), custom_call_target="tpu_custom_call" | custom-call | tf_op jit(solution)/shard_map/pallas_call | solution.py:196
  193.0 1.2 slice.6
  194.2 1.2 broadcast_in_dim.2.value_ref
  195.4 15.4 %shard_map.78 = f32[8,128]{1,0:T(8,128)} custom-call(f32[8,128]{1,0:T(8,128)} %broadcast_in_dim.2.value_ref), custom_call_target="tpu_custom_call" | custom-call | tf_op jit(solution)/shard_map/pallas_call | solution.py:285
  210.8 1.2 slice.7
  (16 shorter events, 1.3 us)
Async XLA Ops:
  3.7 69.3 %all-to-all-start = ((f32[256,8,256]{2,1,0:T(8,128)}), f32[256,8,256]{2,1,0:T(8,128)S(1)}, u32[]{:S(2)}, u32[]{:S(2)}) async-start(f32[256,8,256]{2,1,0:T(8,128)} %bitcast.47), calls=%async_computation | async-start | bytes 4194304 | tf_op jit(solution)/shard_map/all_to_all | solution.py:309
  94.6 5.4 %copy-start = (f32[2048]{0:T(1024)S(1)}, f32[2048]{0:T(1024)}, u32[]{:S(2)}) copy-start(f32[2048]{0:T(1024)} %param.7) | copy-start | bytes 24580
  94.6 53.1 %all-to-all-start.1 = ((f32[2,8,256,256]{3,2,0,1:T(8,128)}), f32[2,8,256,256]{3,2,0,1:T(8,128)}, u32[]{:S(2)}, u32[]{:S(2)}) async-start(f32[2,8,256,256]{3,2,0,1:T(8,128)} %copy.65), calls=%async_computation.1 | async-start | bytes 8388608 | tf_op jit(solution)/shard_map/all_to_all | solution.py:314
  99.5 2.7 %copy-start.1 = (f32[2048]{0:T(1024)S(1)}, f32[2048]{0:T(1024)}, u32[]{:S(2)}) copy-start(f32[2048]{0:T(1024)} %param.9) | copy-start | bytes 24580

commit v3 on v2

--- a/solution.py
+++ b/solution.py
@@ -32,16 +32,17 @@
     return (first, second)
 
 
-def x_stage(rows, devices):
-    count, length = rows.shape
-    width = length // devices
+def x_stage(pieces):
+    blocks, devices, rows, width = pieces.shape
+    length = devices * width
     levels = devices.bit_length() - 1
-    shaped = rows.reshape(count, devices, width)
     group = jnp.arange(devices, dtype=jnp.int32)
     residue = reverse_bits(group, levels)
     cos_8, sin_8 = root_table(group, residue, devices)
-    part_real = jnp.einsum("ygn,gd->dyn", shaped, cos_8, precision=precision_top)
-    part_imag = jnp.einsum("ygn,gd->dyn", shaped, sin_8, precision=precision_top)
+    part_real = jnp.einsum("bgtn,gd->dbtn", pieces, cos_8, precision=precision_top)
+    part_imag = jnp.einsum("bgtn,gd->dbtn", pieces, sin_8, precision=precision_top)
+    part_real = part_real.reshape(devices, blocks * rows, width)
+    part_imag = part_imag.reshape(devices, blocks * rows, width)
     local_index = jnp.arange(width, dtype=jnp.int32)
     twist_cos, twist_sin = root_table(residue, local_index, length)
     twist_cos = twist_cos[:, None, :]
@@ -49,7 +50,8 @@
     turned_real = part_real * twist_cos - part_imag * twist_sin
     turned_imag = part_real * twist_sin + part_imag * twist_cos
     cos_w, sin_w = root_table(local_index, local_index, width)
-    return complex_einsum("dyn,nk->dyk", turned_real, turned_imag, cos_w, sin_w)
+    spec_real, spec_imag = complex_einsum("dyn,nk->dyk", turned_real, turned_imag, cos_w, sin_w)
+    return jnp.stack([spec_real, spec_imag], axis=1)
 
 
 def y_transform(real_part, imag_part):
@@ -80,7 +82,7 @@
              cos_b_ref, sin_b_ref, row_scale_ref, row_rate_ref, col_scale_ref, col_shift_ref,
              col_mix_ref, spectrum_hbm, out_hbm, sum_ref,
              held, step_real, step_imag, staged, in_sems, out_sems):
-    _, high, low, blocks, rows, width = spectrum_hbm.shape
+    high, low, _, blocks, rows, width = spectrum_hbm.shape
     size_b = low * rows
     size_a = high * blocks
     half = width // 2
@@ -88,7 +90,7 @@
     for part in range(2):
         for index in range(size_b):
             copy = pltpu.make_async_copy(
-                spectrum_hbm.at[part, :, index // rows, :, index % rows, :],
+                spectrum_hbm.at[:, index // rows, part, :, index % rows, :],
                 held.at[part, index],
                 in_sems.at[part, index],
             )
@@ -103,7 +105,7 @@
     def first(index, carry):
         for part in range(2):
             pltpu.make_async_copy(
-                spectrum_hbm.at[part, :, index // rows, :, index % rows, :],
+                spectrum_hbm.at[:, index // rows, part, :, index % rows, :],
                 held.at[part, index],
                 in_sems.at[part, index],
             ).wait()
@@ -173,7 +175,8 @@
 
 
 def y_stage(spectrum, row_scale, col_scale, row_rate, col_shift, col_mix, norm_factor, devices, height):
-    _, length, width = spectrum.shape
+    _, _, count, width = spectrum.shape
+    length = devices * count
     size_b = 1 << (length.bit_length() - 1) // 2
     size_a = length // size_b
     blocks = length // height
@@ -192,7 +195,7 @@
     row_rate_t = row_rate.reshape(size_b, size_a).T.reshape(length, 1)
     vmem = pl.BlockSpec(memory_space=pltpu.VMEM)
     anywhere = pl.BlockSpec(memory_space=pl.ANY)
-    shaped = spectrum.reshape(2, high, low, blocks, rows, width)
+    shaped = spectrum.reshape(high, low, 2, blocks, rows, width)
     latent, sums = pl.pallas_call(
         functools.partial(y_kernel, norm_factor),
         out_shape=(
@@ -304,19 +307,16 @@
     devices = lax.axis_size("gx")
     planes, height, width = field.shape
     rows = height // devices
-    outgoing = field.reshape(planes, devices, rows, width).transpose(1, 0, 2, 3)
-    outgoing = outgoing.reshape(devices * planes, rows, width)
-    incoming = lax.all_to_all(outgoing, ("gx", "gy"), split_axis=0, concat_axis=0, tiled=True)
-    incoming = incoming.reshape(devices, planes, rows, width).transpose(1, 2, 0, 3)
-    block = incoming.reshape(planes * rows, devices * width)
-    spec_real, spec_imag = x_stage(block, devices)
-    both = jnp.stack([spec_real, spec_imag])
-    both = lax.all_to_all(both, "gx", split_axis=1, concat_axis=2, tiled=True)
-    length = both.shape[2]
+    outgoing = field.reshape(planes * devices, rows, width)
+    incoming = lax.all_to_all(outgoing, ("gy", "gx"), split_axis=0, concat_axis=0, tiled=True)
+    incoming = incoming.reshape(planes, devices, rows, width)
+    both = x_stage(incoming)
+    both = lax.all_to_all(both, "gx", split_axis=0, concat_axis=0, tiled=True)
+    length = both.shape[0] * both.shape[2]
     total_cols = both.shape[3] * devices
     norm_factor = 1.0 / math.sqrt(length * total_cols)
     latent, part_sum = y_stage(
-        both[:, 0], row_scale, col_scale, row_rate, col_shift, col_mix, norm_factor, devices, height
+        both, row_scale, col_scale, row_rate, col_shift, col_mix, norm_factor, devices, height
     )
     total_sum = total_everywhere(part_sum)
     mode_count = length * total_cols * lax.axis_size("gy")

time: 214 us -> 208 us (0.972)
  local copies, waits for them, and re-layouts: 19.8 us -> 11.9 us
    all_to_all x1 -> x0, local copies, waits for them, and re-layouts: 4.54 us -> none  [per_device(): both = lax.all_to_all(both, 'gx', split_axis=1, concat_axis=2, tiled=True)]
    transpose x2 -> x0, local copies, waits for them, and re-layouts: 4.33 us -> none  [the longest x1 3.11 us: per_device(): outgoing = field.reshape(planes, devices, rows, width).transpose(1, 0, 2, 3)]
where the time goes in v3:
time: 208 us; the launch traced here: 207 us
  waiting for transfers between devices  90.9 us (44%)
  Pallas kernels  56.6 us (27%)
  starting transfers between devices  21.5 us (10%)
  matrix products  17.5 us (8%)
  local copies, waits for them, and re-layouts  11.9 us (6%)
  other arithmetic  6.52 us (3%)
  between operations  2.53 us (1%)
    all_to_all x1, waiting for transfers between devices, per_device(): lax.all_to_all(outgoing, ('gy', 'gx'), split_axis=0, concat_axis=0, tiled...  52.9 us
    pallas_call x1, Pallas kernels, y_stage(): pl.pallas_call(functools.partial(y_kernel, norm_factor), out_shape=(jax.S...  40.8 us
    all_to_all x1, waiting for transfers between devices, per_device(): both = lax.all_to_all(both, 'gx', split_axis=0, concat_axis=0, tiled=True)  38 us
    pallas_call x1, Pallas kernels, total_everywhere(): pl.pallas_call(total_kernel, out_shape=jax.ShapeDtypeStruct((8, 128), jnp...  15.8 us
    all_to_all x1, starting transfers between devices, per_device(): lax.all_to_all(outgoing, ('gy', 'gx'), split_axis=0, concat_axis=0, tiled...  15.7 us
    sin x3, other arithmetic, root_table(): return (jnp.cos(angle), jnp.sin(angle))  5.95 us
    all_to_all x1, starting transfers between devices, per_device(): both = lax.all_to_all(both, 'gx', split_axis=0, concat_axis=0, tiled=True)  5.81 us
  transfers between devices with their start and end apart: 2, of which 2 were waited for; matrix products, arithmetic and copies ran while one was open for 5% of the time, Pallas kernels for 0%

profile of v3, /device:TPU:1, one launch (start us, length us, event | category | flops | bytes accessed | tf_op | source)
XLA Modules:
  0.0 207.3 jit_solution(7620838490607955316)
XLA Ops:
  0.6 15.7 %all-to-all-start = ((f32[256,8,256]{2,1,0:T(8,128)}), f32[256,8,256]{2,1,0:T(8,128)S(1)}, u32[]{:S(2)}, u32[]{:S(2)}) async-start(f32[256,8,256]{2,1,0:T(8,128)} %bitcast.43), calls=%async_computation | async-start | bytes 4194304 | tf_op jit(solution)/shard_map/all_to_all | solution.py:311
  16.4 52.9 %all-to-all-done = f32[256,8,256]{2,1,0:T(8,128)S(1)} async-done(((f32[256,8,256]{2,1,0:T(8,128)}), f32[256,8,256]{2,1,0:T(8,128)S(1)}, u32[]{:S(2)}, u32[]{:S(2)}) %all-to-all-start) | async-done | bytes 2097184 | tf_op jit(solution)/shard_map/all_to_all | solution.py:311
  69.3 0.9 copy.45
  70.2 2.0 fusion.57
  72.2 2.4 %multiply_subtract_fusion = (f32[8,256,256]{2,0,1:T(8,128)S(1)}, f32[8,256,256]{2,0,1:T(8,128)S(1)}) fusion(f32[8,256,256]{2,0,1:T(8,128)S(1)} %fusion.57, f32[8,256]{1,0:T(8,128)S(1)} %get-tuple-element.19, f32[8,256]{1,0:T(8,128)S(1)} %get-tuple-element.18, f32[256,256,8]{1,2,0:T(8,128)S(1)} %bitcast.41, s32[8]{0:T(128)S(1)} %fusion.73), kind=kOutput, calls=%fused_computation.4 | convolution fusion | flops 53478272 | bytes 8405024 | tf_op jit(solution)/shard_map/bgtn,gd->dbtn/dot_general | solution.py:43
  74.6 3.2 %fusion.2 = f32[8,256,256]{2,1,0:T(8,128)S(1)} fusion(f32[8,256,256]{2,0,1:T(8,128)S(1)} %get-tuple-element.15), kind=kOutput, calls=%fused_computation.7 | convolution fusion | flops 1611530240 | bytes 4194304 | tf_op jit(solution)/shard_map/dyn,nk->dyk/dot_general | solution.py:30
  77.8 3.2 %fusion = f32[8,256,256]{2,1,0:T(8,128)S(1)} fusion(f32[8,256,256]{2,0,1:T(8,128)S(1)} %get-tuple-element.15), kind=kOutput, calls=%fused_computation.5 | convolution fusion | flops 1611530240 | bytes 4194304 | tf_op jit(solution)/shard_map/dyn,nk->dyk/dot_general | solution.py:31
  81.0 3.4 %subtract_bitcast_fusion = f32[8,1,256,256]{3,2,0,1:T(8,128)S(1)} fusion(f32[8,256,256]{2,1,0:T(8,128)S(1)} %fusion.2, f32[8,256,256]{2,0,1:T(8,128)S(1)} %get-tuple-element.14), kind=kOutput, calls=%fused_computation.2 | convolution fusion | flops 1612054528 | bytes 6291456 | tf_op jit(solution)/shard_map/dyn,nk->dyk/dot_general | solution.py:28
  84.5 3.2 %add_bitcast_fusion = f32[8,1,256,256]{3,2,0,1:T(8,128)S(1)} fusion(f32[8,256,256]{2,1,0:T(8,128)S(1)} %fusion, f32[8,256,256]{2,0,1:T(8,128)S(1)} %get-tuple-element.14), kind=kOutput, calls=%fused_computation.1 | convolution fusion | flops 1612054528 | bytes 6291456 | tf_op jit(solution)/shard_map/dyn,nk->dyk/dot_general | solution.py:29
  87.7 0.4 pad_maximum_fusion
  88.1 2.4 %copy.50 = f32[8,2,256,256]{3,2,1,0:T(8,128)} copy(f32[8,2,256,256]{3,2,0,1:T(8,128)S(1)} %pad_maximum_fusion) | data formatting | bytes 8388608 | tf_op jit(solution)/shard_map/stack | solution.py:54
  90.6 5.8 %all-to-all-start.1 = ((f32[8,2,256,256]{3,2,1,0:T(8,128)}), f32[8,2,256,256]{3,2,1,0:T(8,128)}, u32[]{:S(2)}, u32[]{:S(2)}) async-start(f32[8,2,256,256]{3,2,1,0:T(8,128)} %copy.50), calls=%async_computation.1 | async-start | bytes 8388608 | tf_op jit(solution)/shard_map/all_to_all | solution.py:314
  96.5 0.4 copy.42
  97.0 2.1 %reshape.234.row_scale_ref = f32[2048,1]{1,0:T(8,128)} reshape(f32[64,32]{1,0:T(8,128)S(1)} %copy.43) | data formatting | bytes 16384 | tf_op jit(solution)/shard_map/reshape | solution.py:194
  99.3 2.1 %reshape.235.row_rate_ref = f32[2048,1]{1,0:T(8,128)} reshape(f32[64,32]{1,0:T(8,128)S(1)} %copy.44) | data formatting | bytes 16384 | tf_op jit(solution)/shard_map/reshape | solution.py:195
  101.4 0.7 fusion.49
  102.1 0.8 fusion.39
  102.9 4.5 %multiply_sine_fusion = (f32[2048,1]{1,0:T(8,128)}, f32[2048,1]{1,0:T(8,128)}) fusion(f32[2048,1]{1,0:T(8,128)S(1)} %copy.42), kind=kLoop, calls=%fused_computation.13 | loop fusion | flops 2048 | bytes 24576 | tf_op jit(solution)/shard_map/sin | solution.py:24
  107.3 38.0 %all-to-all-done.1 = f32[8,2,256,256]{3,2,1,0:T(8,128)} async-done(((f32[8,2,256,256]{3,2,1,0:T(8,128)}), f32[8,2,256,256]{3,2,1,0:T(8,128)}, u32[]{:S(2)}, u32[]{:S(2)}) %all-to-all-start.1) | async-done | bytes 4194336 | tf_op jit(solution)/shard_map/all_to_all | solution.py:314
  145.3 40.8 %shard_map.77 = (f32[2,32,64,256]{3,2,1,0:T(8,128)}, f32[8,128]{1,0:T(8,128)}) custom-call(f32[64,64]{1,0:T(8,128)} %get-tuple-element.21.cos_a_ref, f32[64,64]{1,0:T(8,128)} %get-tuple-element.20.sin_a_ref, f32[2048,1]{1,0:T(8,128)} %get-tuple-element.17.twist_cos_ref, f32[2048,1]{1,0:T(8,128)} %get-tuple-element.16.twist_sin_ref, ...), custom_call_target="tpu_custom_call" | custom-call | tf_op jit(solution)/shard_map/pallas_call | solution.py:199
  186.1 1.2 slice.6
  187.3 1.2 broadcast_in_dim.2.value_ref
  188.5 15.8 %shard_map.78 = f32[8,128]{1,0:T(8,128)} custom-call(f32[8,128]{1,0:T(8,128)} %broadcast_in_dim.2.value_ref), custom_call_target="tpu_custom_call" | custom-call | tf_op jit(solution)/shard_map/pallas_call | solution.py:288
  204.3 1.2 slice.7
  (14 shorter events, 0.6 us)
Async XLA Ops:
  0.6 68.7 %all-to-all-start = ((f32[256,8,256]{2,1,0:T(8,128)}), f32[256,8,256]{2,1,0:T(8,128)S(1)}, u32[]{:S(2)}, u32[]{:S(2)}) async-start(f32[256,8,256]{2,1,0:T(8,128)} %bitcast.43), calls=%async_computation | async-start | bytes 4194304 | tf_op jit(solution)/shard_map/all_to_all | solution.py:311
  90.6 6.3 %copy-start = (f32[2048]{0:T(1024)S(1)}, f32[2048]{0:T(1024)}, u32[]{:S(2)}) copy-start(f32[2048]{0:T(1024)} %param.7) | copy-start | bytes 24580
  90.6 54.7 %all-to-all-start.1 = ((f32[8,2,256,256]{3,2,1,0:T(8,128)}), f32[8,2,256,256]{3,2,1,0:T(8,128)}, u32[]{:S(2)}, u32[]{:S(2)}) async-start(f32[8,2,256,256]{3,2,1,0:T(8,128)} %copy.50), calls=%async_computation.1 | async-start | bytes 8388608 | tf_op jit(solution)/shard_map/all_to_all | solution.py:314
  96.4 2.8 %copy-start.1 = (f32[2048]{0:T(1024)S(1)}, f32[2048]{0:T(1024)}, u32[]{:S(2)}) copy-start(f32[2048]{0:T(1024)} %param.9) | copy-start | bytes 24580

commit v4 on v3

--- a/solution.py
+++ b/solution.py
@@ -218,7 +218,7 @@
         row_scale_t, row_rate_t, col_scale.reshape(1, width), col_shift.reshape(1, width),
         col_mix.reshape(1, width), shaped,
     )
-    return latent.reshape(2, length, width), sums[0, 0]
+    return latent.reshape(2, length, width), sums
 
 MESH_IDS = pl.DeviceIdType.MESH
 
@@ -281,10 +281,9 @@
         copy.wait_send()
 
 
-def total_everywhere(value):
+def total_everywhere(tile):
     count_x = lax.axis_size("gx")
     count_y = lax.axis_size("gy")
-    tile = jnp.broadcast_to(value, (8, 128)).astype(jnp.float32)
     result = pl.pallas_call(
         total_kernel,
         out_shape=jax.ShapeDtypeStruct((8, 128), jnp.float32),

time: 208 us -> 205 us (0.986)
  local copies, waits for them, and re-layouts: 11.9 us -> 9.45 us
where the time goes in v4:
time: 205 us
  waiting for transfers between devices  90.9 us (44%)
  Pallas kernels  56.7 us (28%)
  starting transfers between devices  21.5 us (10%)
  matrix products  17.5 us (9%)
  local copies, waits for them, and re-layouts  9.45 us (5%)
  other arithmetic  6.52 us (3%)
  between operations  2.53 us (1%)
    all_to_all x1, waiting for transfers between devices, per_device(): lax.all_to_all(outgoing, ('gy', 'gx'), split_axis=0, concat_axis=0, tiled...  52.9 us
    pallas_call x1, Pallas kernels, y_stage(): pl.pallas_call(functools.partial(y_kernel, norm_factor), out_shape=(jax.S...  40.8 us
    all_to_all x1, waiting for transfers between devices, per_device(): both = lax.all_to_all(both, 'gx', split_axis=0, concat_axis=0, tiled=True)  38 us
    pallas_call x1, Pallas kernels, total_everywhere(): pl.pallas_call(total_kernel, out_shape=jax.ShapeDtypeStruct((8, 128), jnp...  16 us
    all_to_all x1, starting transfers between devices, per_device(): lax.all_to_all(outgoing, ('gy', 'gx'), split_axis=0, concat_axis=0, tiled...  15.7 us
    sin x3, other arithmetic, root_table(): return (jnp.cos(angle), jnp.sin(angle))  5.95 us
    all_to_all x1, starting transfers between devices, per_device(): both = lax.all_to_all(both, 'gx', split_axis=0, concat_axis=0, tiled=True)  5.81 us
  transfers between devices with their start and end apart: 2, of which 2 were waited for; matrix products, arithmetic and copies ran while one was open for 5% of the time, Pallas kernels for 0%

profile of v4, /device:TPU:1, one launch (start us, length us, event | category | flops | bytes accessed | tf_op | source)
XLA Modules:
  0.0 205.0 jit_solution(16819130644886356619)
XLA Ops:
  0.6 15.7 %all-to-all-start = ((f32[256,8,256]{2,1,0:T(8,128)}), f32[256,8,256]{2,1,0:T(8,128)S(1)}, u32[]{:S(2)}, u32[]{:S(2)}) async-start(f32[256,8,256]{2,1,0:T(8,128)} %bitcast.42), calls=%async_computation | async-start | bytes 4194304 | tf_op jit(solution)/shard_map/all_to_all | solution.py:310
  16.3 0.1 fusion.61
  16.4 52.9 %all-to-all-done = f32[256,8,256]{2,1,0:T(8,128)S(1)} async-done(((f32[256,8,256]{2,1,0:T(8,128)}), f32[256,8,256]{2,1,0:T(8,128)S(1)}, u32[]{:S(2)}, u32[]{:S(2)}) %all-to-all-start) | async-done | bytes 2097184 | tf_op jit(solution)/shard_map/all_to_all | solution.py:310
  69.3 0.9 copy.45
  70.2 2.0 fusion.57
  72.2 2.4 %multiply_subtract_fusion = (f32[8,256,256]{2,0,1:T(8,128)S(1)}, f32[8,256,256]{2,0,1:T(8,128)S(1)}) fusion(f32[8,256,256]{2,0,1:T(8,128)S(1)} %fusion.57, f32[8,256]{1,0:T(8,128)S(1)} %get-tuple-element.19, f32[8,256]{1,0:T(8,128)S(1)} %get-tuple-element.18, f32[256,256,8]{1,2,0:T(8,128)S(1)} %bitcast.40, s32[8]{0:T(128)S(1)} %fusion.73), kind=kOutput, calls=%fused_computation.4 | convolution fusion | flops 53478272 | bytes 8405024 | tf_op jit(solution)/shard_map/bgtn,gd->dbtn/dot_general | solution.py:43
  74.6 3.2 %fusion.2 = f32[8,256,256]{2,1,0:T(8,128)S(1)} fusion(f32[8,256,256]{2,0,1:T(8,128)S(1)} %get-tuple-element.15), kind=kOutput, calls=%fused_computation.7 | convolution fusion | flops 1611530240 | bytes 4194304 | tf_op jit(solution)/shard_map/dyn,nk->dyk/dot_general | solution.py:30
  77.8 3.2 %fusion = f32[8,256,256]{2,1,0:T(8,128)S(1)} fusion(f32[8,256,256]{2,0,1:T(8,128)S(1)} %get-tuple-element.15), kind=kOutput, calls=%fused_computation.5 | convolution fusion | flops 1611530240 | bytes 4194304 | tf_op jit(solution)/shard_map/dyn,nk->dyk/dot_general | solution.py:31
  81.0 3.4 %subtract_bitcast_fusion = f32[8,1,256,256]{3,2,0,1:T(8,128)S(1)} fusion(f32[8,256,256]{2,1,0:T(8,128)S(1)} %fusion.2, f32[8,256,256]{2,0,1:T(8,128)S(1)} %get-tuple-element.14), kind=kOutput, calls=%fused_computation.2 | convolution fusion | flops 1612054528 | bytes 6291456 | tf_op jit(solution)/shard_map/dyn,nk->dyk/dot_general | solution.py:28
  84.5 3.2 %add_bitcast_fusion = f32[8,1,256,256]{3,2,0,1:T(8,128)S(1)} fusion(f32[8,256,256]{2,1,0:T(8,128)S(1)} %fusion, f32[8,256,256]{2,0,1:T(8,128)S(1)} %get-tuple-element.14), kind=kOutput, calls=%fused_computation.1 | convolution fusion | flops 1612054528 | bytes 6291456 | tf_op jit(solution)/shard_map/dyn,nk->dyk/dot_general | solution.py:29
  87.7 0.4 pad_maximum_fusion
  88.1 2.4 %copy.50 = f32[8,2,256,256]{3,2,1,0:T(8,128)} copy(f32[8,2,256,256]{3,2,0,1:T(8,128)S(1)} %pad_maximum_fusion) | data formatting | bytes 8388608 | tf_op jit(solution)/shard_map/stack | solution.py:54
  90.6 5.8 %all-to-all-start.1 = ((f32[8,2,256,256]{3,2,1,0:T(8,128)}), f32[8,2,256,256]{3,2,1,0:T(8,128)}, u32[]{:S(2)}, u32[]{:S(2)}) async-start(f32[8,2,256,256]{3,2,1,0:T(8,128)} %copy.50), calls=%async_computation.1 | async-start | bytes 8388608 | tf_op jit(solution)/shard_map/all_to_all | solution.py:313
  96.5 0.4 copy.42
  97.0 0.1 copy.43
  97.0 2.1 %reshape.234.row_scale_ref = f32[2048,1]{1,0:T(8,128)} reshape(f32[64,32]{1,0:T(8,128)S(1)} %copy.43) | data formatting | bytes 16384 | tf_op jit(solution)/shard_map/reshape | solution.py:194
  99.3 2.1 %reshape.235.row_rate_ref = f32[2048,1]{1,0:T(8,128)} reshape(f32[64,32]{1,0:T(8,128)S(1)} %copy.44) | data formatting | bytes 16384 | tf_op jit(solution)/shard_map/reshape | solution.py:195
  101.4 0.7 fusion.49
  102.1 0.8 fusion.39
  102.9 4.5 %multiply_sine_fusion = (f32[2048,1]{1,0:T(8,128)}, f32[2048,1]{1,0:T(8,128)}) fusion(f32[2048,1]{1,0:T(8,128)S(1)} %copy.42), kind=kLoop, calls=%fused_computation.13 | loop fusion | flops 2048 | bytes 24576 | tf_op jit(solution)/shard_map/sin | solution.py:24
  107.3 38.0 %all-to-all-done.1 = f32[8,2,256,256]{3,2,1,0:T(8,128)} async-done(((f32[8,2,256,256]{3,2,1,0:T(8,128)}), f32[8,2,256,256]{3,2,1,0:T(8,128)}, u32[]{:S(2)}, u32[]{:S(2)}) %all-to-all-start.1) | async-done | bytes 4194336 | tf_op jit(solution)/shard_map/all_to_all | solution.py:313
  145.3 40.8 %shard_map.77 = (f32[2,32,64,256]{3,2,1,0:T(8,128)}, f32[8,128]{1,0:T(8,128)}) custom-call(f32[64,64]{1,0:T(8,128)} %get-tuple-element.21.cos_a_ref, f32[64,64]{1,0:T(8,128)} %get-tuple-element.20.sin_a_ref, f32[2048,1]{1,0:T(8,128)} %get-tuple-element.17.twist_cos_ref, f32[2048,1]{1,0:T(8,128)} %get-tuple-element.16.twist_sin_ref, ...), custom_call_target="tpu_custom_call" | custom-call | tf_op jit(solution)/shard_map/pallas_call | solution.py:199
  186.1 16.0 %shard_map.78 = f32[8,128]{1,0:T(8,128)} custom-call(f32[8,128]{1,0:T(8,128)} %get-tuple-element.5.value_ref), custom_call_target="tpu_custom_call" | custom-call | tf_op jit(solution)/shard_map/pallas_call | solution.py:287
  202.0 1.2 slice.3
  (12 shorter events, 0.4 us)
Async XLA Ops:
  0.6 68.7 %all-to-all-start = ((f32[256,8,256]{2,1,0:T(8,128)}), f32[256,8,256]{2,1,0:T(8,128)S(1)}, u32[]{:S(2)}, u32[]{:S(2)}) async-start(f32[256,8,256]{2,1,0:T(8,128)} %bitcast.42), calls=%async_computation | async-start | bytes 4194304 | tf_op jit(solution)/shard_map/all_to_all | solution.py:310
  90.6 6.3 %copy-start = (f32[2048]{0:T(1024)S(1)}, f32[2048]{0:T(1024)}, u32[]{:S(2)}) copy-start(f32[2048]{0:T(1024)} %param.7) | copy-start | bytes 24580
  90.6 54.7 %all-to-all-start.1 = ((f32[8,2,256,256]{3,2,1,0:T(8,128)}), f32[8,2,256,256]{3,2,1,0:T(8,128)}, u32[]{:S(2)}, u32[]{:S(2)}) async-start(f32[8,2,256,256]{3,2,1,0:T(8,128)} %copy.50), calls=%async_computation.1 | async-start | bytes 8388608 | tf_op jit(solution)/shard_map/all_to_all | solution.py:313
  96.4 2.8 %copy-start.1 = (f32[2048]{0:T(1024)S(1)}, f32[2048]{0:T(1024)}, u32[]{:S(2)}) copy-start(f32[2048]{0:T(1024)} %param.9) | copy-start | bytes 24580

commit v5 on v4

--- a/solution.py
+++ b/solution.py
@@ -9,6 +9,7 @@
 from jax.sharding import PartitionSpec as P
 
 precision_top = lax.Precision.HIGHEST
+precision_mid = lax.Precision.HIGH
 
 
 def reverse_bits(value, count):
@@ -24,11 +25,11 @@
     return (jnp.cos(angle), jnp.sin(angle))
 
 
-def complex_einsum(form, real_part, imag_part, cos_part, sin_part):
-    first = jnp.einsum(form, real_part, cos_part, precision=precision_top)
-    second = jnp.einsum(form, real_part, sin_part, precision=precision_top)
-    first = first - jnp.einsum(form, imag_part, sin_part, precision=precision_top)
-    second = second + jnp.einsum(form, imag_part, cos_part, precision=precision_top)
+def complex_einsum(form, real_part, imag_part, cos_part, sin_part, precision=precision_top):
+    first = jnp.einsum(form, real_part, cos_part, precision=precision)
+    second = jnp.einsum(form, real_part, sin_part, precision=precision)
+    first = first - jnp.einsum(form, imag_part, sin_part, precision=precision)
+    second = second + jnp.einsum(form, imag_part, cos_part, precision=precision)
     return (first, second)
 
 
@@ -50,7 +51,9 @@
     turned_real = part_real * twist_cos - part_imag * twist_sin
     turned_imag = part_real * twist_sin + part_imag * twist_cos
     cos_w, sin_w = root_table(local_index, local_index, width)
-    spec_real, spec_imag = complex_einsum("dyn,nk->dyk", turned_real, turned_imag, cos_w, sin_w)
+    spec_real, spec_imag = complex_einsum(
+        "dyn,nk->dyk", turned_real, turned_imag, cos_w, sin_w, precision_mid
+    )
     return jnp.stack([spec_real, spec_imag], axis=1)
 
 
@@ -98,7 +101,7 @@
             loads.append(copy)
 
     def dot(left, right):
-        return jnp.dot(left, right, precision=precision_top, preferred_element_type=jnp.float32)
+        return jnp.dot(left, right, precision=precision_mid, preferred_element_type=jnp.float32)
 
     both_a = jnp.concatenate([cos_a_ref[...], sin_a_ref[...]], axis=0)
 

time: 205 us -> 195 us (0.951)
  Pallas kernels: 56.7 us -> 49.7 us
  matrix products: 17.5 us -> 14.4 us
    pallas_call x1, Pallas kernels: 40.8 us -> 33.7 us  [y_stage(): pl.pallas_call(functools.partial(y_kernel, norm_factor), out_shape=(jax.S...]
    dot_general x4, matrix products: 13.1 us -> 9.98 us  [the longest x1 2.63 us: complex_einsum(): first = jnp.einsum(form, real_part, cos_part, precision=precision)]
  transfers between devices with their start and end apart: 2 -> 2, of which waited for: 2 -> 2; matrix products, arithmetic and copies ran while one was open for 5% -> 6% of each run, Pallas kernels for 0% -> 0%
where the time goes in v5:
time: 195 us
  waiting for transfers between devices  90.9 us (47%)
  Pallas kernels  49.7 us (25%)
  starting transfers between devices  21.5 us (11%)
  matrix products  14.4 us (7%)
  local copies, waits for them, and re-layouts  9.45 us (5%)
  other arithmetic  6.52 us (3%)
  between operations  2.53 us (1%)
    all_to_all x1, waiting for transfers between devices, per_device(): lax.all_to_all(outgoing, ('gy', 'gx'), split_axis=0, concat_axis=0, tiled...  52.9 us
    all_to_all x1, waiting for transfers between devices, per_device(): both = lax.all_to_all(both, 'gx', split_axis=0, concat_axis=0, tiled=True)  38 us
    pallas_call x1, Pallas kernels, y_stage(): pl.pallas_call(functools.partial(y_kernel, norm_factor), out_shape=(jax.S...  33.7 us
    pallas_call x1, Pallas kernels, total_everywhere(): pl.pallas_call(total_kernel, out_shape=jax.ShapeDtypeStruct((8, 128), jnp...  16 us
    all_to_all x1, starting transfers between devices, per_device(): lax.all_to_all(outgoing, ('gy', 'gx'), split_axis=0, concat_axis=0, tiled...  15.7 us
    sin x3, other arithmetic, root_table(): return (jnp.cos(angle), jnp.sin(angle))  5.95 us
    all_to_all x1, starting transfers between devices, per_device(): both = lax.all_to_all(both, 'gx', split_axis=0, concat_axis=0, tiled=True)  5.81 us
  transfers between devices with their start and end apart: 2, of which 2 were waited for; matrix products, arithmetic and copies ran while one was open for 6% of the time, Pallas kernels for 0%

profile of v5, /device:TPU:1, one launch (start us, length us, event | category | flops | bytes accessed | tf_op | source)
XLA Modules:
  0.0 194.9 jit_solution(13764768814420226098)
XLA Ops:
  0.6 15.7 %all-to-all-start = ((f32[256,8,256]{2,1,0:T(8,128)}), f32[256,8,256]{2,1,0:T(8,128)S(1)}, u32[]{:S(2)}, u32[]{:S(2)}) async-start(f32[256,8,256]{2,1,0:T(8,128)} %bitcast.42), calls=%async_computation | async-start | bytes 4194304 | tf_op jit(solution)/shard_map/all_to_all | solution.py:313
  16.3 0.1 fusion.61
  16.4 52.9 %all-to-all-done = f32[256,8,256]{2,1,0:T(8,128)S(1)} async-done(((f32[256,8,256]{2,1,0:T(8,128)}), f32[256,8,256]{2,1,0:T(8,128)S(1)}, u32[]{:S(2)}, u32[]{:S(2)}) %all-to-all-start) | async-done | bytes 2097184 | tf_op jit(solution)/shard_map/all_to_all | solution.py:313
  69.3 0.9 copy.45
  70.2 2.0 %fusion.57 = f32[8,256,256]{2,0,1:T(8,128)S(1)} fusion(f32[256,256,8]{1,2,0:T(8,128)S(1)} %bitcast.39, s32[8]{0:T(128)S(1)} %fusion.73), kind=kOutput, calls=%fused_computation.75 | convolution fusion | flops 50332544 | bytes 4194336 | tf_op jit(solution)/shard_map/bgtn,gd->dbtn/dot_general | solution.py:43
  72.2 2.4 %multiply_subtract_fusion = (f32[8,256,256]{2,0,1:T(8,128)S(1)}, f32[8,256,256]{2,0,1:T(8,128)S(1)}) fusion(f32[8,256,256]{2,0,1:T(8,128)S(1)} %fusion.57, f32[8,256]{1,0:T(8,128)S(1)} %get-tuple-element.19, f32[8,256]{1,0:T(8,128)S(1)} %get-tuple-element.18, f32[256,256,8]{1,2,0:T(8,128)S(1)} %bitcast.40, s32[8]{0:T(128)S(1)} %fusion.73), kind=kOutput, calls=%fused_computation.4 | convolution fusion | flops 53478272 | bytes 8405024 | tf_op jit(solution)/shard_map/bgtn,gd->dbtn/dot_general | solution.py:44
  74.6 2.5 %fusion.2 = f32[8,256,256]{2,1,0:T(8,128)S(1)} fusion(f32[8,256,256]{2,0,1:T(8,128)S(1)} %get-tuple-element.15), kind=kOutput, calls=%fused_computation.7 | convolution fusion | flops 806223872 | bytes 4194304 | tf_op jit(solution)/shard_map/dyn,nk->dyk/dot_general | solution.py:31
  77.1 2.4 %fusion = f32[8,256,256]{2,1,0:T(8,128)S(1)} fusion(f32[8,256,256]{2,0,1:T(8,128)S(1)} %get-tuple-element.15), kind=kOutput, calls=%fused_computation.5 | convolution fusion | flops 806223872 | bytes 4194304 | tf_op jit(solution)/shard_map/dyn,nk->dyk/dot_general | solution.py:32
  79.5 2.6 %subtract_bitcast_fusion = f32[8,1,256,256]{3,2,0,1:T(8,128)S(1)} fusion(f32[8,256,256]{2,1,0:T(8,128)S(1)} %fusion.2, f32[8,256,256]{2,0,1:T(8,128)S(1)} %get-tuple-element.14), kind=kOutput, calls=%fused_computation.2 | convolution fusion | flops 806748160 | bytes 6291456 | tf_op jit(solution)/shard_map/dyn,nk->dyk/dot_general | solution.py:29
  82.2 2.5 %add_bitcast_fusion = f32[8,1,256,256]{3,2,0,1:T(8,128)S(1)} fusion(f32[8,256,256]{2,1,0:T(8,128)S(1)} %fusion, f32[8,256,256]{2,0,1:T(8,128)S(1)} %get-tuple-element.14), kind=kOutput, calls=%fused_computation.1 | convolution fusion | flops 806748160 | bytes 6291456 | tf_op jit(solution)/shard_map/dyn,nk->dyk/dot_general | solution.py:30
  84.6 0.4 pad_maximum_fusion
  85.0 2.4 %copy.50 = f32[8,2,256,256]{3,2,1,0:T(8,128)} copy(f32[8,2,256,256]{3,2,0,1:T(8,128)S(1)} %pad_maximum_fusion) | data formatting | bytes 8388608 | tf_op jit(solution)/shard_map/stack | solution.py:57
  87.5 5.8 %all-to-all-start.1 = ((f32[8,2,256,256]{3,2,1,0:T(8,128)}), f32[8,2,256,256]{3,2,1,0:T(8,128)}, u32[]{:S(2)}, u32[]{:S(2)}) async-start(f32[8,2,256,256]{3,2,1,0:T(8,128)} %copy.50), calls=%async_computation.1 | async-start | bytes 8388608 | tf_op jit(solution)/shard_map/all_to_all | solution.py:316
  93.4 0.4 copy.42
  94.0 2.1 %reshape.234.row_scale_ref = f32[2048,1]{1,0:T(8,128)} reshape(f32[64,32]{1,0:T(8,128)S(1)} %copy.43) | data formatting | bytes 16384 | tf_op jit(solution)/shard_map/reshape | solution.py:197
  96.1 0.1 copy.44
  96.2 2.1 %reshape.235.row_rate_ref = f32[2048,1]{1,0:T(8,128)} reshape(f32[64,32]{1,0:T(8,128)S(1)} %copy.44) | data formatting | bytes 16384 | tf_op jit(solution)/shard_map/reshape | solution.py:198
  98.3 0.7 fusion.49
  99.0 0.8 fusion.39
  99.8 4.5 %multiply_sine_fusion = (f32[2048,1]{1,0:T(8,128)}, f32[2048,1]{1,0:T(8,128)}) fusion(f32[2048,1]{1,0:T(8,128)S(1)} %copy.42), kind=kLoop, calls=%fused_computation.13 | loop fusion | flops 2048 | bytes 24576 | tf_op jit(solution)/shard_map/sin | solution.py:25
  104.3 38.0 %all-to-all-done.1 = f32[8,2,256,256]{3,2,1,0:T(8,128)} async-done(((f32[8,2,256,256]{3,2,1,0:T(8,128)}), f32[8,2,256,256]{3,2,1,0:T(8,128)}, u32[]{:S(2)}, u32[]{:S(2)}) %all-to-all-start.1) | async-done | bytes 4194336 | tf_op jit(solution)/shard_map/all_to_all | solution.py:316
  142.2 33.7 %shard_map.77 = (f32[2,32,64,256]{3,2,1,0:T(8,128)}, f32[8,128]{1,0:T(8,128)}) custom-call(f32[64,64]{1,0:T(8,128)} %get-tuple-element.21.cos_a_ref, f32[64,64]{1,0:T(8,128)} %get-tuple-element.20.sin_a_ref, f32[2048,1]{1,0:T(8,128)} %get-tuple-element.17.twist_cos_ref, f32[2048,1]{1,0:T(8,128)} %get-tuple-element.16.twist_sin_ref, ...), custom_call_target="tpu_custom_call" | custom-call | tf_op jit(solution)/shard_map/pallas_call | solution.py:202
  176.0 16.0 %shard_map.78 = f32[8,128]{1,0:T(8,128)} custom-call(f32[8,128]{1,0:T(8,128)} %get-tuple-element.5.value_ref), custom_call_target="tpu_custom_call" | custom-call | tf_op jit(solution)/shard_map/pallas_call | solution.py:290
  191.9 1.2 slice.3
  (12 shorter events, 0.4 us)
Async XLA Ops:
  0.6 68.7 %all-to-all-start = ((f32[256,8,256]{2,1,0:T(8,128)}), f32[256,8,256]{2,1,0:T(8,128)S(1)}, u32[]{:S(2)}, u32[]{:S(2)}) async-start(f32[256,8,256]{2,1,0:T(8,128)} %bitcast.42), calls=%async_computation | async-start | bytes 4194304 | tf_op jit(solution)/shard_map/all_to_all | solution.py:313
  87.5 6.3 %copy-start = (f32[2048]{0:T(1024)S(1)}, f32[2048]{0:T(1024)}, u32[]{:S(2)}) copy-start(f32[2048]{0:T(1024)} %param.7) | copy-start | bytes 24580
  87.5 54.7 %all-to-all-start.1 = ((f32[8,2,256,256]{3,2,1,0:T(8,128)}), f32[8,2,256,256]{3,2,1,0:T(8,128)}, u32[]{:S(2)}, u32[]{:S(2)}) async-start(f32[8,2,256,256]{3,2,1,0:T(8,128)} %copy.50), calls=%async_computation.1 | async-start | bytes 8388608 | tf_op jit(solution)/shard_map/all_to_all | solution.py:316
  93.3 2.8 %copy-start.1 = (f32[2048]{0:T(1024)S(1)}, f32[2048]{0:T(1024)}, u32[]{:S(2)}) copy-start(f32[2048]{0:T(1024)} %param.9) | copy-start | bytes 24580

commit v6 on v5

--- a/solution.py
+++ b/solution.py
@@ -45,16 +45,16 @@
     part_real = part_real.reshape(devices, blocks * rows, width)
     part_imag = part_imag.reshape(devices, blocks * rows, width)
     local_index = jnp.arange(width, dtype=jnp.int32)
-    twist_cos, twist_sin = root_table(residue, local_index, length)
-    twist_cos = twist_cos[:, None, :]
-    twist_sin = twist_sin[:, None, :]
-    turned_real = part_real * twist_cos - part_imag * twist_sin
-    turned_imag = part_real * twist_sin + part_imag * twist_cos
-    cos_w, sin_w = root_table(local_index, local_index, width)
-    spec_real, spec_imag = complex_einsum(
-        "dyn,nk->dyk", turned_real, turned_imag, cos_w, sin_w, precision_mid
-    )
-    return jnp.stack([spec_real, spec_imag], axis=1)
+    freqs = residue[:, None] + devices * local_index[None, :]
+    phase = local_index[None, :, None] * freqs[:, None, :] % length
+    angle = phase.astype(jnp.float32) * (-2.0 * math.pi / length)
+    cos_t = jnp.cos(angle)
+    sin_t = jnp.sin(angle)
+    from_real = jnp.concatenate([cos_t, sin_t], axis=2)
+    from_imag = jnp.concatenate([-sin_t, cos_t], axis=2)
+    spectrum = jnp.einsum("dyn,dnk->dyk", part_real, from_real, precision=precision_mid)
+    spectrum = spectrum + jnp.einsum("dyn,dnk->dyk", part_imag, from_imag, precision=precision_mid)
+    return spectrum
 
 
 def y_transform(real_part, imag_part):
@@ -85,7 +85,8 @@
              cos_b_ref, sin_b_ref, row_scale_ref, row_rate_ref, col_scale_ref, col_shift_ref,
              col_mix_ref, spectrum_hbm, out_hbm, sum_ref,
              held, step_real, step_imag, staged, in_sems, out_sems):
-    high, low, _, blocks, rows, width = spectrum_hbm.shape
+    high, low, blocks, rows, both_width = spectrum_hbm.shape
+    width = both_width // 2
     size_b = low * rows
     size_a = high * blocks
     half = width // 2
@@ -93,7 +94,7 @@
     for part in range(2):
         for index in range(size_b):
             copy = pltpu.make_async_copy(
-                spectrum_hbm.at[:, index // rows, part, :, index % rows, :],
+                spectrum_hbm.at[:, index // rows, :, index % rows, pl.ds(part * width, width)],
                 held.at[part, index],
                 in_sems.at[part, index],
             )
@@ -108,7 +109,7 @@
     def first(index, carry):
         for part in range(2):
             pltpu.make_async_copy(
-                spectrum_hbm.at[:, index // rows, part, :, index % rows, :],
+                spectrum_hbm.at[:, index // rows, :, index % rows, pl.ds(part * width, width)],
                 held.at[part, index],
                 in_sems.at[part, index],
             ).wait()
@@ -178,7 +179,8 @@
 
 
 def y_stage(spectrum, row_scale, col_scale, row_rate, col_shift, col_mix, norm_factor, devices, height):
-    _, _, count, width = spectrum.shape
+    _, count, both_width = spectrum.shape
+    width = both_width // 2
     length = devices * count
     size_b = 1 << (length.bit_length() - 1) // 2
     size_a = length // size_b
@@ -198,7 +200,7 @@
     row_rate_t = row_rate.reshape(size_b, size_a).T.reshape(length, 1)
     vmem = pl.BlockSpec(memory_space=pltpu.VMEM)
     anywhere = pl.BlockSpec(memory_space=pl.ANY)
-    shaped = spectrum.reshape(high, low, 2, blocks, rows, width)
+    shaped = spectrum.reshape(high, low, blocks, rows, both_width)
     latent, sums = pl.pallas_call(
         functools.partial(y_kernel, norm_factor),
         out_shape=(
@@ -314,8 +316,8 @@
     incoming = incoming.reshape(planes, devices, rows, width)
     both = x_stage(incoming)
     both = lax.all_to_all(both, "gx", split_axis=0, concat_axis=0, tiled=True)
-    length = both.shape[0] * both.shape[2]
-    total_cols = both.shape[3] * devices
+    length = both.shape[0] * both.shape[1]
+    total_cols = both.shape[2] // 2 * devices
     norm_factor = 1.0 / math.sqrt(length * total_cols)
     latent, part_sum = y_stage(
         both, row_scale, col_scale, row_rate, col_shift, col_mix, norm_factor, devices, height

time: 195 us -> 192 us (0.985)
  waiting for transfers between devices: 90.9 us -> 80.8 us
  other arithmetic: 6.52 us -> 15.3 us
  matrix products: 14.4 us -> 11.9 us
    all_to_all x1, waiting for transfers between devices: 52.9 us -> 42.8 us  [per_device(): lax.all_to_all(outgoing, ('gy', 'gx'), split_axis=0, concat_axis=0, tiled...]
    neg x0 -> x1, other arithmetic: none -> 9.22 us  [x_stage(): from_imag = jnp.concatenate([-sin_t, cos_t], axis=2)]
    another operation x1 -> x0, local copies, waits for them, and re-layouts: 2.44 us -> none  [x_stage(): return jnp.stack([spec_real, spec_imag], axis=1)]
    dot_general x4 -> x2, matrix products: 9.98 us -> 7.91 us  [the longest x1 4.84 us: x_stage(): jnp.einsum('dyn,dnk->dyk', part_imag, from_imag, precision=precision_mid)]
  transfers between devices with their start and end apart: 2 -> 2, of which waited for: 2 -> 2; matrix products, arithmetic and copies ran while one was open for 6% -> 11% of each run, Pallas kernels for 0% -> 0%
where the time goes in v6:
time: 192 us; the launch traced here: 191 us
  waiting for transfers between devices  80.8 us (42%)
  Pallas kernels  49.7 us (26%)
  starting transfers between devices  22.5 us (12%)
  other arithmetic  15.3 us (8%)
  matrix products  11.9 us (6%)
  local copies, waits for them, and re-layouts  8.59 us (4%)
  between operations  2.53 us (1%)
    all_to_all x1, waiting for transfers between devices, per_device(): lax.all_to_all(outgoing, ('gy', 'gx'), split_axis=0, concat_axis=0, tiled...  42.8 us
    all_to_all x1, waiting for transfers between devices, per_device(): both = lax.all_to_all(both, 'gx', split_axis=0, concat_axis=0, tiled=True)  37.9 us
    pallas_call x1, Pallas kernels, y_stage(): pl.pallas_call(functools.partial(y_kernel, norm_factor), out_shape=(jax.S...  33.7 us
    all_to_all x1, starting transfers between devices, per_device(): lax.all_to_all(outgoing, ('gy', 'gx'), split_axis=0, concat_axis=0, tiled...  16.7 us
    pallas_call x1, Pallas kernels, total_everywhere(): pl.pallas_call(total_kernel, out_shape=jax.ShapeDtypeStruct((8, 128), jnp...  16 us
    neg x1, other arithmetic, x_stage(): from_imag = jnp.concatenate([-sin_t, cos_t], axis=2)  9.22 us
    sin x3, other arithmetic, root_table(): return (jnp.cos(angle), jnp.sin(angle))  5.99 us
    all_to_all x1, starting transfers between devices, per_device(): both = lax.all_to_all(both, 'gx', split_axis=0, concat_axis=0, tiled=True)  5.83 us
  transfers between devices with their start and end apart: 2, of which 2 were waited for; matrix products, arithmetic and copies ran while one was open for 11% of the time, Pallas kernels for 0%

profile of v6, /device:TPU:1, one launch (start us, length us, event | category | flops | bytes accessed | tf_op | source)
XLA Modules:
  0.0 191.4 jit_solution(10599565240961020808)
XLA Ops:
  0.6 16.7 %all-to-all-start = ((f32[256,8,256]{2,1,0:T(8,128)}), f32[256,8,256]{2,1,0:T(8,128)}, u32[]{:S(2)}, u32[]{:S(2)}) async-start(f32[256,8,256]{2,1,0:T(8,128)} %bitcast.25), calls=%async_computation | async-start | bytes 4194304 | tf_op jit(solution)/shard_map/all_to_all | solution.py:315
  17.3 0.1 broadcast_add_fusion
  17.4 9.2 %fusion.21 = (f32[8,256,256]{2,1,0:T(8,128)}, f32[8,256,256]{2,1,0:T(8,128)}, f32[8,256,256]{2,1,0:T(8,128)S(1)}) fusion(s32[8,256]{1,0:T(8,128)S(1)} %broadcast_add_fusion), kind=kLoop, calls=%fused_computation.24 | loop fusion | flops 7864320 | bytes 6299648 | tf_op jit(solution)/shard_map/neg | solution.py:54
  26.6 42.8 %all-to-all-done = f32[256,8,256]{2,1,0:T(8,128)} async-done(((f32[256,8,256]{2,1,0:T(8,128)}), f32[256,8,256]{2,1,0:T(8,128)}, u32[]{:S(2)}, u32[]{:S(2)}) %all-to-all-start) | async-done | bytes 2097184 | tf_op jit(solution)/shard_map/all_to_all | solution.py:315
  69.4 2.5 %copy.31 = f32[32,8,256,8]{2,3,1,0:T(8,128)S(1)} copy(f32[32,8,256,8]{2,1,3,0:T(8,128)} %bitcast.8) | data formatting | bytes 4194304 | tf_op jit(solution)/shard_map/bgtn,gd->dbtn/dot_general | solution.py:43
  71.9 2.0 %fusion.45 = f32[8,256,256]{2,0,1:T(8,128)S(1)} fusion(f32[256,256,8]{1,2,0:T(8,128)S(1)} %bitcast.23, s32[8]{0:T(128)S(1)} %fusion.59), kind=kOutput, calls=%fused_computation.61 | convolution fusion | flops 50332544 | bytes 4194336 | tf_op jit(solution)/shard_map/bgtn,gd->dbtn/dot_general | solution.py:43
  73.9 2.0 %fusion.43 = f32[8,256,256]{2,0,1:T(8,128)S(1)} fusion(f32[256,256,8]{1,2,0:T(8,128)S(1)} %bitcast.24, s32[8]{0:T(128)S(1)} %fusion.59), kind=kOutput, calls=%fused_computation.59 | convolution fusion | flops 50332544 | bytes 4194336 | tf_op jit(solution)/shard_map/bgtn,gd->dbtn/dot_general | solution.py:44
  76.0 3.1 %fusion = f32[8,256,512]{2,1,0:T(8,128)S(1)} fusion(f32[8,256,256]{2,1,0:T(8,128)S(1)} %copy-done.1, f32[8,256,256]{2,1,0:T(8,128)S(1)} %get-tuple-element.18, f32[8,256,256]{2,0,1:T(8,128)S(1)} %fusion.45), kind=kOutput, calls=%fused_computation | convolution fusion | flops 1611661312 | bytes 10485760 | tf_op jit(solution)/shard_map/dyn,dnk->dyk/dot_general | solution.py:55
  79.1 4.8 %fusion.8 = f32[8,256,512]{2,1,0:T(8,128)} fusion(f32[8,256,512]{2,1,0:T(8,128)S(1)} %fusion, f32[8,256,256]{2,1,0:T(8,128)S(1)} %get-tuple-element.18, f32[8,256,256]{2,1,0:T(8,128)S(1)} %copy-done, f32[8,256,256]{2,0,1:T(8,128)S(1)} %fusion.43), kind=kOutput, calls=%fused_computation.11 | convolution fusion | flops 1612709888 | bytes 14680064 | tf_op jit(solution)/shard_map/dyn,dnk->dyk/dot_general | solution.py:56
  83.9 5.8 %all-to-all-start.1 = ((f32[8,256,512]{2,1,0:T(8,128)}), f32[8,256,512]{2,1,0:T(8,128)}, u32[]{:S(2)}, u32[]{:S(2)}) async-start(f32[8,256,512]{2,1,0:T(8,128)} %fusion.8), calls=%async_computation.1 | async-start | bytes 8388608 | tf_op jit(solution)/shard_map/all_to_all | solution.py:318
  89.7 0.1 mul.259
  89.9 0.4 copy.28
  90.2 0.1 reshape.201
  90.3 0.1 copy.29
  90.4 2.1 %reshape.213.row_scale_ref = f32[2048,1]{1,0:T(8,128)} reshape(f32[64,32]{1,0:T(8,128)S(1)} %copy.29) | data formatting | bytes 16384 | tf_op jit(solution)/shard_map/reshape | solution.py:199
  92.5 0.1 copy.30
  92.6 2.1 %reshape.214.row_rate_ref = f32[2048,1]{1,0:T(8,128)} reshape(f32[64,32]{1,0:T(8,128)S(1)} %copy.30) | data formatting | bytes 16384 | tf_op jit(solution)/shard_map/reshape | solution.py:200
  94.7 0.7 fusion.38
  95.4 0.8 fusion.33
  96.2 4.5 %multiply_sine_fusion = (f32[2048,1]{1,0:T(8,128)}, f32[2048,1]{1,0:T(8,128)}) fusion(f32[2048,1]{1,0:T(8,128)S(1)} %copy.28), kind=kLoop, calls=%fused_computation.22 | loop fusion | flops 2048 | bytes 24576 | tf_op jit(solution)/shard_map/sin | solution.py:25
  100.7 37.9 %all-to-all-done.1 = f32[8,256,512]{2,1,0:T(8,128)} async-done(((f32[8,256,512]{2,1,0:T(8,128)}), f32[8,256,512]{2,1,0:T(8,128)}, u32[]{:S(2)}, u32[]{:S(2)}) %all-to-all-start.1) | async-done | bytes 4194336 | tf_op jit(solution)/shard_map/all_to_all | solution.py:318
  138.7 33.7 %shard_map.77 = (f32[2,32,64,256]{3,2,1,0:T(8,128)}, f32[8,128]{1,0:T(8,128)}) custom-call(f32[64,64]{1,0:T(8,128)} %get-tuple-element.20.cos_a_ref, f32[64,64]{1,0:T(8,128)} %get-tuple-element.19.sin_a_ref, f32[2048,1]{1,0:T(8,128)} %get-tuple-element.15.twist_cos_ref, f32[2048,1]{1,0:T(8,128)} %get-tuple-element.14.twist_sin_ref, ...), custom_call_target="tpu_custom_call" | custom-call | tf_op jit(solution)/shard_map/pallas_call | solution.py:204
  172.4 16.0 %shard_map.78 = f32[8,128]{1,0:T(8,128)} custom-call(f32[8,128]{1,0:T(8,128)} %get-tuple-element.5.value_ref), custom_call_target="tpu_custom_call" | custom-call | tf_op jit(solution)/shard_map/pallas_call | solution.py:292
  188.4 1.2 slice.3
  (14 shorter events, 0.1 us)
Async XLA Ops:
  0.6 68.8 %all-to-all-start = ((f32[256,8,256]{2,1,0:T(8,128)}), f32[256,8,256]{2,1,0:T(8,128)}, u32[]{:S(2)}, u32[]{:S(2)}) async-start(f32[256,8,256]{2,1,0:T(8,128)} %bitcast.25), calls=%async_computation | async-start | bytes 4194304 | tf_op jit(solution)/shard_map/all_to_all | solution.py:315
  73.9 2.0 %copy-start.1 = (f32[8,256,256]{2,1,0:T(8,128)S(1)}, f32[8,256,256]{2,1,0:T(8,128)}, u32[]{:S(2)}) copy-start(f32[8,256,256]{2,1,0:T(8,128)} %get-tuple-element.17) | copy-start | bytes 6291460
  76.0 3.1 %copy-start = (f32[8,256,256]{2,1,0:T(8,128)S(1)}, f32[8,256,256]{2,1,0:T(8,128)}, u32[]{:S(2)}) copy-start(f32[8,256,256]{2,1,0:T(8,128)} %get-tuple-element.16) | copy-start | bytes 6291460
  83.9 6.3 %copy-start.2 = (f32[2048]{0:T(1024)S(1)}, f32[2048]{0:T(1024)}, u32[]{:S(2)}) copy-start(f32[2048]{0:T(1024)} %param.7) | copy-start | bytes 24580
  83.9 54.8 %all-to-all-start.1 = ((f32[8,256,512]{2,1,0:T(8,128)}), f32[8,256,512]{2,1,0:T(8,128)}, u32[]{:S(2)}, u32[]{:S(2)}) async-start(f32[8,256,512]{2,1,0:T(8,128)} %fusion.8), calls=%async_computation.1 | async-start | bytes 8388608 | tf_op jit(solution)/shard_map/all_to_all | solution.py:318
  89.7 2.7 %copy-start.3 = (f32[2048]{0:T(1024)S(1)}, f32[2048]{0:T(1024)}, u32[]{:S(2)}) copy-start(f32[2048]{0:T(1024)} %param.9) | copy-start | bytes 24580

commit v7 on v6

--- a/solution.py
+++ b/solution.py
@@ -39,11 +39,28 @@
     levels = devices.bit_length() - 1
     group = jnp.arange(devices, dtype=jnp.int32)
     residue = reverse_bits(group, levels)
-    cos_8, sin_8 = root_table(group, residue, devices)
-    part_real = jnp.einsum("bgtn,gd->dbtn", pieces, cos_8, precision=precision_top)
-    part_imag = jnp.einsum("bgtn,gd->dbtn", pieces, sin_8, precision=precision_top)
-    part_real = part_real.reshape(devices, blocks * rows, width)
-    part_imag = part_imag.reshape(devices, blocks * rows, width)
+    slices = [pieces[:, g].reshape(blocks * rows, width) for g in range(devices)]
+    real_slots = []
+    imag_slots = []
+    for slot in range(devices):
+        turn = sum(((slot >> place) & 1) << (levels - 1 - place) for place in range(levels))
+        real_terms = []
+        imag_terms = []
+        for g in range(devices):
+            phase = g * turn % devices
+            angle = -2.0 * math.pi * phase / devices
+            cos_value = 0.0 if phase * 4 % devices == 0 and phase * 4 // devices % 2 == 1 else math.cos(angle)
+            sin_value = 0.0 if phase * 2 % devices == 0 else math.sin(angle)
+            if cos_value != 0.0:
+                real_terms.append(slices[g] * cos_value)
+            if sin_value != 0.0:
+                imag_terms.append(slices[g] * sin_value)
+        real_slots.append(sum(real_terms[1:], real_terms[0]))
+        imag_slots.append(
+            sum(imag_terms[1:], imag_terms[0]) if imag_terms else jnp.zeros_like(slices[0])
+        )
+    part_real = jnp.stack(real_slots)
+    part_imag = jnp.stack(imag_slots)
     local_index = jnp.arange(width, dtype=jnp.int32)
     freqs = residue[:, None] + devices * local_index[None, :]
     phase = local_index[None, :, None] * freqs[:, None, :] % length

time: 192 us -> 192 us (level)
  other arithmetic: 15.3 us -> 21.2 us
  matrix products: 11.9 us -> 7.12 us
    unnamed x0 -> x8, other arithmetic: none -> 5.33 us
    dot_general x2 -> x0, matrix products: 4.01 us -> none  [the longest x1 2.01 us: x_stage(): jnp.einsum('bgtn,gd->dbtn', pieces, sin_8, precision=precision_top)]
    unnamed x8 -> x15, local copies, waits for them, and re-layouts: 0.02 us -> 2.79 us
    dot_general x1 -> x0, local copies, waits for them, and re-layouts: 2.47 us -> none  [x_stage(): jnp.einsum('bgtn,gd->dbtn', pieces, cos_8, precision=precision_top)]
where the time goes in v7:
time: 192 us; the launch traced here: 191 us
  waiting for transfers between devices  80.3 us (42%)
  Pallas kernels  49.7 us (26%)
  starting transfers between devices  21.5 us (11%)
  other arithmetic  21.2 us (11%)
  local copies, waits for them, and re-layouts  8.95 us (5%)
  matrix products  7.12 us (4%)
  between operations  2.55 us (1%)
    all_to_all x1, waiting for transfers between devices, per_device(): lax.all_to_all(outgoing, ('gy', 'gx'), split_axis=0, concat_axis=0, tiled...  42.3 us
    all_to_all x1, waiting for transfers between devices, per_device(): both = lax.all_to_all(both, 'gx', split_axis=0, concat_axis=0, tiled=True)  37.9 us
    pallas_call x1, Pallas kernels, y_stage(): pl.pallas_call(functools.partial(y_kernel, norm_factor), out_shape=(jax.S...  33.7 us
    pallas_call x1, Pallas kernels, total_everywhere(): pl.pallas_call(total_kernel, out_shape=jax.ShapeDtypeStruct((8, 128), jnp...  16 us
    all_to_all x1, starting transfers between devices, per_device(): lax.all_to_all(outgoing, ('gy', 'gx'), split_axis=0, concat_axis=0, tiled...  15.7 us
    neg x1, other arithmetic, x_stage(): from_imag = jnp.concatenate([-sin_t, cos_t], axis=2)  9.8 us
    sin x3, other arithmetic, root_table(): return (jnp.cos(angle), jnp.sin(angle))  5.97 us
    all_to_all x1, starting transfers between devices, per_device(): both = lax.all_to_all(both, 'gx', split_axis=0, concat_axis=0, tiled=True)  5.82 us
  transfers between devices with their start and end apart: 2, of which 2 were waited for; matrix products, arithmetic and copies ran while one was open for 11% of the time, Pallas kernels for 0%

profile of v7, /device:TPU:1, one launch (start us, length us, event | category | flops | bytes accessed | tf_op | source)
XLA Modules:
  0.0 191.3 jit_solution(7246897810735533126)
XLA Ops:
  0.6 15.7 %all-to-all-start = ((f32[256,8,256]{2,1,0:T(8,128)}), f32[256,8,256]{2,1,0:T(8,128)S(1)}, u32[]{:S(2)}, u32[]{:S(2)}) async-start(f32[256,8,256]{2,1,0:T(8,128)} %bitcast.182), calls=%async_computation | async-start | bytes 4194304 | tf_op jit(solution)/shard_map/all_to_all | solution.py:332
  16.3 0.8 broadcast_dynamic-update-slice_fusion
  17.2 9.8 %fusion.19 = (f32[8,256,256]{2,1,0:T(8,128)}, f32[8,256,256]{2,1,0:T(8,128)}, f32[8,256,256]{2,1,0:T(8,128)}) fusion(s32[8,256]{1,0:T(8,128)S(1)} %broadcast_add_fusion), kind=kLoop, calls=%fused_computation.22 | loop fusion | flops 7864320 | bytes 6299648 | tf_op jit(solution)/shard_map/neg | solution.py:71
  27.0 42.3 %all-to-all-done = f32[256,8,256]{2,1,0:T(8,128)S(1)} async-done(((f32[256,8,256]{2,1,0:T(8,128)}), f32[256,8,256]{2,1,0:T(8,128)S(1)}, u32[]{:S(2)}, u32[]{:S(2)}) %all-to-all-start) | async-done | bytes 2097184 | tf_op jit(solution)/shard_map/all_to_all | solution.py:332
  69.3 0.8 add_dynamic-update-slice_fusion.5
  70.2 0.8 add_dynamic-update-slice_fusion.4
  71.0 0.8 add_dynamic-update-slice_fusion.3
  71.8 0.8 add_dynamic-update-slice_fusion.2
  72.7 0.9 add_dynamic-update-slice_fusion.1
  73.6 0.8 constant_dynamic-update-slice_fusion.5
  74.8 1.2 copy-done.2
  76.0 0.7 copy-done
  76.7 2.5 %fusion = f32[8,256,512]{2,1,0:T(8,128)S(1)} fusion(f32[8,256,256]{2,1,0:T(8,128)S(1)} %constant_dynamic-update-slice_fusion, f32[8,256,256]{2,1,0:T(8,128)S(1)} %copy-done.2, f32[8,256,256]{2,1,0:T(8,128)S(1)} %copy-done), kind=kOutput, calls=%fused_computation | convolution fusion | flops 1611661312 | bytes 10485760 | tf_op jit(solution)/shard_map/dyn,dnk->dyk/dot_general | solution.py:72
  79.2 4.6 %fusion.8 = f32[8,256,512]{2,1,0:T(8,128)} fusion(f32[8,256,512]{2,1,0:T(8,128)S(1)} %fusion, f32[8,256,256]{2,1,0:T(8,128)S(1)} %copy-done.3, f32[8,256,256]{2,1,0:T(8,128)S(1)} %copy-done, f32[8,256,256]{2,1,0:T(8,128)S(1)} %copy-done.1), kind=kOutput, calls=%fused_computation.11 | convolution fusion | flops 1612709888 | bytes 14680064 | tf_op jit(solution)/shard_map/dyn,dnk->dyk/dot_general | solution.py:73
  83.8 5.8 %all-to-all-start.1 = ((f32[8,256,512]{2,1,0:T(8,128)}), f32[8,256,512]{2,1,0:T(8,128)}, u32[]{:S(2)}, u32[]{:S(2)}) async-start(f32[8,256,512]{2,1,0:T(8,128)} %fusion.8), calls=%async_computation.1 | async-start | bytes 8388608 | tf_op jit(solution)/shard_map/all_to_all | solution.py:335
  90.3 2.1 %reshape.769.row_scale_ref = f32[2048,1]{1,0:T(8,128)} reshape(f32[64,32]{1,0:T(8,128)S(1)} %copy.18) | data formatting | bytes 16384 | tf_op jit(solution)/shard_map/reshape | solution.py:216
  92.5 2.1 %reshape.770.row_rate_ref = f32[2048,1]{1,0:T(8,128)} reshape(f32[64,32]{1,0:T(8,128)S(1)} %copy.19) | data formatting | bytes 16384 | tf_op jit(solution)/shard_map/reshape | solution.py:217
  94.7 0.7 fusion.36
  95.4 0.8 fusion.31
  96.1 4.5 %multiply_sine_fusion = (f32[2048,1]{1,0:T(8,128)}, f32[2048,1]{1,0:T(8,128)}) fusion(f32[2048,1]{1,0:T(8,128)S(1)} %copy.17), kind=kLoop, calls=%fused_computation.20 | loop fusion | flops 2048 | bytes 24576 | tf_op jit(solution)/shard_map/sin | solution.py:25
  100.6 37.9 %all-to-all-done.1 = f32[8,256,512]{2,1,0:T(8,128)} async-done(((f32[8,256,512]{2,1,0:T(8,128)}), f32[8,256,512]{2,1,0:T(8,128)}, u32[]{:S(2)}, u32[]{:S(2)}) %all-to-all-start.1) | async-done | bytes 4194336 | tf_op jit(solution)/shard_map/all_to_all | solution.py:335
  138.6 33.7 %shard_map.77 = (f32[2,32,64,256]{3,2,1,0:T(8,128)}, f32[8,128]{1,0:T(8,128)}) custom-call(f32[64,64]{1,0:T(8,128)} %get-tuple-element.29.cos_a_ref, f32[64,64]{1,0:T(8,128)} %get-tuple-element.28.sin_a_ref, f32[2048,1]{1,0:T(8,128)} %get-tuple-element.24.twist_cos_ref, f32[2048,1]{1,0:T(8,128)} %get-tuple-element.23.twist_sin_ref, ...), custom_call_target="tpu_custom_call" | custom-call | tf_op jit(solution)/shard_map/pallas_call | solution.py:221
  172.3 16.0 %shard_map.78 = f32[8,128]{1,0:T(8,128)} custom-call(f32[8,128]{1,0:T(8,128)} %get-tuple-element.5.value_ref), custom_call_target="tpu_custom_call" | custom-call | tf_op jit(solution)/shard_map/pallas_call | solution.py:309
  188.3 1.2 slice.35
  (27 shorter events, 1.2 us)
Async XLA Ops:
  0.6 68.7 %all-to-all-start = ((f32[256,8,256]{2,1,0:T(8,128)}), f32[256,8,256]{2,1,0:T(8,128)S(1)}, u32[]{:S(2)}, u32[]{:S(2)}) async-start(f32[256,8,256]{2,1,0:T(8,128)} %bitcast.182), calls=%async_computation | async-start | bytes 4194304 | tf_op jit(solution)/shard_map/all_to_all | solution.py:332
  74.4 1.6 copy-start.2
  74.6 2.1 %copy-start = (f32[8,256,256]{2,1,0:T(8,128)S(1)}, f32[8,256,256]{2,1,0:T(8,128)}, u32[]{:S(2)}) copy-start(f32[8,256,256]{2,1,0:T(8,128)} %get-tuple-element.27) | copy-start | bytes 6291460
  76.7 2.5 %copy-start.1 = (f32[8,256,256]{2,1,0:T(8,128)S(1)}, f32[8,256,256]{2,1,0:T(8,128)}, u32[]{:S(2)}) copy-start(f32[8,256,256]{2,1,0:T(8,128)} %get-tuple-element.25) | copy-start | bytes 6291460
  76.7 2.6 %copy-start.3 = (f32[8,256,256]{2,1,0:T(8,128)S(1)}, f32[8,256,256]{2,1,0:T(8,128)}, u32[]{:S(2)}) copy-start(f32[8,256,256]{2,1,0:T(8,128)} %get-tuple-element.18) | copy-start | bytes 6291460
  83.8 6.3 %copy-start.4 = (f32[2048]{0:T(1024)S(1)}, f32[2048]{0:T(1024)}, u32[]{:S(2)}) copy-start(f32[2048]{0:T(1024)} %param.7) | copy-start | bytes 24580
  83.8 54.8 %all-to-all-start.1 = ((f32[8,256,512]{2,1,0:T(8,128)}), f32[8,256,512]{2,1,0:T(8,128)}, u32[]{:S(2)}, u32[]{:S(2)}) async-start(f32[8,256,512]{2,1,0:T(8,128)} %fusion.8), calls=%async_computation.1 | async-start | bytes 8388608 | tf_op jit(solution)/shard_map/all_to_all | solution.py:335
  89.7 2.7 %copy-start.5 = (f32[2048]{0:T(1024)S(1)}, f32[2048]{0:T(1024)}, u32[]{:S(2)}) copy-start(f32[2048]{0:T(1024)} %param.9) | copy-start | bytes 24580

commit v8 on v7

--- a/solution.py
+++ b/solution.py
@@ -156,33 +156,38 @@
 
     def second(index, total):
         picked = pl.ds(index, size_b, stride=size_a)
-        part_real = jnp.concatenate([step_real[0, picked, :], step_real[1, picked, :]], axis=1)
-        part_imag = jnp.concatenate([step_imag[0, picked, :], step_imag[1, picked, :]], axis=1)
-        from_real = dot(both_b, part_real)
-        from_imag = dot(both_b, part_imag)
-        spec_real = from_real[:size_b] - from_imag[size_b:]
-        spec_imag = from_imag[:size_b] + from_real[size_b:]
         rows = pl.ds(pl.multiple_of(index * size_b, size_b), size_b)
-        scale = row_scale_ref[rows, :] * col_scale
-        latent_u = spec_real * norm_factor * scale
-        latent_v = spec_imag * norm_factor * scale
-        log_scale = row_rate_ref[rows, :] * jnp.tanh(latent_u + col_shift)
-        latent_w = latent_v * jnp.exp(log_scale) + col_mix * latent_u
-        terms = (
-            -0.5 * (latent_u * latent_u + latent_w * latent_w)
-            - math.log(2.0 * math.pi)
-            + log_scale
-            + 2.0 * jnp.log(scale)
-        )
-        staged[0, index] = latent_u
-        staged[1, index] = latent_w
+        row_scale = row_scale_ref[rows, :]
+        row_rate = row_rate_ref[rows, :]
+        for side in range(2):
+            lanes = slice(side * half, (side + 1) * half)
+            part_real = step_real[side, picked, :]
+            part_imag = step_imag[side, picked, :]
+            from_real = dot(both_b, part_real)
+            from_imag = dot(both_b, part_imag)
+            spec_real = from_real[:size_b] - from_imag[size_b:]
+            spec_imag = from_imag[:size_b] + from_real[size_b:]
+            scale = row_scale * col_scale[:, lanes]
+            latent_u = spec_real * norm_factor * scale
+            latent_v = spec_imag * norm_factor * scale
+            log_scale = row_rate * jnp.tanh(latent_u + col_shift[:, lanes])
+            latent_w = latent_v * jnp.exp(log_scale) + col_mix[:, lanes] * latent_u
+            terms = (
+                -0.5 * (latent_u * latent_u + latent_w * latent_w)
+                - math.log(2.0 * math.pi)
+                + log_scale
+                + 2.0 * jnp.log(scale)
+            )
+            staged[0, index, :, lanes] = latent_u
+            staged[1, index, :, lanes] = latent_w
+            total = total + terms
         for part in range(2):
             pltpu.make_async_copy(
                 staged.at[part, index], out_hbm.at[part, :, index, :], out_sems.at[part, index]
             ).start()
-        return total + terms
-
-    total = lax.fori_loop(0, size_a, second, jnp.zeros((size_b, width), jnp.float32))
+        return total
+
+    total = lax.fori_loop(0, size_a, second, jnp.zeros((size_b, half), jnp.float32))
     sum_ref[...] = jnp.broadcast_to(jnp.sum(total), sum_ref.shape)
 
     def finish(index, carry):

time: 192 us -> 190 us (0.990)
  no operation moved by 1% of the time
where the time goes in v8:
time: 190 us
  waiting for transfers between devices  80.3 us (42%)
  Pallas kernels  47.9 us (25%)
  starting transfers between devices  21.5 us (11%)
  other arithmetic  21.2 us (11%)
  local copies, waits for them, and re-layouts  8.95 us (5%)
  matrix products  7.12 us (4%)
  between operations  2.55 us (1%)
    all_to_all x1, waiting for transfers between devices, per_device(): lax.all_to_all(outgoing, ('gy', 'gx'), split_axis=0, concat_axis=0, tiled...  42.3 us
    all_to_all x1, waiting for transfers between devices, per_device(): both = lax.all_to_all(both, 'gx', split_axis=0, concat_axis=0, tiled=True)  37.9 us
    pallas_call x1, Pallas kernels, y_stage(): pl.pallas_call(functools.partial(y_kernel, norm_factor), out_shape=(jax.S...  32 us
    pallas_call x1, Pallas kernels, total_everywhere(): pl.pallas_call(total_kernel, out_shape=jax.ShapeDtypeStruct((8, 128), jnp...  16 us
    all_to_all x1, starting transfers between devices, per_device(): lax.all_to_all(outgoing, ('gy', 'gx'), split_axis=0, concat_axis=0, tiled...  15.7 us
    neg x1, other arithmetic, x_stage(): from_imag = jnp.concatenate([-sin_t, cos_t], axis=2)  9.8 us
    sin x3, other arithmetic, root_table(): return (jnp.cos(angle), jnp.sin(angle))  5.97 us
    all_to_all x1, starting transfers between devices, per_device(): both = lax.all_to_all(both, 'gx', split_axis=0, concat_axis=0, tiled=True)  5.82 us
  transfers between devices with their start and end apart: 2, of which 2 were waited for; matrix products, arithmetic and copies ran while one was open for 11% of the time, Pallas kernels for 0%

profile of v8, /device:TPU:1, one launch (start us, length us, event | category | flops | bytes accessed | tf_op | source)
XLA Modules:
  0.0 189.5 jit_solution(491161290781143134)
XLA Ops:
  0.6 15.7 %all-to-all-start = ((f32[256,8,256]{2,1,0:T(8,128)}), f32[256,8,256]{2,1,0:T(8,128)S(1)}, u32[]{:S(2)}, u32[]{:S(2)}) async-start(f32[256,8,256]{2,1,0:T(8,128)} %bitcast.182), calls=%async_computation | async-start | bytes 4194304 | tf_op jit(solution)/shard_map/all_to_all | solution.py:337
  16.3 0.8 broadcast_dynamic-update-slice_fusion
  17.2 9.8 %fusion.19 = (f32[8,256,256]{2,1,0:T(8,128)}, f32[8,256,256]{2,1,0:T(8,128)}, f32[8,256,256]{2,1,0:T(8,128)}) fusion(s32[8,256]{1,0:T(8,128)S(1)} %broadcast_add_fusion), kind=kLoop, calls=%fused_computation.22 | loop fusion | flops 7864320 | bytes 6299648 | tf_op jit(solution)/shard_map/neg | solution.py:71
  27.0 42.3 %all-to-all-done = f32[256,8,256]{2,1,0:T(8,128)S(1)} async-done(((f32[256,8,256]{2,1,0:T(8,128)}), f32[256,8,256]{2,1,0:T(8,128)S(1)}, u32[]{:S(2)}, u32[]{:S(2)}) %all-to-all-start) | async-done | bytes 2097184 | tf_op jit(solution)/shard_map/all_to_all | solution.py:337
  69.3 0.8 add_dynamic-update-slice_fusion.5
  70.2 0.8 add_dynamic-update-slice_fusion.4
  71.0 0.8 add_dynamic-update-slice_fusion.3
  71.8 0.8 add_dynamic-update-slice_fusion.2
  72.7 0.9 add_dynamic-update-slice_fusion.1
  73.6 0.8 constant_dynamic-update-slice_fusion.5
  74.8 1.2 copy-done.2
  76.0 0.7 copy-done
  76.7 2.5 %fusion = f32[8,256,512]{2,1,0:T(8,128)S(1)} fusion(f32[8,256,256]{2,1,0:T(8,128)S(1)} %constant_dynamic-update-slice_fusion, f32[8,256,256]{2,1,0:T(8,128)S(1)} %copy-done.2, f32[8,256,256]{2,1,0:T(8,128)S(1)} %copy-done), kind=kOutput, calls=%fused_computation | convolution fusion | flops 1611661312 | bytes 10485760 | tf_op jit(solution)/shard_map/dyn,dnk->dyk/dot_general | solution.py:72
  79.2 4.6 %fusion.8 = f32[8,256,512]{2,1,0:T(8,128)} fusion(f32[8,256,512]{2,1,0:T(8,128)S(1)} %fusion, f32[8,256,256]{2,1,0:T(8,128)S(1)} %copy-done.3, f32[8,256,256]{2,1,0:T(8,128)S(1)} %copy-done, f32[8,256,256]{2,1,0:T(8,128)S(1)} %copy-done.1), kind=kOutput, calls=%fused_computation.11 | convolution fusion | flops 1612709888 | bytes 14680064 | tf_op jit(solution)/shard_map/dyn,dnk->dyk/dot_general | solution.py:73
  83.8 5.8 %all-to-all-start.1 = ((f32[8,256,512]{2,1,0:T(8,128)}), f32[8,256,512]{2,1,0:T(8,128)}, u32[]{:S(2)}, u32[]{:S(2)}) async-start(f32[8,256,512]{2,1,0:T(8,128)} %fusion.8), calls=%async_computation.1 | async-start | bytes 8388608 | tf_op jit(solution)/shard_map/all_to_all | solution.py:340
  90.3 2.1 %reshape.769.row_scale_ref = f32[2048,1]{1,0:T(8,128)} reshape(f32[64,32]{1,0:T(8,128)S(1)} %copy.18) | data formatting | bytes 16384 | tf_op jit(solution)/shard_map/reshape | solution.py:221
  92.5 2.1 %reshape.770.row_rate_ref = f32[2048,1]{1,0:T(8,128)} reshape(f32[64,32]{1,0:T(8,128)S(1)} %copy.19) | data formatting | bytes 16384 | tf_op jit(solution)/shard_map/reshape | solution.py:222
  94.7 0.7 fusion.36
  95.4 0.8 fusion.31
  96.1 4.5 %multiply_sine_fusion = (f32[2048,1]{1,0:T(8,128)}, f32[2048,1]{1,0:T(8,128)}) fusion(f32[2048,1]{1,0:T(8,128)S(1)} %copy.17), kind=kLoop, calls=%fused_computation.20 | loop fusion | flops 2048 | bytes 24576 | tf_op jit(solution)/shard_map/sin | solution.py:25
  100.6 37.9 %all-to-all-done.1 = f32[8,256,512]{2,1,0:T(8,128)} async-done(((f32[8,256,512]{2,1,0:T(8,128)}), f32[8,256,512]{2,1,0:T(8,128)}, u32[]{:S(2)}, u32[]{:S(2)}) %all-to-all-start.1) | async-done | bytes 4194336 | tf_op jit(solution)/shard_map/all_to_all | solution.py:340
  138.6 32.0 %shard_map.77 = (f32[2,32,64,256]{3,2,1,0:T(8,128)}, f32[8,128]{1,0:T(8,128)}) custom-call(f32[64,64]{1,0:T(8,128)} %get-tuple-element.29.cos_a_ref, f32[64,64]{1,0:T(8,128)} %get-tuple-element.28.sin_a_ref, f32[2048,1]{1,0:T(8,128)} %get-tuple-element.24.twist_cos_ref, f32[2048,1]{1,0:T(8,128)} %get-tuple-element.23.twist_sin_ref, ...), custom_call_target="tpu_custom_call" | custom-call | tf_op jit(solution)/shard_map/pallas_call | solution.py:226
  170.5 16.0 %shard_map.78 = f32[8,128]{1,0:T(8,128)} custom-call(f32[8,128]{1,0:T(8,128)} %get-tuple-element.5.value_ref), custom_call_target="tpu_custom_call" | custom-call | tf_op jit(solution)/shard_map/pallas_call | solution.py:314
  186.5 1.2 slice.35
  (27 shorter events, 1.2 us)
Async XLA Ops:
  0.6 68.7 %all-to-all-start = ((f32[256,8,256]{2,1,0:T(8,128)}), f32[256,8,256]{2,1,0:T(8,128)S(1)}, u32[]{:S(2)}, u32[]{:S(2)}) async-start(f32[256,8,256]{2,1,0:T(8,128)} %bitcast.182), calls=%async_computation | async-start | bytes 4194304 | tf_op jit(solution)/shard_map/all_to_all | solution.py:337
  74.4 1.6 copy-start.2
  74.6 2.1 %copy-start = (f32[8,256,256]{2,1,0:T(8,128)S(1)}, f32[8,256,256]{2,1,0:T(8,128)}, u32[]{:S(2)}) copy-start(f32[8,256,256]{2,1,0:T(8,128)} %get-tuple-element.27) | copy-start | bytes 6291460
  76.7 2.5 %copy-start.1 = (f32[8,256,256]{2,1,0:T(8,128)S(1)}, f32[8,256,256]{2,1,0:T(8,128)}, u32[]{:S(2)}) copy-start(f32[8,256,256]{2,1,0:T(8,128)} %get-tuple-element.25) | copy-start | bytes 6291460
  76.7 2.6 %copy-start.3 = (f32[8,256,256]{2,1,0:T(8,128)S(1)}, f32[8,256,256]{2,1,0:T(8,128)}, u32[]{:S(2)}) copy-start(f32[8,256,256]{2,1,0:T(8,128)} %get-tuple-element.18) | copy-start | bytes 6291460
  83.8 6.3 %copy-start.4 = (f32[2048]{0:T(1024)S(1)}, f32[2048]{0:T(1024)}, u32[]{:S(2)}) copy-start(f32[2048]{0:T(1024)} %param.7) | copy-start | bytes 24580
  83.8 54.8 %all-to-all-start.1 = ((f32[8,256,512]{2,1,0:T(8,128)}), f32[8,256,512]{2,1,0:T(8,128)}, u32[]{:S(2)}, u32[]{:S(2)}) async-start(f32[8,256,512]{2,1,0:T(8,128)} %fusion.8), calls=%async_computation.1 | async-start | bytes 8388608 | tf_op jit(solution)/shard_map/all_to_all | solution.py:340
  89.7 2.7 %copy-start.5 = (f32[2048]{0:T(1024)S(1)}, f32[2048]{0:T(1024)}, u32[]{:S(2)}) copy-start(f32[2048]{0:T(1024)} %param.9) | copy-start | bytes 24580

commit v9 on v8

--- a/solution.py
+++ b/solution.py
@@ -59,8 +59,9 @@
         imag_slots.append(
             sum(imag_terms[1:], imag_terms[0]) if imag_terms else jnp.zeros_like(slices[0])
         )
-    part_real = jnp.stack(real_slots)
-    part_imag = jnp.stack(imag_slots)
+    parts = jnp.stack(
+        [jnp.concatenate([re, im], axis=1) for re, im in zip(real_slots, imag_slots)]
+    )
     local_index = jnp.arange(width, dtype=jnp.int32)
     freqs = residue[:, None] + devices * local_index[None, :]
     phase = local_index[None, :, None] * freqs[:, None, :] % length
@@ -69,8 +70,8 @@
     sin_t = jnp.sin(angle)
     from_real = jnp.concatenate([cos_t, sin_t], axis=2)
     from_imag = jnp.concatenate([-sin_t, cos_t], axis=2)
-    spectrum = jnp.einsum("dyn,dnk->dyk", part_real, from_real, precision=precision_mid)
-    spectrum = spectrum + jnp.einsum("dyn,dnk->dyk", part_imag, from_imag, precision=precision_mid)
+    table = jnp.concatenate([from_real, from_imag], axis=1)
+    spectrum = jnp.einsum("dyn,dnk->dyk", parts, table, precision=precision_mid)
     return spectrum
 
 

time: 190 us -> 186 us (0.979)
  other arithmetic: 21.2 us -> 17 us
    neg x1 -> x0, other arithmetic: 9.8 us -> none  [x_stage(): from_imag = jnp.concatenate([-sin_t, cos_t], axis=2)]
    sin x0 -> x1, other arithmetic: none -> 9.79 us  [x_stage(): sin_t = jnp.sin(angle)]
    unnamed x8 -> x5, other arithmetic: 5.33 us -> 0.31 us
    dot_general x2 -> x1, matrix products: 7.12 us -> 7.08 us  [x_stage(): spectrum = jnp.einsum('dyn,dnk->dyk', parts, table, precision=precision_mid)]
where the time goes in v9:
time: 186 us
  waiting for transfers between devices  81.1 us (44%)
  Pallas kernels  47.9 us (26%)
  starting transfers between devices  21.5 us (12%)
  other arithmetic  17 us (9%)
  local copies, waits for them, and re-layouts  8.57 us (5%)
  matrix products  7.08 us (4%)
  between operations  2.58 us (1%)
    all_to_all x1, waiting for transfers between devices, per_device(): lax.all_to_all(outgoing, ('gy', 'gx'), split_axis=0, concat_axis=0, tiled...  43.2 us
    all_to_all x1, waiting for transfers between devices, per_device(): both = lax.all_to_all(both, 'gx', split_axis=0, concat_axis=0, tiled=True)  37.9 us
    pallas_call x1, Pallas kernels, y_stage(): pl.pallas_call(functools.partial(y_kernel, norm_factor), out_shape=(jax.S...  32 us
    pallas_call x1, Pallas kernels, total_everywhere(): pl.pallas_call(total_kernel, out_shape=jax.ShapeDtypeStruct((8, 128), jnp...  16 us
    all_to_all x1, starting transfers between devices, per_device(): lax.all_to_all(outgoing, ('gy', 'gx'), split_axis=0, concat_axis=0, tiled...  15.7 us
    sin x1, other arithmetic, x_stage(): sin_t = jnp.sin(angle)  9.79 us
    dot_general x1, matrix products, x_stage(): spectrum = jnp.einsum('dyn,dnk->dyk', parts, table, precision=precision_mid)  7.08 us
    sin x3, other arithmetic, root_table(): return (jnp.cos(angle), jnp.sin(angle))  5.97 us
  transfers between devices with their start and end apart: 2, of which 2 were waited for; matrix products, arithmetic and copies ran while one was open for 11% of the time, Pallas kernels for 0%

profile of v9, /device:TPU:1, one launch (start us, length us, event | category | flops | bytes accessed | tf_op | source)
XLA Modules:
  0.0 185.7 jit_solution(1863811704939939192)
XLA Ops:
  0.6 15.7 %all-to-all-start = ((f32[256,8,256]{2,1,0:T(8,128)}), f32[256,8,256]{2,1,0:T(8,128)S(1)}, u32[]{:S(2)}, u32[]{:S(2)}) async-start(f32[256,8,256]{2,1,0:T(8,128)} %bitcast.189), calls=%async_computation | async-start | bytes 4194304 | tf_op jit(solution)/shard_map/all_to_all | solution.py:338
  16.4 9.8 %fusion.14 = (f32[8,256,256]{2,1,0:T(8,128)}, f32[8,256,256]{2,1,0:T(8,128)}, f32[8,256,256]{2,1,0:T(8,128)}) fusion(s32[8,256]{1,0:T(8,128)S(1)} %broadcast_add_fusion), kind=kLoop, calls=%fused_computation.17 | loop fusion | flops 7864320 | bytes 6299648 | tf_op jit(solution)/shard_map/sin | solution.py:70
  26.2 43.2 %all-to-all-done = f32[256,8,256]{2,1,0:T(8,128)S(1)} async-done(((f32[256,8,256]{2,1,0:T(8,128)}), f32[256,8,256]{2,1,0:T(8,128)S(1)}, u32[]{:S(2)}, u32[]{:S(2)}) %all-to-all-start) | async-done | bytes 2097184 | tf_op jit(solution)/shard_map/all_to_all | solution.py:338
  69.3 0.2 add_add_fusion.2
  69.6 0.1 add_add_fusion.6
  69.7 0.2 add_add_fusion
  69.9 0.2 add_add_fusion.1
  70.7 1.0 copy-done
  71.7 0.6 copy-done.1
  72.3 0.6 copy-done.2
  73.0 7.1 %fusion = f32[8,256,512]{2,1,0:T(8,128)} fusion(f32[8,256,512]{2,1,0:T(8,128)S(1)} %fusion.24, f32[8,256,256]{2,1,0:T(8,128)S(1)} %copy-done.2, f32[8,256,256]{2,1,0:T(8,128)S(1)} %copy-done.1, f32[8,256,256]{2,1,0:T(8,128)S(1)} %copy-done), kind=kOutput, calls=%fused_computation | convolution fusion | flops 3227516928 | bytes 14680064 | tf_op jit(solution)/shard_map/dyn,dnk->dyk/dot_general | solution.py:74
  80.1 5.8 %all-to-all-start.1 = ((f32[8,256,512]{2,1,0:T(8,128)}), f32[8,256,512]{2,1,0:T(8,128)}, u32[]{:S(2)}, u32[]{:S(2)}) async-start(f32[8,256,512]{2,1,0:T(8,128)} %fusion), calls=%async_computation.1 | async-start | bytes 8388608 | tf_op jit(solution)/shard_map/all_to_all | solution.py:341
  85.9 0.1 mul.298
  86.0 0.4 copy.17
  86.5 0.1 copy.18
  86.5 2.1 %reshape.192.row_scale_ref = f32[2048,1]{1,0:T(8,128)} reshape(f32[64,32]{1,0:T(8,128)S(1)} %copy.18) | data formatting | bytes 16384 | tf_op jit(solution)/shard_map/reshape | solution.py:222
  88.8 2.1 %reshape.193.row_rate_ref = f32[2048,1]{1,0:T(8,128)} reshape(f32[64,32]{1,0:T(8,128)S(1)} %copy.19) | data formatting | bytes 16384 | tf_op jit(solution)/shard_map/reshape | solution.py:223
  90.9 0.7 fusion.45
  91.6 0.8 fusion.40
  92.4 4.5 %multiply_sine_fusion = (f32[2048,1]{1,0:T(8,128)}, f32[2048,1]{1,0:T(8,128)}) fusion(f32[2048,1]{1,0:T(8,128)S(1)} %copy.17), kind=kLoop, calls=%fused_computation.19 | loop fusion | flops 2048 | bytes 24576 | tf_op jit(solution)/shard_map/sin | solution.py:25
  96.9 37.9 %all-to-all-done.1 = f32[8,256,512]{2,1,0:T(8,128)} async-done(((f32[8,256,512]{2,1,0:T(8,128)}), f32[8,256,512]{2,1,0:T(8,128)}, u32[]{:S(2)}, u32[]{:S(2)}) %all-to-all-start.1) | async-done | bytes 4194336 | tf_op jit(solution)/shard_map/all_to_all | solution.py:341
  134.8 32.0 %shard_map.77 = (f32[2,32,64,256]{3,2,1,0:T(8,128)}, f32[8,128]{1,0:T(8,128)}) custom-call(f32[64,64]{1,0:T(8,128)} %get-tuple-element.29.cos_a_ref, f32[64,64]{1,0:T(8,128)} %get-tuple-element.28.sin_a_ref, f32[2048,1]{1,0:T(8,128)} %get-tuple-element.24.twist_cos_ref, f32[2048,1]{1,0:T(8,128)} %get-tuple-element.23.twist_sin_ref, ...), custom_call_target="tpu_custom_call" | custom-call | tf_op jit(solution)/shard_map/pallas_call | solution.py:227
  166.8 16.0 %shard_map.78 = f32[8,128]{1,0:T(8,128)} custom-call(f32[8,128]{1,0:T(8,128)} %get-tuple-element.5.value_ref), custom_call_target="tpu_custom_call" | custom-call | tf_op jit(solution)/shard_map/pallas_call | solution.py:315
  182.8 1.2 slice.35
  (24 shorter events, 0.8 us)
Async XLA Ops:
  0.6 68.7 %all-to-all-start = ((f32[256,8,256]{2,1,0:T(8,128)}), f32[256,8,256]{2,1,0:T(8,128)S(1)}, u32[]{:S(2)}, u32[]{:S(2)}) async-start(f32[256,8,256]{2,1,0:T(8,128)} %bitcast.189), calls=%async_computation | async-start | bytes 4194304 | tf_op jit(solution)/shard_map/all_to_all | solution.py:338
  70.1 1.6 copy-start
  70.1 2.2 %copy-start.1 = (f32[8,256,256]{2,1,0:T(8,128)S(1)}, f32[8,256,256]{2,1,0:T(8,128)}, u32[]{:S(2)}) copy-start(f32[8,256,256]{2,1,0:T(8,128)} %get-tuple-element.26) | copy-start | bytes 6291460
  70.1 2.8 %copy-start.2 = (f32[8,256,256]{2,1,0:T(8,128)S(1)}, f32[8,256,256]{2,1,0:T(8,128)}, u32[]{:S(2)}) copy-start(f32[8,256,256]{2,1,0:T(8,128)} %get-tuple-element.27) | copy-start | bytes 6291460
  80.1 6.3 %copy-start.3 = (f32[2048]{0:T(1024)S(1)}, f32[2048]{0:T(1024)}, u32[]{:S(2)}) copy-start(f32[2048]{0:T(1024)} %param.7) | copy-start | bytes 24580
  80.1 8.6 %copy-start.4 = (f32[2048]{0:T(1024)S(1)}, f32[2048]{0:T(1024)}, u32[]{:S(2)}) copy-start(f32[2048]{0:T(1024)} %param.9) | copy-start | bytes 24580
  80.1 54.7 %all-to-all-start.1 = ((f32[8,256,512]{2,1,0:T(8,128)}), f32[8,256,512]{2,1,0:T(8,128)}, u32[]{:S(2)}, u32[]{:S(2)}) async-start(f32[8,256,512]{2,1,0:T(8,128)} %fusion), calls=%async_computation.1 | async-start | bytes 8388608 | tf_op jit(solution)/shard_map/all_to_all | solution.py:341

commit v10 on v9

--- a/solution.py
+++ b/solution.py
@@ -122,7 +122,11 @@
     def dot(left, right):
         return jnp.dot(left, right, precision=precision_mid, preferred_element_type=jnp.float32)
 
-    both_a = jnp.concatenate([cos_a_ref[...], sin_a_ref[...]], axis=0)
+    cos_a = cos_a_ref[...]
+    sin_a = sin_a_ref[...]
+    both_a = jnp.concatenate(
+        [jnp.concatenate([cos_a, -sin_a], axis=1), jnp.concatenate([sin_a, cos_a], axis=1)], axis=0
+    )
 
     def first(index, carry):
         for part in range(2):
@@ -131,12 +135,12 @@
                 held.at[part, index],
                 in_sems.at[part, index],
             ).wait()
-        part_real = held[0, index].reshape(size_a, width)
-        part_imag = held[1, index].reshape(size_a, width)
-        from_real = dot(both_a, part_real)
-        from_imag = dot(both_a, part_imag)
-        out_real = from_real[:size_a] - from_imag[size_a:]
-        out_imag = from_imag[:size_a] + from_real[size_a:]
+        part = jnp.concatenate(
+            [held[0, index].reshape(size_a, width), held[1, index].reshape(size_a, width)], axis=0
+        )
+        result = dot(both_a, part)
+        out_real = result[:size_a]
+        out_imag = result[size_a:]
         rows_here = pl.ds(pl.multiple_of(index * size_a, size_a), size_a)
         twist_cos = twist_cos_ref[rows_here, :]
         twist_sin = twist_sin_ref[rows_here, :]
@@ -153,7 +157,11 @@
     col_scale = col_scale_ref[...]
     col_shift = col_shift_ref[...]
     col_mix = col_mix_ref[...]
-    both_b = jnp.concatenate([cos_b_ref[...], sin_b_ref[...]], axis=0)
+    cos_b = cos_b_ref[...]
+    sin_b = sin_b_ref[...]
+    both_b = jnp.concatenate(
+        [jnp.concatenate([cos_b, -sin_b], axis=1), jnp.concatenate([sin_b, cos_b], axis=1)], axis=0
+    )
 
     def second(index, total):
         picked = pl.ds(index, size_b, stride=size_a)
@@ -162,12 +170,10 @@
         row_rate = row_rate_ref[rows, :]
         for side in range(2):
             lanes = slice(side * half, (side + 1) * half)
-            part_real = step_real[side, picked, :]
-            part_imag = step_imag[side, picked, :]
-            from_real = dot(both_b, part_real)
-            from_imag = dot(both_b, part_imag)
-            spec_real = from_real[:size_b] - from_imag[size_b:]
-            spec_imag = from_imag[:size_b] + from_real[size_b:]
+            part = jnp.concatenate([step_real[side, picked, :], step_imag[side, picked, :]], axis=0)
+            result = dot(both_b, part)
+            spec_real = result[:size_b]
+            spec_imag = result[size_b:]
             scale = row_scale * col_scale[:, lanes]
             latent_u = spec_real * norm_factor * scale
             latent_v = spec_imag * norm_factor * scale

time: 186 us -> 184 us (0.989)
  Pallas kernels: 47.9 us -> 45.6 us
    pallas_call x1, Pallas kernels: 32 us -> 29.6 us  [y_stage(): pl.pallas_call(functools.partial(y_kernel, norm_factor), out_shape=(jax.S...]
where the time goes in v10:
time: 184 us; the launch traced here: 183 us
  waiting for transfers between devices  81.1 us (44%)
  Pallas kernels  45.6 us (25%)
  starting transfers between devices  21.5 us (12%)
  other arithmetic  17 us (9%)
  local copies, waits for them, and re-layouts  8.57 us (5%)
  matrix products  7.08 us (4%)
  between operations  2.58 us (1%)
    all_to_all x1, waiting for transfers between devices, per_device(): lax.all_to_all(outgoing, ('gy', 'gx'), split_axis=0, concat_axis=0, tiled...  43.2 us
    all_to_all x1, waiting for transfers between devices, per_device(): both = lax.all_to_all(both, 'gx', split_axis=0, concat_axis=0, tiled=True)  37.9 us
    pallas_call x1, Pallas kernels, y_stage(): pl.pallas_call(functools.partial(y_kernel, norm_factor), out_shape=(jax.S...  29.6 us
    pallas_call x1, Pallas kernels, total_everywhere(): pl.pallas_call(total_kernel, out_shape=jax.ShapeDtypeStruct((8, 128), jnp...  16 us
    all_to_all x1, starting transfers between devices, per_device(): lax.all_to_all(outgoing, ('gy', 'gx'), split_axis=0, concat_axis=0, tiled...  15.7 us
    sin x1, other arithmetic, x_stage(): sin_t = jnp.sin(angle)  9.79 us
    dot_general x1, matrix products, x_stage(): spectrum = jnp.einsum('dyn,dnk->dyk', parts, table, precision=precision_mid)  7.08 us
    sin x3, other arithmetic, root_table(): return (jnp.cos(angle), jnp.sin(angle))  5.97 us
  transfers between devices with their start and end apart: 2, of which 2 were waited for; matrix products, arithmetic and copies ran while one was open for 11% of the time, Pallas kernels for 0%

profile of v10, /device:TPU:1, one launch (start us, length us, event | category | flops | bytes accessed | tf_op | source)
XLA Modules:
  0.0 183.4 jit_solution(11929560741571228716)
XLA Ops:
  0.6 15.7 %all-to-all-start = ((f32[256,8,256]{2,1,0:T(8,128)}), f32[256,8,256]{2,1,0:T(8,128)S(1)}, u32[]{:S(2)}, u32[]{:S(2)}) async-start(f32[256,8,256]{2,1,0:T(8,128)} %bitcast.189), calls=%async_computation | async-start | bytes 4194304 | tf_op jit(solution)/shard_map/all_to_all | solution.py:344
  16.4 9.8 %fusion.14 = (f32[8,256,256]{2,1,0:T(8,128)}, f32[8,256,256]{2,1,0:T(8,128)}, f32[8,256,256]{2,1,0:T(8,128)}) fusion(s32[8,256]{1,0:T(8,128)S(1)} %broadcast_add_fusion), kind=kLoop, calls=%fused_computation.17 | loop fusion | flops 7864320 | bytes 6299648 | tf_op jit(solution)/shard_map/sin | solution.py:70
  26.2 43.2 %all-to-all-done = f32[256,8,256]{2,1,0:T(8,128)S(1)} async-done(((f32[256,8,256]{2,1,0:T(8,128)}), f32[256,8,256]{2,1,0:T(8,128)S(1)}, u32[]{:S(2)}, u32[]{:S(2)}) %all-to-all-start) | async-done | bytes 2097184 | tf_op jit(solution)/shard_map/all_to_all | solution.py:344
  69.3 0.2 add_add_fusion.2
  69.6 0.1 add_add_fusion.6
  69.7 0.2 add_add_fusion
  69.9 0.2 add_add_fusion.1
  70.7 1.0 copy-done
  71.7 0.6 copy-done.1
  72.3 0.6 copy-done.2
  73.0 7.1 %fusion = f32[8,256,512]{2,1,0:T(8,128)} fusion(f32[8,256,512]{2,1,0:T(8,128)S(1)} %fusion.24, f32[8,256,256]{2,1,0:T(8,128)S(1)} %copy-done.2, f32[8,256,256]{2,1,0:T(8,128)S(1)} %copy-done.1, f32[8,256,256]{2,1,0:T(8,128)S(1)} %copy-done), kind=kOutput, calls=%fused_computation | convolution fusion | flops 3227516928 | bytes 14680064 | tf_op jit(solution)/shard_map/dyn,dnk->dyk/dot_general | solution.py:74
  80.1 5.8 %all-to-all-start.1 = ((f32[8,256,512]{2,1,0:T(8,128)}), f32[8,256,512]{2,1,0:T(8,128)}, u32[]{:S(2)}, u32[]{:S(2)}) async-start(f32[8,256,512]{2,1,0:T(8,128)} %fusion), calls=%async_computation.1 | async-start | bytes 8388608 | tf_op jit(solution)/shard_map/all_to_all | solution.py:347
  85.9 0.1 mul.298
  86.0 0.4 copy.17
  86.5 0.1 copy.18
  86.5 2.1 %reshape.192.row_scale_ref = f32[2048,1]{1,0:T(8,128)} reshape(f32[64,32]{1,0:T(8,128)S(1)} %copy.18) | data formatting | bytes 16384 | tf_op jit(solution)/shard_map/reshape | solution.py:228
  88.8 2.1 %reshape.193.row_rate_ref = f32[2048,1]{1,0:T(8,128)} reshape(f32[64,32]{1,0:T(8,128)S(1)} %copy.19) | data formatting | bytes 16384 | tf_op jit(solution)/shard_map/reshape | solution.py:229
  90.9 0.7 fusion.45
  91.6 0.8 fusion.40
  92.4 4.5 %multiply_sine_fusion = (f32[2048,1]{1,0:T(8,128)}, f32[2048,1]{1,0:T(8,128)}) fusion(f32[2048,1]{1,0:T(8,128)S(1)} %copy.17), kind=kLoop, calls=%fused_computation.19 | loop fusion | flops 2048 | bytes 24576 | tf_op jit(solution)/shard_map/sin | solution.py:25
  96.9 37.9 %all-to-all-done.1 = f32[8,256,512]{2,1,0:T(8,128)} async-done(((f32[8,256,512]{2,1,0:T(8,128)}), f32[8,256,512]{2,1,0:T(8,128)}, u32[]{:S(2)}, u32[]{:S(2)}) %all-to-all-start.1) | async-done | bytes 4194336 | tf_op jit(solution)/shard_map/all_to_all | solution.py:347
  134.8 29.6 %shard_map.77 = (f32[2,32,64,256]{3,2,1,0:T(8,128)}, f32[8,128]{1,0:T(8,128)}) custom-call(f32[64,64]{1,0:T(8,128)} %get-tuple-element.29.cos_a_ref, f32[64,64]{1,0:T(8,128)} %get-tuple-element.28.sin_a_ref, f32[2048,1]{1,0:T(8,128)} %get-tuple-element.24.twist_cos_ref, f32[2048,1]{1,0:T(8,128)} %get-tuple-element.23.twist_sin_ref, ...), custom_call_target="tpu_custom_call" | custom-call | tf_op jit(solution)/shard_map/pallas_call | solution.py:233
  164.4 16.0 %shard_map.78 = f32[8,128]{1,0:T(8,128)} custom-call(f32[8,128]{1,0:T(8,128)} %get-tuple-element.5.value_ref), custom_call_target="tpu_custom_call" | custom-call | tf_op jit(solution)/shard_map/pallas_call | solution.py:321
  180.4 1.2 slice.35
  (24 shorter events, 0.8 us)
Async XLA Ops:
  0.6 68.7 %all-to-all-start = ((f32[256,8,256]{2,1,0:T(8,128)}), f32[256,8,256]{2,1,0:T(8,128)S(1)}, u32[]{:S(2)}, u32[]{:S(2)}) async-start(f32[256,8,256]{2,1,0:T(8,128)} %bitcast.189), calls=%async_computation | async-start | bytes 4194304 | tf_op jit(solution)/shard_map/all_to_all | solution.py:344
  70.1 1.6 copy-start
  70.1 2.2 %copy-start.1 = (f32[8,256,256]{2,1,0:T(8,128)S(1)}, f32[8,256,256]{2,1,0:T(8,128)}, u32[]{:S(2)}) copy-start(f32[8,256,256]{2,1,0:T(8,128)} %get-tuple-element.26) | copy-start | bytes 6291460
  70.1 2.8 %copy-start.2 = (f32[8,256,256]{2,1,0:T(8,128)S(1)}, f32[8,256,256]{2,1,0:T(8,128)}, u32[]{:S(2)}) copy-start(f32[8,256,256]{2,1,0:T(8,128)} %get-tuple-element.27) | copy-start | bytes 6291460
  80.1 6.3 %copy-start.3 = (f32[2048]{0:T(1024)S(1)}, f32[2048]{0:T(1024)}, u32[]{:S(2)}) copy-start(f32[2048]{0:T(1024)} %param.7) | copy-start | bytes 24580
  80.1 8.6 %copy-start.4 = (f32[2048]{0:T(1024)S(1)}, f32[2048]{0:T(1024)}, u32[]{:S(2)}) copy-start(f32[2048]{0:T(1024)} %param.9) | copy-start | bytes 24580
  80.1 54.7 %all-to-all-start.1 = ((f32[8,256,512]{2,1,0:T(8,128)}), f32[8,256,512]{2,1,0:T(8,128)}, u32[]{:S(2)}, u32[]{:S(2)}) async-start(f32[8,256,512]{2,1,0:T(8,128)} %fusion), calls=%async_computation.1 | async-start | bytes 8388608 | tf_op jit(solution)/shard_map/all_to_all | solution.py:347

commit v11 on v10

--- a/solution.py
+++ b/solution.py
@@ -99,8 +99,7 @@
     return (final_real.reshape(planes, length, width), final_imag.reshape(planes, length, width))
 
 
-def y_kernel(norm_factor, cos_a_ref, sin_a_ref, twist_cos_ref, twist_sin_ref,
-             cos_b_ref, sin_b_ref, row_scale_ref, row_rate_ref, col_scale_ref, col_shift_ref,
+def y_kernel(norm_factor, cos_a_ref, sin_a_ref, table_b_ref, row_scale_ref, row_rate_ref, col_scale_ref, col_shift_ref,
              col_mix_ref, spectrum_hbm, out_hbm, sum_ref,
              held, step_real, step_imag, staged, in_sems, out_sems):
     high, low, blocks, rows, both_width = spectrum_hbm.shape
@@ -139,13 +138,9 @@
             [held[0, index].reshape(size_a, width), held[1, index].reshape(size_a, width)], axis=0
         )
         result = dot(both_a, part)
-        out_real = result[:size_a]
-        out_imag = result[size_a:]
+        turned_real = result[:size_a]
+        turned_imag = result[size_a:]
         rows_here = pl.ds(pl.multiple_of(index * size_a, size_a), size_a)
-        twist_cos = twist_cos_ref[rows_here, :]
-        twist_sin = twist_sin_ref[rows_here, :]
-        turned_real = out_real * twist_cos - out_imag * twist_sin
-        turned_imag = out_real * twist_sin + out_imag * twist_cos
         for side in range(2):
             lanes = slice(side * half, (side + 1) * half)
             step_real[side, rows_here, :] = turned_real[:, lanes]
@@ -157,11 +152,6 @@
     col_scale = col_scale_ref[...]
     col_shift = col_shift_ref[...]
     col_mix = col_mix_ref[...]
-    cos_b = cos_b_ref[...]
-    sin_b = sin_b_ref[...]
-    both_b = jnp.concatenate(
-        [jnp.concatenate([cos_b, -sin_b], axis=1), jnp.concatenate([sin_b, cos_b], axis=1)], axis=0
-    )
 
     def second(index, total):
         picked = pl.ds(index, size_b, stride=size_a)
@@ -171,7 +161,7 @@
         for side in range(2):
             lanes = slice(side * half, (side + 1) * half)
             part = jnp.concatenate([step_real[side, picked, :], step_imag[side, picked, :]], axis=0)
-            result = dot(both_b, part)
+            result = dot(table_b_ref[index], part)
             spec_real = result[:size_b]
             spec_imag = result[size_b:]
             scale = row_scale * col_scale[:, lanes]
@@ -221,10 +211,14 @@
     index_b = jnp.arange(size_b, dtype=jnp.int32)
     order_a = (index_a % blocks) * high + index_a // blocks
     cos_a, sin_a = root_table(index_a, order_a, size_a)
-    cos_b, sin_b = root_table(index_b, index_b, size_b)
-    twist_cos, twist_sin = root_table(index_b, index_a, length)
-    twist_cos = twist_cos.reshape(length, 1)
-    twist_sin = twist_sin.reshape(length, 1)
+    out_rows = size_a * index_b[None, :, None] + index_a[:, None, None]
+    phase = index_b[None, None, :] * out_rows % length
+    angle = phase.astype(jnp.float32) * (-2.0 * math.pi / length)
+    cos_b = jnp.cos(angle)
+    sin_b = jnp.sin(angle)
+    table_b = jnp.concatenate(
+        [jnp.concatenate([cos_b, -sin_b], axis=2), jnp.concatenate([sin_b, cos_b], axis=2)], axis=1
+    )
     row_scale_t = row_scale.reshape(size_b, size_a).T.reshape(length, 1)
     row_rate_t = row_rate.reshape(size_b, size_a).T.reshape(length, 1)
     vmem = pl.BlockSpec(memory_space=pltpu.VMEM)
@@ -236,7 +230,7 @@
             jax.ShapeDtypeStruct((2, size_b, size_a, width), jnp.float32),
             jax.ShapeDtypeStruct((8, 128), jnp.float32),
         ),
-        in_specs=[vmem] * 11 + [anywhere],
+        in_specs=[vmem] * 8 + [anywhere],
         out_specs=(anywhere, vmem),
         scratch_shapes=[
             pltpu.VMEM((2, size_b, high, blocks, width), jnp.float32),
@@ -248,7 +242,7 @@
         ],
         compiler_params=pltpu.CompilerParams(vmem_limit_bytes=60 * 1024 * 1024),
     )(
-        cos_a, sin_a, twist_cos, twist_sin, cos_b, sin_b,
+        cos_a, sin_a, table_b,
         row_scale_t, row_rate_t, col_scale.reshape(1, width), col_shift.reshape(1, width),
         col_mix.reshape(1, width), shaped,
     )

time: 184 us -> 184 us (level)
    sin x3 -> x1, other arithmetic: 5.97 us -> 0.77 us  [root_table(): return (jnp.cos(angle), jnp.sin(angle))]
    neg x0 -> x1, other arithmetic: none -> 4.16 us  [y_stage(): -sin_b]
    concatenate x0 -> x1, other arithmetic: none -> 1.97 us  [y_stage(): jnp.concatenate([jnp.concatenate([cos_b, -sin_b], axis=2), jnp.concatenat...]
  transfers between devices with their start and end apart: 2 -> 2, of which waited for: 2 -> 2; matrix products, arithmetic and copies ran while one was open for 11% -> 12% of each run, Pallas kernels for 0% -> 0%
where the time goes in v11:
time: 184 us; the launch traced here: 183 us
  waiting for transfers between devices  80.6 us (44%)
  Pallas kernels  45.3 us (25%)
  starting transfers between devices  21.5 us (12%)
  other arithmetic  17.9 us (10%)
  local copies, waits for them, and re-layouts  8.28 us (4%)
  matrix products  7.07 us (4%)
  between operations  2.57 us (1%)
    all_to_all x1, waiting for transfers between devices, per_device(): lax.all_to_all(outgoing, ('gy', 'gx'), split_axis=0, concat_axis=0, tiled...  43.2 us
    all_to_all x1, waiting for transfers between devices, per_device(): both = lax.all_to_all(both, 'gx', split_axis=0, concat_axis=0, tiled=True)  37.5 us
    pallas_call x1, Pallas kernels, y_stage(): pl.pallas_call(functools.partial(y_kernel, norm_factor), out_shape=(jax.S...  29.4 us
    pallas_call x1, Pallas kernels, total_everywhere(): pl.pallas_call(total_kernel, out_shape=jax.ShapeDtypeStruct((8, 128), jnp...  16 us
    all_to_all x1, starting transfers between devices, per_device(): lax.all_to_all(outgoing, ('gy', 'gx'), split_axis=0, concat_axis=0, tiled...  15.7 us
    sin x1, other arithmetic, x_stage(): sin_t = jnp.sin(angle)  9.78 us
    dot_general x1, matrix products, x_stage(): spectrum = jnp.einsum('dyn,dnk->dyk', parts, table, precision=precision_mid)  7.07 us
    all_to_all x1, starting transfers between devices, per_device(): both = lax.all_to_all(both, 'gx', split_axis=0, concat_axis=0, tiled=True)  5.82 us
  transfers between devices with their start and end apart: 2, of which 2 were waited for; matrix products, arithmetic and copies ran while one was open for 12% of the time, Pallas kernels for 0%

profile of v11, /device:TPU:1, one launch (start us, length us, event | category | flops | bytes accessed | tf_op | source)
XLA Modules:
  0.0 183.3 jit_solution(16820570084775760786)
XLA Ops:
  0.6 15.7 %all-to-all-start = ((f32[256,8,256]{2,1,0:T(8,128)}), f32[256,8,256]{2,1,0:T(8,128)S(1)}, u32[]{:S(2)}, u32[]{:S(2)}) async-start(f32[256,8,256]{2,1,0:T(8,128)} %bitcast.189), calls=%async_computation | async-start | bytes 4194304 | tf_op jit(solution)/shard_map/all_to_all | solution.py:338
  16.3 0.1 broadcast_add_fusion
  16.4 9.8 %fusion.17 = (f32[8,256,256]{2,1,0:T(8,128)}, f32[8,256,256]{2,1,0:T(8,128)}, f32[8,256,256]{2,1,0:T(8,128)}) fusion(s32[8,256]{1,0:T(8,128)S(1)} %broadcast_add_fusion), kind=kLoop, calls=%fused_computation.24 | loop fusion | flops 7864320 | bytes 6299648 | tf_op jit(solution)/shard_map/sin | solution.py:70
  26.2 43.2 %all-to-all-done = f32[256,8,256]{2,1,0:T(8,128)S(1)} async-done(((f32[256,8,256]{2,1,0:T(8,128)}), f32[256,8,256]{2,1,0:T(8,128)S(1)}, u32[]{:S(2)}, u32[]{:S(2)}) %all-to-all-start) | async-done | bytes 2097184 | tf_op jit(solution)/shard_map/all_to_all | solution.py:338
  69.3 0.2 add_add_fusion.2
  69.6 0.1 add_add_fusion.6
  69.7 0.2 add_add_fusion
  69.9 0.2 add_add_fusion.1
  70.7 1.2 copy-done.2
  71.8 0.7 copy-done
  72.5 0.6 copy-done.1
  73.1 7.1 %fusion = f32[8,256,512]{2,1,0:T(8,128)} fusion(f32[8,256,512]{2,1,0:T(8,128)S(1)} %fusion.30, f32[8,256,256]{2,1,0:T(8,128)S(1)} %copy-done.2, f32[8,256,256]{2,1,0:T(8,128)S(1)} %copy-done.1, f32[8,256,256]{2,1,0:T(8,128)S(1)} %copy-done), kind=kOutput, calls=%fused_computation | convolution fusion | flops 3227516928 | bytes 14680064 | tf_op jit(solution)/shard_map/dyn,dnk->dyk/dot_general | solution.py:74
  80.2 5.8 %all-to-all-start.1 = ((f32[8,256,512]{2,1,0:T(8,128)}), f32[8,256,512]{2,1,0:T(8,128)}, u32[]{:S(2)}, u32[]{:S(2)}) async-start(f32[8,256,512]{2,1,0:T(8,128)} %fusion), calls=%async_computation.1 | async-start | bytes 8388608 | tf_op jit(solution)/shard_map/all_to_all | solution.py:341
  86.1 0.1 copy.9
  86.2 2.1 %reshape.139.row_scale_ref = f32[2048,1]{1,0:T(8,128)} reshape(f32[64,32]{1,0:T(8,128)S(1)} %copy.9) | data formatting | bytes 16384 | tf_op jit(solution)/shard_map/reshape | solution.py:222
  88.3 0.1 copy.10
  88.4 2.1 %reshape.140.row_rate_ref = f32[2048,1]{1,0:T(8,128)} reshape(f32[64,32]{1,0:T(8,128)S(1)} %copy.10) | data formatting | bytes 16384 | tf_op jit(solution)/shard_map/reshape | solution.py:223
  90.6 4.2 %fusion.37 = (f32[64,32,32]{2,1,0:T(8,128)S(1)}, f32[64,32,32]{2,1,0:T(8,128)S(1)}, f32[64,32,32]{2,1,0:T(8,128)S(1)}) fusion(s32[64,32]{1,0:T(8,128)S(1)} %iota_add_fusion), kind=kLoop, calls=%fused_computation.52 | loop fusion | flops 983040 | bytes 794624 | tf_op jit(solution)/shard_map/neg | solution.py:220
  94.7 2.0 %maximum_maximum_fusion.table_b_ref = f32[64,64,64]{2,1,0:T(8,128)} fusion(f32[64,32,32]{2,1,0:T(8,128)S(1)} %get-tuple-element.23, f32[64,32,32]{2,1,0:T(8,128)S(1)} %get-tuple-element.22, f32[64,32,32]{2,1,0:T(8,128)S(1)} %get-tuple-element.21), kind=kLoop, calls=%fused_computation.14 | loop fusion | flops 786432 | bytes 1835008 | tf_op jit(solution)/shard_map/concatenate | solution.py:219
  96.7 0.8 fusion.44
  97.5 37.5 %all-to-all-done.1 = f32[8,256,512]{2,1,0:T(8,128)} async-done(((f32[8,256,512]{2,1,0:T(8,128)}), f32[8,256,512]{2,1,0:T(8,128)}, u32[]{:S(2)}, u32[]{:S(2)}) %all-to-all-start.1) | async-done | bytes 4194336 | tf_op jit(solution)/shard_map/all_to_all | solution.py:341
  135.0 29.4 %shard_map.77 = (f32[2,32,64,256]{3,2,1,0:T(8,128)}, f32[8,128]{1,0:T(8,128)}) custom-call(f32[64,64]{1,0:T(8,128)} %get-tuple-element.28.cos_a_ref, f32[64,64]{1,0:T(8,128)} %get-tuple-element.27.sin_a_ref, f32[64,64,64]{2,1,0:T(8,128)} %maximum_maximum_fusion.table_b_ref, f32[2048,1]{1,0:T(8,128)} %reshape.139.row_scale_ref, ...), custom_call_target="tpu_custom_call" | custom-call | tf_op jit(solution)/shard_map/pallas_call | solution.py:227
  164.3 16.0 %shard_map.78 = f32[8,128]{1,0:T(8,128)} custom-call(f32[8,128]{1,0:T(8,128)} %get-tuple-element.5.value_ref), custom_call_target="tpu_custom_call" | custom-call | tf_op jit(solution)/shard_map/pallas_call | solution.py:315
  180.3 1.2 slice.35
  (22 shorter events, 0.6 us)
Async XLA Ops:
  0.6 68.7 %all-to-all-start = ((f32[256,8,256]{2,1,0:T(8,128)}), f32[256,8,256]{2,1,0:T(8,128)S(1)}, u32[]{:S(2)}, u32[]{:S(2)}) async-start(f32[256,8,256]{2,1,0:T(8,128)} %bitcast.189), calls=%async_computation | async-start | bytes 4194304 | tf_op jit(solution)/shard_map/all_to_all | solution.py:338
  70.2 1.6 copy-start.2
  70.4 2.1 %copy-start = (f32[8,256,256]{2,1,0:T(8,128)S(1)}, f32[8,256,256]{2,1,0:T(8,128)}, u32[]{:S(2)}) copy-start(f32[8,256,256]{2,1,0:T(8,128)} %get-tuple-element.24) | copy-start | bytes 6291460
  70.4 2.7 %copy-start.1 = (f32[8,256,256]{2,1,0:T(8,128)S(1)}, f32[8,256,256]{2,1,0:T(8,128)}, u32[]{:S(2)}) copy-start(f32[8,256,256]{2,1,0:T(8,128)} %get-tuple-element.25) | copy-start | bytes 6291460
  80.2 5.8 %copy-start.3 = (f32[2048]{0:T(1024)S(1)}, f32[2048]{0:T(1024)}, u32[]{:S(2)}) copy-start(f32[2048]{0:T(1024)} %param.7) | copy-start | bytes 24580
  80.2 8.1 %copy-start.4 = (f32[2048]{0:T(1024)S(1)}, f32[2048]{0:T(1024)}, u32[]{:S(2)}) copy-start(f32[2048]{0:T(1024)} %param.9) | copy-start | bytes 24580
  80.2 54.7 %all-to-all-start.1 = ((f32[8,256,512]{2,1,0:T(8,128)}), f32[8,256,512]{2,1,0:T(8,128)}, u32[]{:S(2)}, u32[]{:S(2)}) async-start(f32[8,256,512]{2,1,0:T(8,128)} %fusion), calls=%async_computation.1 | async-start | bytes 8388608 | tf_op jit(solution)/shard_map/all_to_all | solution.py:341

commit v12 on v11

--- a/solution.py
+++ b/solution.py
@@ -101,7 +101,7 @@
 
 def y_kernel(norm_factor, cos_a_ref, sin_a_ref, table_b_ref, row_scale_ref, row_rate_ref, col_scale_ref, col_shift_ref,
              col_mix_ref, spectrum_hbm, out_hbm, sum_ref,
-             held, step_real, step_imag, staged, in_sems, out_sems):
+             held, step_a, turned, staged, in_sems, out_sems, turn_sems):
     high, low, blocks, rows, both_width = spectrum_hbm.shape
     width = both_width // 2
     size_b = low * rows
@@ -138,53 +138,55 @@
             [held[0, index].reshape(size_a, width), held[1, index].reshape(size_a, width)], axis=0
         )
         result = dot(both_a, part)
-        turned_real = result[:size_a]
-        turned_imag = result[size_a:]
-        rows_here = pl.ds(pl.multiple_of(index * size_a, size_a), size_a)
-        for side in range(2):
-            lanes = slice(side * half, (side + 1) * half)
-            step_real[side, rows_here, :] = turned_real[:, lanes]
-            step_imag[side, rows_here, :] = turned_imag[:, lanes]
+        step_a[0, index] = result[:size_a]
+        step_a[1, index] = result[size_a:]
+        for part in range(2):
+            pltpu.make_async_copy(
+                step_a.at[part, index], turned.at[part, :, index, :], turn_sems.at[part, index]
+            ).start()
         return carry
 
     lax.fori_loop(0, size_b, first, 0)
+
+    def settle(index, carry):
+        for part in range(2):
+            pltpu.make_async_copy(
+                step_a.at[part, index], turned.at[part, :, index, :], turn_sems.at[part, index]
+            ).wait()
+        return carry
+
+    lax.fori_loop(0, size_b, settle, 0)
 
     col_scale = col_scale_ref[...]
     col_shift = col_shift_ref[...]
     col_mix = col_mix_ref[...]
 
     def second(index, total):
-        picked = pl.ds(index, size_b, stride=size_a)
         rows = pl.ds(pl.multiple_of(index * size_b, size_b), size_b)
-        row_scale = row_scale_ref[rows, :]
-        row_rate = row_rate_ref[rows, :]
-        for side in range(2):
-            lanes = slice(side * half, (side + 1) * half)
-            part = jnp.concatenate([step_real[side, picked, :], step_imag[side, picked, :]], axis=0)
-            result = dot(table_b_ref[index], part)
-            spec_real = result[:size_b]
-            spec_imag = result[size_b:]
-            scale = row_scale * col_scale[:, lanes]
-            latent_u = spec_real * norm_factor * scale
-            latent_v = spec_imag * norm_factor * scale
-            log_scale = row_rate * jnp.tanh(latent_u + col_shift[:, lanes])
-            latent_w = latent_v * jnp.exp(log_scale) + col_mix[:, lanes] * latent_u
-            terms = (
-                -0.5 * (latent_u * latent_u + latent_w * latent_w)
-                - math.log(2.0 * math.pi)
-                + log_scale
-                + 2.0 * jnp.log(scale)
-            )
-            staged[0, index, :, lanes] = latent_u
-            staged[1, index, :, lanes] = latent_w
-            total = total + terms
+        part = jnp.concatenate([turned[0, index], turned[1, index]], axis=0)
+        result = dot(table_b_ref[index], part)
+        spec_real = result[:size_b]
+        spec_imag = result[size_b:]
+        scale = row_scale_ref[rows, :] * col_scale
+        latent_u = spec_real * norm_factor * scale
+        latent_v = spec_imag * norm_factor * scale
+        log_scale = row_rate_ref[rows, :] * jnp.tanh(latent_u + col_shift)
+        latent_w = latent_v * jnp.exp(log_scale) + col_mix * latent_u
+        terms = (
+            -0.5 * (latent_u * latent_u + latent_w * latent_w)
+            - math.log(2.0 * math.pi)
+            + log_scale
+            + 2.0 * jnp.log(scale)
+        )
+        staged[0, index] = latent_u
+        staged[1, index] = latent_w
         for part in range(2):
             pltpu.make_async_copy(
                 staged.at[part, index], out_hbm.at[part, :, index, :], out_sems.at[part, index]
             ).start()
-        return total
-
-    total = lax.fori_loop(0, size_a, second, jnp.zeros((size_b, half), jnp.float32))
+        return total + terms
+
+    total = lax.fori_loop(0, size_a, second, jnp.zeros((size_b, width), jnp.float32))
     sum_ref[...] = jnp.broadcast_to(jnp.sum(total), sum_ref.shape)
 
     def finish(index, carry):
@@ -234,11 +236,12 @@
         out_specs=(anywhere, vmem),
         scratch_shapes=[
             pltpu.VMEM((2, size_b, high, blocks, width), jnp.float32),
-            pltpu.VMEM((2, length, width // 2), jnp.float32),
-            pltpu.VMEM((2, length, width // 2), jnp.float32),
+            pltpu.VMEM((2, size_b, size_a, width), jnp.float32),
+            pltpu.VMEM((2, size_a, size_b, width), jnp.float32),
             pltpu.VMEM((2, size_a, size_b, width), jnp.float32),
             pltpu.SemaphoreType.DMA((2, size_b)),
             pltpu.SemaphoreType.DMA((2, size_a)),
+            pltpu.SemaphoreType.DMA((2, size_b)),
         ],
         compiler_params=pltpu.CompilerParams(vmem_limit_bytes=60 * 1024 * 1024),
     )(

time: 184 us -> 183 us (level)
  no operation moved by 1% of the time
where the time goes in v12:
time: 183 us
  waiting for transfers between devices  80.6 us (44%)
  Pallas kernels  44.6 us (24%)
  starting transfers between devices  21.5 us (12%)
  other arithmetic  17.9 us (10%)
  local copies, waits for them, and re-layouts  8.28 us (5%)
  matrix products  7.07 us (4%)
  between operations  2.57 us (1%)
    all_to_all x1, waiting for transfers between devices, per_device(): lax.all_to_all(outgoing, ('gy', 'gx'), split_axis=0, concat_axis=0, tiled...  43.2 us
    all_to_all x1, waiting for transfers between devices, per_device(): both = lax.all_to_all(both, 'gx', split_axis=0, concat_axis=0, tiled=True)  37.5 us
    pallas_call x1, Pallas kernels, y_stage(): pl.pallas_call(functools.partial(y_kernel, norm_factor), out_shape=(jax.S...  28.6 us
    pallas_call x1, Pallas kernels, total_everywhere(): pl.pallas_call(total_kernel, out_shape=jax.ShapeDtypeStruct((8, 128), jnp...  16 us
    all_to_all x1, starting transfers between devices, per_device(): lax.all_to_all(outgoing, ('gy', 'gx'), split_axis=0, concat_axis=0, tiled...  15.7 us
    sin x1, other arithmetic, x_stage(): sin_t = jnp.sin(angle)  9.78 us
    dot_general x1, matrix products, x_stage(): spectrum = jnp.einsum('dyn,dnk->dyk', parts, table, precision=precision_mid)  7.07 us
    all_to_all x1, starting transfers between devices, per_device(): both = lax.all_to_all(both, 'gx', split_axis=0, concat_axis=0, tiled=True)  5.82 us
  transfers between devices with their start and end apart: 2, of which 2 were waited for; matrix products, arithmetic and copies ran while one was open for 12% of the time, Pallas kernels for 0%

profile of v12, /device:TPU:1, one launch (start us, length us, event | category | flops | bytes accessed | tf_op | source)
XLA Modules:
  0.0 182.6 jit_solution(452626155919233922)
XLA Ops:
  0.6 15.7 %all-to-all-start = ((f32[256,8,256]{2,1,0:T(8,128)}), f32[256,8,256]{2,1,0:T(8,128)S(1)}, u32[]{:S(2)}, u32[]{:S(2)}) async-start(f32[256,8,256]{2,1,0:T(8,128)} %bitcast.189), calls=%async_computation | async-start | bytes 4194304 | tf_op jit(solution)/shard_map/all_to_all | solution.py:341
  16.3 0.1 broadcast_add_fusion
  16.4 9.8 %fusion.17 = (f32[8,256,256]{2,1,0:T(8,128)}, f32[8,256,256]{2,1,0:T(8,128)}, f32[8,256,256]{2,1,0:T(8,128)}) fusion(s32[8,256]{1,0:T(8,128)S(1)} %broadcast_add_fusion), kind=kLoop, calls=%fused_computation.24 | loop fusion | flops 7864320 | bytes 6299648 | tf_op jit(solution)/shard_map/sin | solution.py:70
  26.2 43.2 %all-to-all-done = f32[256,8,256]{2,1,0:T(8,128)S(1)} async-done(((f32[256,8,256]{2,1,0:T(8,128)}), f32[256,8,256]{2,1,0:T(8,128)S(1)}, u32[]{:S(2)}, u32[]{:S(2)}) %all-to-all-start) | async-done | bytes 2097184 | tf_op jit(solution)/shard_map/all_to_all | solution.py:341
  69.3 0.2 add_add_fusion.2
  69.6 0.1 add_add_fusion.6
  69.7 0.2 add_add_fusion
  69.9 0.2 add_add_fusion.1
  70.7 1.2 copy-done.2
  71.8 0.7 copy-done
  72.5 0.6 copy-done.1
  73.1 7.1 %fusion = f32[8,256,512]{2,1,0:T(8,128)} fusion(f32[8,256,512]{2,1,0:T(8,128)S(1)} %fusion.30, f32[8,256,256]{2,1,0:T(8,128)S(1)} %copy-done.2, f32[8,256,256]{2,1,0:T(8,128)S(1)} %copy-done.1, f32[8,256,256]{2,1,0:T(8,128)S(1)} %copy-done), kind=kOutput, calls=%fused_computation | convolution fusion | flops 3227516928 | bytes 14680064 | tf_op jit(solution)/shard_map/dyn,dnk->dyk/dot_general | solution.py:74
  80.2 5.8 %all-to-all-start.1 = ((f32[8,256,512]{2,1,0:T(8,128)}), f32[8,256,512]{2,1,0:T(8,128)}, u32[]{:S(2)}, u32[]{:S(2)}) async-start(f32[8,256,512]{2,1,0:T(8,128)} %fusion), calls=%async_computation.1 | async-start | bytes 8388608 | tf_op jit(solution)/shard_map/all_to_all | solution.py:344
  86.1 0.1 copy.9
  86.2 2.1 %reshape.139.row_scale_ref = f32[2048,1]{1,0:T(8,128)} reshape(f32[64,32]{1,0:T(8,128)S(1)} %copy.9) | data formatting | bytes 16384 | tf_op jit(solution)/shard_map/reshape | solution.py:224
  88.3 0.1 copy.10
  88.4 2.1 %reshape.140.row_rate_ref = f32[2048,1]{1,0:T(8,128)} reshape(f32[64,32]{1,0:T(8,128)S(1)} %copy.10) | data formatting | bytes 16384 | tf_op jit(solution)/shard_map/reshape | solution.py:225
  90.6 4.2 %fusion.37 = (f32[64,32,32]{2,1,0:T(8,128)S(1)}, f32[64,32,32]{2,1,0:T(8,128)S(1)}, f32[64,32,32]{2,1,0:T(8,128)S(1)}) fusion(s32[64,32]{1,0:T(8,128)S(1)} %iota_add_fusion), kind=kLoop, calls=%fused_computation.52 | loop fusion | flops 983040 | bytes 794624 | tf_op jit(solution)/shard_map/neg | solution.py:222
  94.7 2.0 %maximum_maximum_fusion.table_b_ref = f32[64,64,64]{2,1,0:T(8,128)} fusion(f32[64,32,32]{2,1,0:T(8,128)S(1)} %get-tuple-element.23, f32[64,32,32]{2,1,0:T(8,128)S(1)} %get-tuple-element.22, f32[64,32,32]{2,1,0:T(8,128)S(1)} %get-tuple-element.21), kind=kLoop, calls=%fused_computation.14 | loop fusion | flops 786432 | bytes 1835008 | tf_op jit(solution)/shard_map/concatenate | solution.py:221
  96.7 0.8 fusion.44
  97.5 37.5 %all-to-all-done.1 = f32[8,256,512]{2,1,0:T(8,128)} async-done(((f32[8,256,512]{2,1,0:T(8,128)}), f32[8,256,512]{2,1,0:T(8,128)}, u32[]{:S(2)}, u32[]{:S(2)}) %all-to-all-start.1) | async-done | bytes 4194336 | tf_op jit(solution)/shard_map/all_to_all | solution.py:344
  135.0 28.6 %shard_map.77 = (f32[2,32,64,256]{3,2,1,0:T(8,128)}, f32[8,128]{1,0:T(8,128)}) custom-call(f32[64,64]{1,0:T(8,128)} %get-tuple-element.28.cos_a_ref, f32[64,64]{1,0:T(8,128)} %get-tuple-element.27.sin_a_ref, f32[64,64,64]{2,1,0:T(8,128)} %maximum_maximum_fusion.table_b_ref, f32[2048,1]{1,0:T(8,128)} %reshape.139.row_scale_ref, ...), custom_call_target="tpu_custom_call" | custom-call | tf_op jit(solution)/shard_map/pallas_call | solution.py:229
  163.6 16.0 %shard_map.78 = f32[8,128]{1,0:T(8,128)} custom-call(f32[8,128]{1,0:T(8,128)} %get-tuple-element.5.value_ref), custom_call_target="tpu_custom_call" | custom-call | tf_op jit(solution)/shard_map/pallas_call | solution.py:318
  179.6 1.2 slice.35
  (22 shorter events, 0.6 us)
Async XLA Ops:
  0.6 68.7 %all-to-all-start = ((f32[256,8,256]{2,1,0:T(8,128)}), f32[256,8,256]{2,1,0:T(8,128)S(1)}, u32[]{:S(2)}, u32[]{:S(2)}) async-start(f32[256,8,256]{2,1,0:T(8,128)} %bitcast.189), calls=%async_computation | async-start | bytes 4194304 | tf_op jit(solution)/shard_map/all_to_all | solution.py:341
  70.2 1.6 copy-start.2
  70.4 2.1 %copy-start = (f32[8,256,256]{2,1,0:T(8,128)S(1)}, f32[8,256,256]{2,1,0:T(8,128)}, u32[]{:S(2)}) copy-start(f32[8,256,256]{2,1,0:T(8,128)} %get-tuple-element.24) | copy-start | bytes 6291460
  70.4 2.7 %copy-start.1 = (f32[8,256,256]{2,1,0:T(8,128)S(1)}, f32[8,256,256]{2,1,0:T(8,128)}, u32[]{:S(2)}) copy-start(f32[8,256,256]{2,1,0:T(8,128)} %get-tuple-element.25) | copy-start | bytes 6291460
  80.2 5.8 %copy-start.3 = (f32[2048]{0:T(1024)S(1)}, f32[2048]{0:T(1024)}, u32[]{:S(2)}) copy-start(f32[2048]{0:T(1024)} %param.7) | copy-start | bytes 24580
  80.2 8.1 %copy-start.4 = (f32[2048]{0:T(1024)S(1)}, f32[2048]{0:T(1024)}, u32[]{:S(2)}) copy-start(f32[2048]{0:T(1024)} %param.9) | copy-start | bytes 24580
  80.2 54.7 %all-to-all-start.1 = ((f32[8,256,512]{2,1,0:T(8,128)}), f32[8,256,512]{2,1,0:T(8,128)}, u32[]{:S(2)}, u32[]{:S(2)}) async-start(f32[8,256,512]{2,1,0:T(8,128)} %fusion), calls=%async_computation.1 | async-start | bytes 8388608 | tf_op jit(solution)/shard_map/all_to_all | solution.py:344

commit v13 on v12

--- a/solution.py
+++ b/solution.py
@@ -112,7 +112,7 @@
         for index in range(size_b):
             copy = pltpu.make_async_copy(
                 spectrum_hbm.at[:, index // rows, :, index % rows, pl.ds(part * width, width)],
-                held.at[part, index],
+                held.at[index, part],
                 in_sems.at[part, index],
             )
             copy.start()
@@ -131,18 +131,15 @@
         for part in range(2):
             pltpu.make_async_copy(
                 spectrum_hbm.at[:, index // rows, :, index % rows, pl.ds(part * width, width)],
-                held.at[part, index],
+                held.at[index, part],
                 in_sems.at[part, index],
             ).wait()
-        part = jnp.concatenate(
-            [held[0, index].reshape(size_a, width), held[1, index].reshape(size_a, width)], axis=0
-        )
-        result = dot(both_a, part)
+        result = dot(both_a, held[index].reshape(2 * size_a, width))
         step_a[0, index] = result[:size_a]
         step_a[1, index] = result[size_a:]
         for part in range(2):
             pltpu.make_async_copy(
-                step_a.at[part, index], turned.at[part, :, index, :], turn_sems.at[part, index]
+                step_a.at[part, index], turned.at[:, part, index, :], turn_sems.at[part, index]
             ).start()
         return carry
 
@@ -151,7 +148,7 @@
     def settle(index, carry):
         for part in range(2):
             pltpu.make_async_copy(
-                step_a.at[part, index], turned.at[part, :, index, :], turn_sems.at[part, index]
+                step_a.at[part, index], turned.at[:, part, index, :], turn_sems.at[part, index]
             ).wait()
         return carry
 
@@ -163,8 +160,7 @@
 
     def second(index, total):
         rows = pl.ds(pl.multiple_of(index * size_b, size_b), size_b)
-        part = jnp.concatenate([turned[0, index], turned[1, index]], axis=0)
-        result = dot(table_b_ref[index], part)
+        result = dot(table_b_ref[index], turned[index].reshape(2 * size_b, width))
         spec_real = result[:size_b]
         spec_imag = result[size_b:]
         scale = row_scale_ref[rows, :] * col_scale
@@ -235,9 +231,9 @@
         in_specs=[vmem] * 8 + [anywhere],
         out_specs=(anywhere, vmem),
         scratch_shapes=[
-            pltpu.VMEM((2, size_b, high, blocks, width), jnp.float32),
+            pltpu.VMEM((size_b, 2, high, blocks, width), jnp.float32),
             pltpu.VMEM((2, size_b, size_a, width), jnp.float32),
-            pltpu.VMEM((2, size_a, size_b, width), jnp.float32),
+            pltpu.VMEM((size_a, 2, size_b, width), jnp.float32),
             pltpu.VMEM((2, size_a, size_b, width), jnp.float32),
             pltpu.SemaphoreType.DMA((2, size_b)),
             pltpu.SemaphoreType.DMA((2, size_a)),

time: 183 us -> 183 us (level)
  no operation moved by 1% of the time
where the time goes in v13:
time: 183 us
  waiting for transfers between devices  80.6 us (44%)
  Pallas kernels  44.6 us (24%)
  starting transfers between devices  21.5 us (12%)
  other arithmetic  17.9 us (10%)
  local copies, waits for them, and re-layouts  8.28 us (5%)
  matrix products  7.07 us (4%)
  between operations  2.57 us (1%)
    all_to_all x1, waiting for transfers between devices, per_device(): lax.all_to_all(outgoing, ('gy', 'gx'), split_axis=0, concat_axis=0, tiled...  43.2 us
    all_to_all x1, waiting for transfers between devices, per_device(): both = lax.all_to_all(both, 'gx', split_axis=0, concat_axis=0, tiled=True)  37.5 us
    pallas_call x1, Pallas kernels, y_stage(): pl.pallas_call(functools.partial(y_kernel, norm_factor), out_shape=(jax.S...  28.6 us
    pallas_call x1, Pallas kernels, total_everywhere(): pl.pallas_call(total_kernel, out_shape=jax.ShapeDtypeStruct((8, 128), jnp...  16 us
    all_to_all x1, starting transfers between devices, per_device(): lax.all_to_all(outgoing, ('gy', 'gx'), split_axis=0, concat_axis=0, tiled...  15.7 us
    sin x1, other arithmetic, x_stage(): sin_t = jnp.sin(angle)  9.78 us
    dot_general x1, matrix products, x_stage(): spectrum = jnp.einsum('dyn,dnk->dyk', parts, table, precision=precision_mid)  7.07 us
    all_to_all x1, starting transfers between devices, per_device(): both = lax.all_to_all(both, 'gx', split_axis=0, concat_axis=0, tiled=True)  5.82 us
  transfers between devices with their start and end apart: 2, of which 2 were waited for; matrix products, arithmetic and copies ran while one was open for 12% of the time, Pallas kernels for 0%

profile of v13, /device:TPU:1, one launch (start us, length us, event | category | flops | bytes accessed | tf_op | source)
XLA Modules:
  0.0 182.6 jit_solution(5382128065377483849)
XLA Ops:
  0.6 15.7 %all-to-all-start = ((f32[256,8,256]{2,1,0:T(8,128)}), f32[256,8,256]{2,1,0:T(8,128)S(1)}, u32[]{:S(2)}, u32[]{:S(2)}) async-start(f32[256,8,256]{2,1,0:T(8,128)} %bitcast.189), calls=%async_computation | async-start | bytes 4194304 | tf_op jit(solution)/shard_map/all_to_all | solution.py:337
  16.3 0.1 broadcast_add_fusion
  16.4 9.8 %fusion.17 = (f32[8,256,256]{2,1,0:T(8,128)}, f32[8,256,256]{2,1,0:T(8,128)}, f32[8,256,256]{2,1,0:T(8,128)}) fusion(s32[8,256]{1,0:T(8,128)S(1)} %broadcast_add_fusion), kind=kLoop, calls=%fused_computation.24 | loop fusion | flops 7864320 | bytes 6299648 | tf_op jit(solution)/shard_map/sin | solution.py:70
  26.2 43.2 %all-to-all-done = f32[256,8,256]{2,1,0:T(8,128)S(1)} async-done(((f32[256,8,256]{2,1,0:T(8,128)}), f32[256,8,256]{2,1,0:T(8,128)S(1)}, u32[]{:S(2)}, u32[]{:S(2)}) %all-to-all-start) | async-done | bytes 2097184 | tf_op jit(solution)/shard_map/all_to_all | solution.py:337
  69.3 0.2 add_add_fusion.2
  69.6 0.1 add_add_fusion.6
  69.7 0.2 add_add_fusion
  69.9 0.2 add_add_fusion.1
  70.7 1.2 copy-done.2
  71.8 0.7 copy-done
  72.5 0.6 copy-done.1
  73.1 7.1 %fusion = f32[8,256,512]{2,1,0:T(8,128)} fusion(f32[8,256,512]{2,1,0:T(8,128)S(1)} %fusion.30, f32[8,256,256]{2,1,0:T(8,128)S(1)} %copy-done.2, f32[8,256,256]{2,1,0:T(8,128)S(1)} %copy-done.1, f32[8,256,256]{2,1,0:T(8,128)S(1)} %copy-done), kind=kOutput, calls=%fused_computation | convolution fusion | flops 3227516928 | bytes 14680064 | tf_op jit(solution)/shard_map/dyn,dnk->dyk/dot_general | solution.py:74
  80.2 5.8 %all-to-all-start.1 = ((f32[8,256,512]{2,1,0:T(8,128)}), f32[8,256,512]{2,1,0:T(8,128)}, u32[]{:S(2)}, u32[]{:S(2)}) async-start(f32[8,256,512]{2,1,0:T(8,128)} %fusion), calls=%async_computation.1 | async-start | bytes 8388608 | tf_op jit(solution)/shard_map/all_to_all | solution.py:340
  86.1 0.1 copy.9
  86.2 2.1 %reshape.139.row_scale_ref = f32[2048,1]{1,0:T(8,128)} reshape(f32[64,32]{1,0:T(8,128)S(1)} %copy.9) | data formatting | bytes 16384 | tf_op jit(solution)/shard_map/reshape | solution.py:220
  88.3 0.1 copy.10
  88.4 2.1 %reshape.140.row_rate_ref = f32[2048,1]{1,0:T(8,128)} reshape(f32[64,32]{1,0:T(8,128)S(1)} %copy.10) | data formatting | bytes 16384 | tf_op jit(solution)/shard_map/reshape | solution.py:221
  90.6 4.2 %fusion.37 = (f32[64,32,32]{2,1,0:T(8,128)S(1)}, f32[64,32,32]{2,1,0:T(8,128)S(1)}, f32[64,32,32]{2,1,0:T(8,128)S(1)}) fusion(s32[64,32]{1,0:T(8,128)S(1)} %iota_add_fusion), kind=kLoop, calls=%fused_computation.52 | loop fusion | flops 983040 | bytes 794624 | tf_op jit(solution)/shard_map/neg | solution.py:218
  94.7 2.0 %maximum_maximum_fusion.table_b_ref = f32[64,64,64]{2,1,0:T(8,128)} fusion(f32[64,32,32]{2,1,0:T(8,128)S(1)} %get-tuple-element.23, f32[64,32,32]{2,1,0:T(8,128)S(1)} %get-tuple-element.22, f32[64,32,32]{2,1,0:T(8,128)S(1)} %get-tuple-element.21), kind=kLoop, calls=%fused_computation.14 | loop fusion | flops 786432 | bytes 1835008 | tf_op jit(solution)/shard_map/concatenate | solution.py:217
  96.7 0.8 fusion.44
  97.5 37.5 %all-to-all-done.1 = f32[8,256,512]{2,1,0:T(8,128)} async-done(((f32[8,256,512]{2,1,0:T(8,128)}), f32[8,256,512]{2,1,0:T(8,128)}, u32[]{:S(2)}, u32[]{:S(2)}) %all-to-all-start.1) | async-done | bytes 4194336 | tf_op jit(solution)/shard_map/all_to_all | solution.py:340
  135.0 28.6 %shard_map.77 = (f32[2,32,64,256]{3,2,1,0:T(8,128)}, f32[8,128]{1,0:T(8,128)}) custom-call(f32[64,64]{1,0:T(8,128)} %get-tuple-element.28.cos_a_ref, f32[64,64]{1,0:T(8,128)} %get-tuple-element.27.sin_a_ref, f32[64,64,64]{2,1,0:T(8,128)} %maximum_maximum_fusion.table_b_ref, f32[2048,1]{1,0:T(8,128)} %reshape.139.row_scale_ref, ...), custom_call_target="tpu_custom_call" | custom-call | tf_op jit(solution)/shard_map/pallas_call | solution.py:225
  163.6 16.0 %shard_map.78 = f32[8,128]{1,0:T(8,128)} custom-call(f32[8,128]{1,0:T(8,128)} %get-tuple-element.5.value_ref), custom_call_target="tpu_custom_call" | custom-call | tf_op jit(solution)/shard_map/pallas_call | solution.py:314
  179.6 1.2 slice.35
  (22 shorter events, 0.6 us)
Async XLA Ops:
  0.6 68.7 %all-to-all-start = ((f32[256,8,256]{2,1,0:T(8,128)}), f32[256,8,256]{2,1,0:T(8,128)S(1)}, u32[]{:S(2)}, u32[]{:S(2)}) async-start(f32[256,8,256]{2,1,0:T(8,128)} %bitcast.189), calls=%async_computation | async-start | bytes 4194304 | tf_op jit(solution)/shard_map/all_to_all | solution.py:337
  70.2 1.6 copy-start.2
  70.4 2.1 %copy-start = (f32[8,256,256]{2,1,0:T(8,128)S(1)}, f32[8,256,256]{2,1,0:T(8,128)}, u32[]{:S(2)}) copy-start(f32[8,256,256]{2,1,0:T(8,128)} %get-tuple-element.24) | copy-start | bytes 6291460
  70.4 2.7 %copy-start.1 = (f32[8,256,256]{2,1,0:T(8,128)S(1)}, f32[8,256,256]{2,1,0:T(8,128)}, u32[]{:S(2)}) copy-start(f32[8,256,256]{2,1,0:T(8,128)} %get-tuple-element.25) | copy-start | bytes 6291460
  80.2 5.8 %copy-start.3 = (f32[2048]{0:T(1024)S(1)}, f32[2048]{0:T(1024)}, u32[]{:S(2)}) copy-start(f32[2048]{0:T(1024)} %param.7) | copy-start | bytes 24580
  80.2 8.1 %copy-start.4 = (f32[2048]{0:T(1024)S(1)}, f32[2048]{0:T(1024)}, u32[]{:S(2)}) copy-start(f32[2048]{0:T(1024)} %param.9) | copy-start | bytes 24580
  80.2 54.7 %all-to-all-start.1 = ((f32[8,256,512]{2,1,0:T(8,128)}), f32[8,256,512]{2,1,0:T(8,128)}, u32[]{:S(2)}, u32[]{:S(2)}) async-start(f32[8,256,512]{2,1,0:T(8,128)} %fusion), calls=%async_computation.1 | async-start | bytes 8388608 | tf_op jit(solution)/shard_map/all_to_all | solution.py:340

commit v14 on v13

--- a/solution.py
+++ b/solution.py
@@ -99,7 +99,8 @@
     return (final_real.reshape(planes, length, width), final_imag.reshape(planes, length, width))
 
 
-def y_kernel(norm_factor, cos_a_ref, sin_a_ref, table_b_ref, row_scale_ref, row_rate_ref, col_scale_ref, col_shift_ref,
+def y_kernel(norm_factor, cos_a_ref, sin_a_ref, table_b_ref, row_scale_ref, row_rate_ref, row_log_ref,
+             col_scale_ref, col_log_ref, col_shift_ref,
              col_mix_ref, spectrum_hbm, out_hbm, sum_ref,
              held, step_a, turned, staged, in_sems, out_sems, turn_sems):
     high, low, blocks, rows, both_width = spectrum_hbm.shape
@@ -155,6 +156,7 @@
     lax.fori_loop(0, size_b, settle, 0)
 
     col_scale = col_scale_ref[...]
+    col_log = col_log_ref[...]
     col_shift = col_shift_ref[...]
     col_mix = col_mix_ref[...]
 
@@ -172,7 +174,7 @@
             -0.5 * (latent_u * latent_u + latent_w * latent_w)
             - math.log(2.0 * math.pi)
             + log_scale
-            + 2.0 * jnp.log(scale)
+            + 2.0 * (row_log_ref[rows, :] + col_log)
         )
         staged[0, index] = latent_u
         staged[1, index] = latent_w
@@ -228,7 +230,7 @@
             jax.ShapeDtypeStruct((2, size_b, size_a, width), jnp.float32),
             jax.ShapeDtypeStruct((8, 128), jnp.float32),
         ),
-        in_specs=[vmem] * 8 + [anywhere],
+        in_specs=[vmem] * 10 + [anywhere],
         out_specs=(anywhere, vmem),
         scratch_shapes=[
             pltpu.VMEM((size_b, 2, high, blocks, width), jnp.float32),
@@ -242,7 +244,8 @@
         compiler_params=pltpu.CompilerParams(vmem_limit_bytes=60 * 1024 * 1024),
     )(
         cos_a, sin_a, table_b,
-        row_scale_t, row_rate_t, col_scale.reshape(1, width), col_shift.reshape(1, width),
+        row_scale_t, row_rate_t, jnp.log(row_scale_t), col_scale.reshape(1, width),
+        jnp.log(col_scale).reshape(1, width), col_shift.reshape(1, width),
         col_mix.reshape(1, width), shaped,
     )
     return latent.reshape(2, length, width), sums

time: 183 us -> 183 us (level)
    log x0 -> x3, local copies, waits for them, and re-layouts: none -> 2.02 us  [the longest x2 1.44 us: y_stage(): jnp.log(row_scale_t)]
where the time goes in v14:
time: 183 us
  waiting for transfers between devices  79.2 us (43%)
  Pallas kernels  45 us (25%)
  starting transfers between devices  21.5 us (12%)
  other arithmetic  17.9 us (10%)
  local copies, waits for them, and re-layouts  9.67 us (5%)
  matrix products  7.07 us (4%)
  between operations  2.6 us (1%)
    all_to_all x1, waiting for transfers between devices, per_device(): lax.all_to_all(outgoing, ('gy', 'gx'), split_axis=0, concat_axis=0, tiled...  43.2 us
    all_to_all x1, waiting for transfers between devices, per_device(): both = lax.all_to_all(both, 'gx', split_axis=0, concat_axis=0, tiled=True)  36 us
    pallas_call x1, Pallas kernels, y_stage(): pl.pallas_call(functools.partial(y_kernel, norm_factor), out_shape=(jax.S...  29 us
    pallas_call x1, Pallas kernels, total_everywhere(): pl.pallas_call(total_kernel, out_shape=jax.ShapeDtypeStruct((8, 128), jnp...  16 us
    all_to_all x1, starting transfers between devices, per_device(): lax.all_to_all(outgoing, ('gy', 'gx'), split_axis=0, concat_axis=0, tiled...  15.7 us
    sin x1, other arithmetic, x_stage(): sin_t = jnp.sin(angle)  9.79 us
    dot_general x1, matrix products, x_stage(): spectrum = jnp.einsum('dyn,dnk->dyk', parts, table, precision=precision_mid)  7.07 us
    all_to_all x1, starting transfers between devices, per_device(): both = lax.all_to_all(both, 'gx', split_axis=0, concat_axis=0, tiled=True)  5.81 us
  transfers between devices with their start and end apart: 2, of which 2 were waited for; matrix products, arithmetic and copies ran while one was open for 12% of the time, Pallas kernels for 0%

profile of v14, /device:TPU:1, one launch (start us, length us, event | category | flops | bytes accessed | tf_op | source)
XLA Modules:
  0.0 182.9 jit_solution(17293679503219529417)
XLA Ops:
  0.6 15.7 %all-to-all-start = ((f32[256,8,256]{2,1,0:T(8,128)}), f32[256,8,256]{2,1,0:T(8,128)S(1)}, u32[]{:S(2)}, u32[]{:S(2)}) async-start(f32[256,8,256]{2,1,0:T(8,128)} %bitcast.190), calls=%async_computation | async-start | bytes 4194304 | tf_op jit(solution)/shard_map/all_to_all | solution.py:340
  16.4 9.8 %fusion.17 = (f32[8,256,256]{2,1,0:T(8,128)}, f32[8,256,256]{2,1,0:T(8,128)}, f32[8,256,256]{2,1,0:T(8,128)}) fusion(s32[8,256]{1,0:T(8,128)S(1)} %broadcast_add_fusion), kind=kLoop, calls=%fused_computation.24 | loop fusion | flops 7864320 | bytes 6299648 | tf_op jit(solution)/shard_map/sin | solution.py:70
  26.2 43.2 %all-to-all-done = f32[256,8,256]{2,1,0:T(8,128)S(1)} async-done(((f32[256,8,256]{2,1,0:T(8,128)}), f32[256,8,256]{2,1,0:T(8,128)S(1)}, u32[]{:S(2)}, u32[]{:S(2)}) %all-to-all-start) | async-done | bytes 2097184 | tf_op jit(solution)/shard_map/all_to_all | solution.py:340
  69.3 0.2 add_add_fusion.2
  69.6 0.1 add_add_fusion.6
  69.7 0.2 add_add_fusion
  69.9 0.2 add_add_fusion.1
  70.7 1.2 copy-done.2
  71.8 0.7 copy-done
  72.5 0.6 copy-done.1
  73.1 7.1 %fusion = f32[8,256,512]{2,1,0:T(8,128)} fusion(f32[8,256,512]{2,1,0:T(8,128)S(1)} %fusion.30, f32[8,256,256]{2,1,0:T(8,128)S(1)} %copy-done.2, f32[8,256,256]{2,1,0:T(8,128)S(1)} %copy-done.1, f32[8,256,256]{2,1,0:T(8,128)S(1)} %copy-done), kind=kOutput, calls=%fused_computation | convolution fusion | flops 3227516928 | bytes 14680064 | tf_op jit(solution)/shard_map/dyn,dnk->dyk/dot_general | solution.py:74
  80.2 5.8 %all-to-all-start.1 = ((f32[8,256,512]{2,1,0:T(8,128)}), f32[8,256,512]{2,1,0:T(8,128)}, u32[]{:S(2)}, u32[]{:S(2)}) async-start(f32[8,256,512]{2,1,0:T(8,128)} %fusion), calls=%async_computation.1 | async-start | bytes 8388608 | tf_op jit(solution)/shard_map/all_to_all | solution.py:343
  86.2 0.1 reshape.145
  86.3 1.4 copy.17.row_scale_ref
  87.7 1.4 copy.19.row_log_ref
  89.3 2.1 %reshape.155.row_rate_ref = f32[2048,1]{1,0:T(8,128)} reshape(f32[64,32]{1,0:T(8,128)S(1)} %copy.16) | data formatting | bytes 16384 | tf_op jit(solution)/shard_map/reshape | solution.py:223
  91.4 0.6 log.7
  92.0 4.2 %fusion.37 = (f32[64,32,32]{2,1,0:T(8,128)S(1)}, f32[64,32,32]{2,1,0:T(8,128)S(1)}, f32[64,32,32]{2,1,0:T(8,128)S(1)}) fusion(s32[64,32]{1,0:T(8,128)S(1)} %iota_add_fusion), kind=kLoop, calls=%fused_computation.52 | loop fusion | flops 983040 | bytes 794624 | tf_op jit(solution)/shard_map/neg | solution.py:220
  96.2 2.0 %maximum_maximum_fusion.table_b_ref = f32[64,64,64]{2,1,0:T(8,128)} fusion(f32[64,32,32]{2,1,0:T(8,128)S(1)} %get-tuple-element.25, f32[64,32,32]{2,1,0:T(8,128)S(1)} %get-tuple-element.24, f32[64,32,32]{2,1,0:T(8,128)S(1)} %get-tuple-element.23), kind=kLoop, calls=%fused_computation.14 | loop fusion | flops 786432 | bytes 1835008 | tf_op jit(solution)/shard_map/concatenate | solution.py:219
  98.1 0.8 fusion.44
  98.9 36.0 %all-to-all-done.1 = f32[8,256,512]{2,1,0:T(8,128)} async-done(((f32[8,256,512]{2,1,0:T(8,128)}), f32[8,256,512]{2,1,0:T(8,128)}, u32[]{:S(2)}, u32[]{:S(2)}) %all-to-all-start.1) | async-done | bytes 4194336 | tf_op jit(solution)/shard_map/all_to_all | solution.py:343
  134.9 29.0 %shard_map.77 = (f32[2,32,64,256]{3,2,1,0:T(8,128)}, f32[8,128]{1,0:T(8,128)}) custom-call(f32[64,64]{1,0:T(8,128)} %get-tuple-element.30.cos_a_ref, f32[64,64]{1,0:T(8,128)} %get-tuple-element.29.sin_a_ref, f32[64,64,64]{2,1,0:T(8,128)} %maximum_maximum_fusion.table_b_ref, f32[2048,1]{1,0:T(8,128)} %copy.17.row_scale_ref, f32[2048,1]{1,0:T(8,128)} %reshape.155.row_rate_ref, ...), custom_call_target="tpu_custom_call" | custom-call | tf_op jit(solution)/shard_map/pallas_call | solution.py:227
  163.9 16.0 %shard_map.78 = f32[8,128]{1,0:T(8,128)} custom-call(f32[8,128]{1,0:T(8,128)} %get-tuple-element.5.value_ref), custom_call_target="tpu_custom_call" | custom-call | tf_op jit(solution)/shard_map/pallas_call | solution.py:317
  179.9 1.2 slice.35
  (28 shorter events, 0.9 us)
Async XLA Ops:
  0.6 68.7 %all-to-all-start = ((f32[256,8,256]{2,1,0:T(8,128)}), f32[256,8,256]{2,1,0:T(8,128)S(1)}, u32[]{:S(2)}, u32[]{:S(2)}) async-start(f32[256,8,256]{2,1,0:T(8,128)} %bitcast.190), calls=%async_computation | async-start | bytes 4194304 | tf_op jit(solution)/shard_map/all_to_all | solution.py:340
  70.2 1.6 copy-start.2
  70.4 2.1 %copy-start = (f32[8,256,256]{2,1,0:T(8,128)S(1)}, f32[8,256,256]{2,1,0:T(8,128)}, u32[]{:S(2)}) copy-start(f32[8,256,256]{2,1,0:T(8,128)} %get-tuple-element.26) | copy-start | bytes 6291460
  70.4 2.7 %copy-start.1 = (f32[8,256,256]{2,1,0:T(8,128)S(1)}, f32[8,256,256]{2,1,0:T(8,128)}, u32[]{:S(2)}) copy-start(f32[8,256,256]{2,1,0:T(8,128)} %get-tuple-element.27) | copy-start | bytes 6291460
  80.2 5.8 %copy-start.3 = (f32[2048]{0:T(1024)S(1)}, f32[2048]{0:T(1024)}, u32[]{:S(2)}) copy-start(f32[2048]{0:T(1024)} %param.7) | copy-start | bytes 24580
  80.2 54.7 %all-to-all-start.1 = ((f32[8,256,512]{2,1,0:T(8,128)}), f32[8,256,512]{2,1,0:T(8,128)}, u32[]{:S(2)}, u32[]{:S(2)}) async-start(f32[8,256,512]{2,1,0:T(8,128)} %fusion), calls=%async_computation.1 | async-start | bytes 8388608 | tf_op jit(solution)/shard_map/all_to_all | solution.py:343
  86.0 3.1 %copy-start.4 = (f32[2048]{0:T(1024)S(1)}, f32[2048]{0:T(1024)}, u32[]{:S(2)}) copy-start(f32[2048]{0:T(1024)} %param.9) | copy-start | bytes 24580
  86.0 5.4 %copy-start.5 = (f32[256]{0:T(256)S(1)}, f32[256]{0:T(256)}, u32[]{:S(2)}) copy-start(f32[256]{0:T(256)} %param.8) | copy-start | bytes 3076
